TPU v7x, 512 devices: a whole 4x4x16 slice. The times are simulated.
512 devices in a mesh: tm: 128 (over x_lo, y, z), rows: 4 (over x_hi, core).
Axes of the slice: x: 4 (x_hi: 2, x_lo: 2; x = x_hi * 2 + x_lo), y: 4, z: 16, core: 2. Of those that a mesh axis runs over, the one named last changes fastest.
Arguments:
- start_state: float32 [4, 32, 512], P(None, 'rows'), may hold values from -0.15 to 1.15, as said below
- initial_guess: float32 [128, 4, 32, 512], P('tm', None, 'rows'), may hold values from -0.15 to 1.15, as said below
- land_mask: int32 [32, 512], P('rows'), may hold values 0 or 1
- bed_class: int32 [32, 512], P('rows'), may hold values from 0 to 15
- bed_table: float32 [16], replicated, may hold values from -0.5 to 0.5
Outputs:
- corrected: float32 [128, 4, 32, 512], P('tm', None, 'rows')
Inputs may be any that keep to these rules, and one draw needn't show every extreme that they name: `start_state`: component 0 lies in 0.85 to 1.15, components 1 and 2 in -0.15 to 0.15, component 3 in 0.15 to 0.45. `initial_guess`: component 0 lies in 0.85 to 1.15, components 1 and 2 in -0.15 to 0.15, component 3 in 0.15 to 0.45.
All inputs are finite; a program needn't handle non-finite values. No bound on the sum of `land_mask` on one device may be relied on, other than what follows from the above.
Results may differ from a plain program's by a relative error of at most 0.00002.
Values sent between devices are 32-bit elements; how exact they have to be, the bound alone decides.
No kernel may reach another device: no remote copies, remote signals or barrier semaphores. Data moves between devices by JAX's collectives and lax.ppermute only.
A program may use at most 64 MiB of HBM per device.

v0:
```python
import jax
import jax.numpy as jnp
from jax import lax
from jax.sharding import PartitionSpec as P

FINE_STEPS = 8
BLOCK_LEN = 4
RELAXES = 2


FINE_COURANT = 0.0375
FINE_VISCOUS = 0.025
COARSE_COURANT = 0.3
COARSE_VISCOUS = 0.2


def with_halo(array, sides, width):
    for axis, dim in sides:
        devices, length = (lax.axis_size(axis), array.shape[dim])
        up = [(i, (i + 1) % devices) for i in range(devices)]
        down = [(j, i) for i, j in up]
        last = lax.slice_in_dim(array, length - width, length, axis=dim)
        initial = lax.slice_in_dim(array, 0, width, axis=dim)
        before = lax.ppermute(last, axis, up)
        after = lax.ppermute(initial, axis, down)
        array = jnp.concatenate([before, array, after], axis=dim)
    return array


def from_behind(value, axis, steps):
    count = lax.axis_size(axis)
    initial, last = (max(0, -steps), min(count, count - steps))
    return lax.ppermute(value, axis, [(source, source + steps) for source in range(initial, last)])


def across(values):
    return jnp.roll(values, -1, axis=-1) - jnp.roll(values, 1, axis=-1)


def advance(padded, statics, stability_ratio, viscous):
    east_velocity = padded[1] / padded[0]
    north_velocity = padded[2] / padded[0]
    inner_cells = padded[:, 1:-1]
    fluid_thickness = inner_cells[0]
    row_fluxes = jnp.stack(
        [
            padded[2],
            padded[1] * north_velocity,
            padded[2] * north_velocity + 0.5 * padded[0] * padded[0],
            padded[3] * north_velocity,
        ]
    )
    inner_east = east_velocity[1:-1]
    inner_north = north_velocity[1:-1]
    pressure_term = 0.5 * fluid_thickness * fluid_thickness
    column_fluxes = jnp.stack(
        [
            inner_cells[1],
            inner_cells[1] * inner_east + pressure_term,
            inner_cells[2] * inner_east,
            inner_cells[3] * inner_east,
        ]
    )
    column_sum = jnp.roll(inner_cells, -1, axis=-1) + jnp.roll(inner_cells, 1, axis=-1)
    neighbours = column_sum + padded[:, 2:] + padded[:, :-2]
    advanced_fields = (
        inner_cells
        - 0.5 * stability_ratio * (across(column_fluxes) + (row_fluxes[:, 2:] - row_fluxes[:, :-2]))
        + viscous * (neighbours - 4.0 * inner_cells)
    )
    bed_level = statics[0]
    wet_cells = statics[1, 1:-1]
    flow_magnitude = jnp.sqrt(inner_east * inner_east + inner_north * inner_north)
    slope_east = 0.5 * across(bed_level[1:-1])
    slope_north = 0.5 * (bed_level[2:] - bed_level[:-2])
    new_zonal_motion = wet_cells * (
        advanced_fields[1]
        - stability_ratio * (fluid_thickness * slope_east + 0.02 * flow_magnitude * inner_east)
    )
    new_meridional_motion = wet_cells * (
        advanced_fields[2]
        - stability_ratio * (fluid_thickness * slope_north + 0.02 * flow_magnitude * inner_north)
    )
    new_bedload_amount = advanced_fields[3] + stability_ratio * (
        0.05 * flow_magnitude * flow_magnitude - 0.3 * inner_cells[3] / fluid_thickness
    )
    return jnp.stack(
        [advanced_fields[0], new_zonal_motion, new_meridional_motion, new_bedload_amount]
    )


def on_device(start_state, initial_guess, land_mask, bed_class, bed_table):
    time_index = lax.axis_index("tm")
    classes = jnp.arange(bed_table.shape[0], dtype=jnp.int32)
    bed_level = jnp.sum(
        jnp.where(bed_class[None] == classes[:, None, None], bed_table[:, None, None], 0.0), axis=0
    )
    statics = jnp.stack([bed_level, land_mask.astype(jnp.float32)])
    near_static = with_halo(statics, (("rows", 1),), 1)

    def propagate(model_state):
        for repeat in range(FINE_STEPS):
            padded = with_halo(model_state, (("rows", 1),), 1)
            model_state = advance(padded, near_static, FINE_COURANT, FINE_VISCOUS)
        return model_state

    def coarse(model_state):
        padded = with_halo(model_state, (("rows", 1),), 1)
        return advance(padded, near_static, COARSE_COURANT, COARSE_VISCOUS)

    def previous(model_state):
        arrived = from_behind(model_state, "tm", 1)
        return jnp.where(time_index == 0, start_state, arrived)

    updated = propagate(previous(initial_guess[0]))
    before = previous(updated)
    reached = propagate(before)
    forcing = reached - coarse(before)
    position = time_index % BLOCK_LEN
    values = updated
    for relax_turn in range(RELAXES):
        for offset in range(BLOCK_LEN):
            arrived = from_behind(values, "tm", 1)
            arrived = jnp.where(time_index == 0, start_state, arrived)
            stepped = coarse(arrived) + forcing
            values = jnp.where(position == offset, stepped, values)
    return values[None]


def solution(mesh):
    in_specs = (
        P(None, "rows", None),
        P("tm", None, "rows", None),
        P("rows", None),
        P("rows", None),
        P(),
    )
    out_specs = P("tm", None, "rows", None)
    return jax.shard_map(
        on_device, mesh=mesh, in_specs=in_specs, out_specs=out_specs, check_vma=False
    )
```

profile of v0, /device:TPU:6, one launch (start us, length us, event | category | flops | bytes accessed | tf_op | source)
XLA Modules:
  0.0 317.0 jit_solution(16616028098406053309)
XLA Ops:
  0.9 2.8 collective-permute-start.3
  3.7 1.9 collective-permute-start.4
  5.6 3.8 %collective-permute-start = (f32[4,8,512]{2,1,0:T(8,128)S(1)}, f32[4,8,512]{2,1,0:T(8,128)S(1)}, u32[]{:S(2)}, u32[]{:S(2)}) collective-permute-start(f32[4,8,512]{2,1,0:T(8,128)S(1)} %bitcast.1725), channel_id=1, source_target_pairs={{0,4},{4,8},{8,12},{12,16},{16,20},{20,24},{24,28},{28,32},{32,36}... | collective-permute-start | bytes 196616 | tf_op jit(solution)/shard_map/ppermute | solution.py:33
  9.6 12.0 %collective-permute-done = f32[4,8,512]{2,1,0:T(8,128)S(1)} collective-permute-done((f32[4,8,512]{2,1,0:T(8,128)S(1)}, f32[4,8,512]{2,1,0:T(8,128)S(1)}, u32[]{:S(2)}, u32[]{:S(2)}) %collective-permute-start) | collective-permute-done | bytes 65568 | tf_op jit(solution)/shard_map/ppermute | solution.py:33
  21.7 5.4 %collective-permute-start.2 = (f32[4,1,512]{2,1,0:T(1,128)S(1)}, f32[4,1,512]{2,1,0:T(1,128)S(1)}, u32[]{:S(2)}, u32[]{:S(2)}) collective-permute-start(f32[4,1,512]{2,1,0:T(1,128)S(1)} %get-tuple-element.570), channel_id=1, source_target_pairs={{1,0},{2,1},{3,2},{0,3},{5,4},{6,5},{7,6},{4,7},{9,8},{10,9},{11,1... | collective-permute-start | bytes 24584 | tf_op jit(solution)/shard_map/ppermute | solution.py:25
  27.1 1.9 collective-permute-start.1
  29.1 4.5 %collective-permute-done.1 = f32[4,1,512]{2,1,0:T(1,128)S(1)} collective-permute-done((f32[4,1,512]{2,1,0:T(1,128)S(1)}, f32[4,1,512]{2,1,0:T(1,128)S(1)}, u32[]{:S(2)}, u32[]{:S(2)}) %collective-permute-start.1) | collective-permute-done | bytes 8224 | tf_op jit(solution)/shard_map/ppermute | solution.py:24
  36.9 2.4 collective-permute-start.5
  39.4 4.0 %collective-permute-done.5 = f32[4,1,512]{2,1,0:T(1,128)S(1)} collective-permute-done((f32[4,1,512]{2,1,0:T(1,128)S(1)}, f32[4,1,512]{2,1,0:T(1,128)S(1)}, u32[]{:S(2)}, u32[]{:S(2)}) %collective-permute-start.5) | collective-permute-done | bytes 8224 | tf_op jit(solution)/shard_map/ppermute | solution.py:24
  45.9 2.4 collective-permute-start.7
  48.4 4.0 %collective-permute-done.7 = f32[4,1,512]{2,1,0:T(1,128)S(1)} collective-permute-done((f32[4,1,512]{2,1,0:T(1,128)S(1)}, f32[4,1,512]{2,1,0:T(1,128)S(1)}, u32[]{:S(2)}, u32[]{:S(2)}) %collective-permute-start.7) | collective-permute-done | bytes 8224 | tf_op jit(solution)/shard_map/ppermute | solution.py:24
  54.9 2.4 collective-permute-start.9
  57.4 4.0 %collective-permute-done.9 = f32[4,1,512]{2,1,0:T(1,128)S(1)} collective-permute-done((f32[4,1,512]{2,1,0:T(1,128)S(1)}, f32[4,1,512]{2,1,0:T(1,128)S(1)}, u32[]{:S(2)}, u32[]{:S(2)}) %collective-permute-start.9) | collective-permute-done | bytes 8224 | tf_op jit(solution)/shard_map/ppermute | solution.py:24
  63.9 2.4 collective-permute-start.11
  66.4 4.0 %collective-permute-done.11 = f32[4,1,512]{2,1,0:T(1,128)S(1)} collective-permute-done((f32[4,1,512]{2,1,0:T(1,128)S(1)}, f32[4,1,512]{2,1,0:T(1,128)S(1)}, u32[]{:S(2)}, u32[]{:S(2)}) %collective-permute-start.11) | collective-permute-done | bytes 8224 | tf_op jit(solution)/shard_map/ppermute | solution.py:24
  72.9 2.4 collective-permute-start.13
  75.4 4.0 %collective-permute-done.13 = f32[4,1,512]{2,1,0:T(1,128)S(1)} collective-permute-done((f32[4,1,512]{2,1,0:T(1,128)S(1)}, f32[4,1,512]{2,1,0:T(1,128)S(1)}, u32[]{:S(2)}, u32[]{:S(2)}) %collective-permute-start.13) | collective-permute-done | bytes 8224 | tf_op jit(solution)/shard_map/ppermute | solution.py:24
  81.9 2.4 collective-permute-start.15
  84.4 4.0 %collective-permute-done.15 = f32[4,1,512]{2,1,0:T(1,128)S(1)} collective-permute-done((f32[4,1,512]{2,1,0:T(1,128)S(1)}, f32[4,1,512]{2,1,0:T(1,128)S(1)}, u32[]{:S(2)}, u32[]{:S(2)}) %collective-permute-start.15) | collective-permute-done | bytes 8224 | tf_op jit(solution)/shard_map/ppermute | solution.py:24
  90.9 2.4 collective-permute-start.17
  93.3 4.0 %collective-permute-done.17 = f32[4,1,512]{2,1,0:T(1,128)S(1)} collective-permute-done((f32[4,1,512]{2,1,0:T(1,128)S(1)}, f32[4,1,512]{2,1,0:T(1,128)S(1)}, u32[]{:S(2)}, u32[]{:S(2)}) %collective-permute-start.17) | collective-permute-done | bytes 8224 | tf_op jit(solution)/shard_map/ppermute | solution.py:24
  97.8 1.9 collective-permute-start.19
  99.8 8.4 %collective-permute-done.19 = f32[4,8,512]{2,1,0:T(8,128)S(1)} collective-permute-done((f32[4,8,512]{2,1,0:T(8,128)S(1)}, f32[4,8,512]{2,1,0:T(8,128)S(1)}, u32[]{:S(2)}, u32[]{:S(2)}) %collective-permute-start.19) | collective-permute-done | bytes 65568 | tf_op jit(solution)/shard_map/ppermute | solution.py:33
  110.2 2.4 collective-permute-start.20
  112.7 4.0 %collective-permute-done.20 = f32[4,1,512]{2,1,0:T(1,128)S(1)} collective-permute-done((f32[4,1,512]{2,1,0:T(1,128)S(1)}, f32[4,1,512]{2,1,0:T(1,128)S(1)}, u32[]{:S(2)}, u32[]{:S(2)}) %collective-permute-start.20) | collective-permute-done | bytes 8224 | tf_op jit(solution)/shard_map/ppermute | solution.py:24
  119.4 2.4 collective-permute-start.22
  121.9 4.0 %collective-permute-done.22 = f32[4,1,512]{2,1,0:T(1,128)S(1)} collective-permute-done((f32[4,1,512]{2,1,0:T(1,128)S(1)}, f32[4,1,512]{2,1,0:T(1,128)S(1)}, u32[]{:S(2)}, u32[]{:S(2)}) %collective-permute-start.22) | collective-permute-done | bytes 8224 | tf_op jit(solution)/shard_map/ppermute | solution.py:24
  128.5 2.4 collective-permute-start.24
  131.0 4.0 %collective-permute-done.24 = f32[4,1,512]{2,1,0:T(1,128)S(1)} collective-permute-done((f32[4,1,512]{2,1,0:T(1,128)S(1)}, f32[4,1,512]{2,1,0:T(1,128)S(1)}, u32[]{:S(2)}, u32[]{:S(2)}) %collective-permute-start.24) | collective-permute-done | bytes 8224 | tf_op jit(solution)/shard_map/ppermute | solution.py:24
  137.5 2.4 collective-permute-start.26
  139.9 4.0 %collective-permute-done.26 = f32[4,1,512]{2,1,0:T(1,128)S(1)} collective-permute-done((f32[4,1,512]{2,1,0:T(1,128)S(1)}, f32[4,1,512]{2,1,0:T(1,128)S(1)}, u32[]{:S(2)}, u32[]{:S(2)}) %collective-permute-start.26) | collective-permute-done | bytes 8224 | tf_op jit(solution)/shard_map/ppermute | solution.py:24
  146.5 2.4 collective-permute-start.28
  148.9 4.0 %collective-permute-done.28 = f32[4,1,512]{2,1,0:T(1,128)S(1)} collective-permute-done((f32[4,1,512]{2,1,0:T(1,128)S(1)}, f32[4,1,512]{2,1,0:T(1,128)S(1)}, u32[]{:S(2)}, u32[]{:S(2)}) %collective-permute-start.28) | collective-permute-done | bytes 8224 | tf_op jit(solution)/shard_map/ppermute | solution.py:24
  155.5 2.4 collective-permute-start.30
  157.9 4.0 %collective-permute-done.30 = f32[4,1,512]{2,1,0:T(1,128)S(1)} collective-permute-done((f32[4,1,512]{2,1,0:T(1,128)S(1)}, f32[4,1,512]{2,1,0:T(1,128)S(1)}, u32[]{:S(2)}, u32[]{:S(2)}) %collective-permute-start.30) | collective-permute-done | bytes 8224 | tf_op jit(solution)/shard_map/ppermute | solution.py:24
  164.5 2.4 collective-permute-start.32
  166.9 4.0 %collective-permute-done.32 = f32[4,1,512]{2,1,0:T(1,128)S(1)} collective-permute-done((f32[4,1,512]{2,1,0:T(1,128)S(1)}, f32[4,1,512]{2,1,0:T(1,128)S(1)}, u32[]{:S(2)}, u32[]{:S(2)}) %collective-permute-start.32) | collective-permute-done | bytes 8224 | tf_op jit(solution)/shard_map/ppermute | solution.py:24
  173.5 2.4 collective-permute-start.34
  175.9 4.0 %collective-permute-done.34 = f32[4,1,512]{2,1,0:T(1,128)S(1)} collective-permute-done((f32[4,1,512]{2,1,0:T(1,128)S(1)}, f32[4,1,512]{2,1,0:T(1,128)S(1)}, u32[]{:S(2)}, u32[]{:S(2)}) %collective-permute-start.34) | collective-permute-done | bytes 8224 | tf_op jit(solution)/shard_map/ppermute | solution.py:24
  180.4 1.9 collective-permute-start.36
  182.4 8.5 %collective-permute-done.36 = f32[4,8,512]{2,1,0:T(8,128)S(1)} collective-permute-done((f32[4,8,512]{2,1,0:T(8,128)S(1)}, f32[4,8,512]{2,1,0:T(8,128)S(1)}, u32[]{:S(2)}, u32[]{:S(2)}) %collective-permute-start.36) | collective-permute-done | bytes 65568 | tf_op jit(solution)/shard_map/ppermute | solution.py:33
  192.9 2.4 collective-permute-start.37
  195.4 4.0 %collective-permute-done.37 = f32[4,1,512]{2,1,0:T(1,128)S(1)} collective-permute-done((f32[4,1,512]{2,1,0:T(1,128)S(1)}, f32[4,1,512]{2,1,0:T(1,128)S(1)}, u32[]{:S(2)}, u32[]{:S(2)}) %collective-permute-start.37) | collective-permute-done | bytes 8224 | tf_op jit(solution)/shard_map/ppermute | solution.py:24
  199.9 1.9 collective-permute-start.39
  201.8 8.4 %collective-permute-done.39 = f32[4,8,512]{2,1,0:T(8,128)S(1)} collective-permute-done((f32[4,8,512]{2,1,0:T(8,128)S(1)}, f32[4,8,512]{2,1,0:T(8,128)S(1)}, u32[]{:S(2)}, u32[]{:S(2)}) %collective-permute-start.39) | collective-permute-done | bytes 65568 | tf_op jit(solution)/shard_map/ppermute | solution.py:33
  212.3 2.4 collective-permute-start.40
  214.8 4.0 %collective-permute-done.40 = f32[4,1,512]{2,1,0:T(1,128)S(1)} collective-permute-done((f32[4,1,512]{2,1,0:T(1,128)S(1)}, f32[4,1,512]{2,1,0:T(1,128)S(1)}, u32[]{:S(2)}, u32[]{:S(2)}) %collective-permute-start.40) | collective-permute-done | bytes 8224 | tf_op jit(solution)/shard_map/ppermute | solution.py:24
  221.2 8.4 %collective-permute-done.42 = f32[4,8,512]{2,1,0:T(8,128)S(1)} collective-permute-done((f32[4,8,512]{2,1,0:T(8,128)S(1)}, f32[4,8,512]{2,1,0:T(8,128)S(1)}, u32[]{:S(2)}, u32[]{:S(2)}) %collective-permute-start.42) | collective-permute-done | bytes 65568 | tf_op jit(solution)/shard_map/ppermute | solution.py:33
  231.7 2.4 collective-permute-start.43
  234.2 4.0 %collective-permute-done.43 = f32[4,1,512]{2,1,0:T(1,128)S(1)} collective-permute-done((f32[4,1,512]{2,1,0:T(1,128)S(1)}, f32[4,1,512]{2,1,0:T(1,128)S(1)}, u32[]{:S(2)}, u32[]{:S(2)}) %collective-permute-start.43) | collective-permute-done | bytes 8224 | tf_op jit(solution)/shard_map/ppermute | solution.py:24
  238.7 1.9 collective-permute-start.45
  240.6 8.4 %collective-permute-done.45 = f32[4,8,512]{2,1,0:T(8,128)S(1)} collective-permute-done((f32[4,8,512]{2,1,0:T(8,128)S(1)}, f32[4,8,512]{2,1,0:T(8,128)S(1)}, u32[]{:S(2)}, u32[]{:S(2)}) %collective-permute-start.45) | collective-permute-done | bytes 65568 | tf_op jit(solution)/shard_map/ppermute | solution.py:33
  251.1 2.4 collective-permute-start.46
  253.6 4.0 %collective-permute-done.46 = f32[4,1,512]{2,1,0:T(1,128)S(1)} collective-permute-done((f32[4,1,512]{2,1,0:T(1,128)S(1)}, f32[4,1,512]{2,1,0:T(1,128)S(1)}, u32[]{:S(2)}, u32[]{:S(2)}) %collective-permute-start.46) | collective-permute-done | bytes 8224 | tf_op jit(solution)/shard_map/ppermute | solution.py:24
  258.1 1.9 collective-permute-start.48
  260.0 8.4 %collective-permute-done.48 = f32[4,8,512]{2,1,0:T(8,128)S(1)} collective-permute-done((f32[4,8,512]{2,1,0:T(8,128)S(1)}, f32[4,8,512]{2,1,0:T(8,128)S(1)}, u32[]{:S(2)}, u32[]{:S(2)}) %collective-permute-start.48) | collective-permute-done | bytes 65568 | tf_op jit(solution)/shard_map/ppermute | solution.py:33
  270.5 2.4 collective-permute-start.49
  273.0 4.0 %collective-permute-done.49 = f32[4,1,512]{2,1,0:T(1,128)S(1)} collective-permute-done((f32[4,1,512]{2,1,0:T(1,128)S(1)}, f32[4,1,512]{2,1,0:T(1,128)S(1)}, u32[]{:S(2)}, u32[]{:S(2)}) %collective-permute-start.49) | collective-permute-done | bytes 8224 | tf_op jit(solution)/shard_map/ppermute | solution.py:24
  279.4 8.4 %collective-permute-done.51 = f32[4,8,512]{2,1,0:T(8,128)S(1)} collective-permute-done((f32[4,8,512]{2,1,0:T(8,128)S(1)}, f32[4,8,512]{2,1,0:T(8,128)S(1)}, u32[]{:S(2)}, u32[]{:S(2)}) %collective-permute-start.51) | collective-permute-done | bytes 65568 | tf_op jit(solution)/shard_map/ppermute | solution.py:33
  289.9 2.4 collective-permute-start.52
  292.4 4.0 %collective-permute-done.52 = f32[4,1,512]{2,1,0:T(1,128)S(1)} collective-permute-done((f32[4,1,512]{2,1,0:T(1,128)S(1)}, f32[4,1,512]{2,1,0:T(1,128)S(1)}, u32[]{:S(2)}, u32[]{:S(2)}) %collective-permute-start.52) | collective-permute-done | bytes 8224 | tf_op jit(solution)/shard_map/ppermute | solution.py:24
  298.8 8.4 %collective-permute-done.54 = f32[4,8,512]{2,1,0:T(8,128)S(1)} collective-permute-done((f32[4,8,512]{2,1,0:T(8,128)S(1)}, f32[4,8,512]{2,1,0:T(8,128)S(1)}, u32[]{:S(2)}, u32[]{:S(2)}) %collective-permute-start.54) | collective-permute-done | bytes 65568 | tf_op jit(solution)/shard_map/ppermute | solution.py:33
  309.3 2.4 collective-permute-start.55
  311.8 4.0 %collective-permute-done.55 = f32[4,1,512]{2,1,0:T(1,128)S(1)} collective-permute-done((f32[4,1,512]{2,1,0:T(1,128)S(1)}, f32[4,1,512]{2,1,0:T(1,128)S(1)}, u32[]{:S(2)}, u32[]{:S(2)}) %collective-permute-start.55) | collective-permute-done | bytes 8224 | tf_op jit(solution)/shard_map/ppermute | solution.py:24
  (455 shorter events, 64.3 us)
Async XLA Ops:
  0.0 0.8 copy-start.3
  0.0 0.8 copy-start.2
  0.0 5.6 %copy-start.4 = (f32[1,4,8,512]{3,2,1,0:T(8,128)S(1)}, f32[1,4,8,512]{3,2,1,0:T(8,128)}, u32[]{:S(2)}) copy-start(f32[1,4,8,512]{3,2,1,0:T(8,128)} %param.6) | copy-start | bytes 196612
  0.9 20.7 %copy-start.1 = (f32[4,8,512]{2,1,0:T(8,128)S(1)}, f32[4,8,512]{2,1,0:T(8,128)}, u32[]{:S(2)}) copy-start(f32[4,8,512]{2,1,0:T(8,128)} %param.5) | copy-start | bytes 196612
  0.9 33.2 %collective-permute-start.3 = (f32[2,1,512]{2,1,0:T(1,128)S(1)}, f32[2,1,512]{2,1,0:T(1,128)S(1)}, u32[]{:S(2)}, u32[]{:S(2)}) collective-permute-start(f32[2,1,512]{2,1,0:T(1,128)S(1)} %get-tuple-element.572), channel_id=1, source_target_pairs={{1,0},{2,1},{3,2},{0,3},{5,4},{6,5},{7,6},{4,7},{9,8},{10,9},{11,1... | collective-permute-start | bytes 12296 | tf_op jit(solution)/shard_map/ppermute | solution.py:25
  3.7 30.4 %collective-permute-start.4 = (f32[2,1,512]{2,1,0:T(1,128)S(1)}, f32[2,1,512]{2,1,0:T(1,128)S(1)}, u32[]{:S(2)}, u32[]{:S(2)}) collective-permute-start(f32[2,1,512]{2,1,0:T(1,128)S(1)} %get-tuple-element.573), channel_id=1, source_target_pairs={{0,1},{1,2},{2,3},{3,0},{4,5},{5,6},{6,7},{7,4},{8,9},{9,10},{10,1... | collective-permute-start | bytes 12296 | tf_op jit(solution)/shard_map/ppermute | solution.py:24
  5.6 16.0 %collective-permute-start = (f32[4,8,512]{2,1,0:T(8,128)S(1)}, f32[4,8,512]{2,1,0:T(8,128)S(1)}, u32[]{:S(2)}, u32[]{:S(2)}) collective-permute-start(f32[4,8,512]{2,1,0:T(8,128)S(1)} %bitcast.1725), channel_id=1, source_target_pairs={{0,4},{4,8},{8,12},{12,16},{16,20},{20,24},{24,28},{28,32},{32,36}... | collective-permute-start | bytes 196616 | tf_op jit(solution)/shard_map/ppermute | solution.py:33
  21.7 7.4 %collective-permute-start.2 = (f32[4,1,512]{2,1,0:T(1,128)S(1)}, f32[4,1,512]{2,1,0:T(1,128)S(1)}, u32[]{:S(2)}, u32[]{:S(2)}) collective-permute-start(f32[4,1,512]{2,1,0:T(1,128)S(1)} %get-tuple-element.570), channel_id=1, source_target_pairs={{1,0},{2,1},{3,2},{0,3},{5,4},{6,5},{7,6},{4,7},{9,8},{10,9},{11,1... | collective-permute-start | bytes 24584 | tf_op jit(solution)/shard_map/ppermute | solution.py:25
  27.1 6.5 %collective-permute-start.1 = (f32[4,1,512]{2,1,0:T(1,128)S(1)}, f32[4,1,512]{2,1,0:T(1,128)S(1)}, u32[]{:S(2)}, u32[]{:S(2)}) collective-permute-start(f32[4,1,512]{2,1,0:T(1,128)S(1)} %get-tuple-element.571), channel_id=1, source_target_pairs={{0,1},{1,2},{2,3},{3,0},{4,5},{5,6},{6,7},{7,4},{8,9},{9,10},{10,1... | collective-permute-start | bytes 24584 | tf_op jit(solution)/shard_map/ppermute | solution.py:24
  34.0 0.7 copy-start
  35.0 4.4 %collective-permute-start.6 = (f32[4,1,512]{2,1,0:T(1,128)S(1)}, f32[4,1,512]{2,1,0:T(1,128)S(1)}, u32[]{:S(2)}, u32[]{:S(2)}) collective-permute-start(f32[4,1,512]{2,1,0:T(1,128)S(1)} %get-tuple-element.560), channel_id=1, source_target_pairs={{1,0},{2,1},{3,2},{0,3},{5,4},{6,5},{7,6},{4,7},{9,8},{10,9},{11,1... | collective-permute-start | bytes 24584 | tf_op jit(solution)/shard_map/ppermute | solution.py:25
  36.9 6.5 %collective-permute-start.5 = (f32[4,1,512]{2,1,0:T(1,128)S(1)}, f32[4,1,512]{2,1,0:T(1,128)S(1)}, u32[]{:S(2)}, u32[]{:S(2)}) collective-permute-start(f32[4,1,512]{2,1,0:T(1,128)S(1)} %get-tuple-element.561), channel_id=1, source_target_pairs={{0,1},{1,2},{2,3},{3,0},{4,5},{5,6},{6,7},{7,4},{8,9},{9,10},{10,1... | collective-permute-start | bytes 24584 | tf_op jit(solution)/shard_map/ppermute | solution.py:24
  44.0 4.4 %collective-permute-start.8 = (f32[4,1,512]{2,1,0:T(1,128)S(1)}, f32[4,1,512]{2,1,0:T(1,128)S(1)}, u32[]{:S(2)}, u32[]{:S(2)}) collective-permute-start(f32[4,1,512]{2,1,0:T(1,128)S(1)} %get-tuple-element.550), channel_id=1, source_target_pairs={{1,0},{2,1},{3,2},{0,3},{5,4},{6,5},{7,6},{4,7},{9,8},{10,9},{11,1... | collective-permute-start | bytes 24584 | tf_op jit(solution)/shard_map/ppermute | solution.py:25
  45.9 6.5 %collective-permute-start.7 = (f32[4,1,512]{2,1,0:T(1,128)S(1)}, f32[4,1,512]{2,1,0:T(1,128)S(1)}, u32[]{:S(2)}, u32[]{:S(2)}) collective-permute-start(f32[4,1,512]{2,1,0:T(1,128)S(1)} %get-tuple-element.551), channel_id=1, source_target_pairs={{0,1},{1,2},{2,3},{3,0},{4,5},{5,6},{6,7},{7,4},{8,9},{9,10},{10,1... | collective-permute-start | bytes 24584 | tf_op jit(solution)/shard_map/ppermute | solution.py:24
  52.9 4.4 %collective-permute-start.10 = (f32[4,1,512]{2,1,0:T(1,128)S(1)}, f32[4,1,512]{2,1,0:T(1,128)S(1)}, u32[]{:S(2)}, u32[]{:S(2)}) collective-permute-start(f32[4,1,512]{2,1,0:T(1,128)S(1)} %get-tuple-element.540), channel_id=1, source_target_pairs={{1,0},{2,1},{3,2},{0,3},{5,4},{6,5},{7,6},{4,7},{9,8},{10,9},{11,1... | collective-permute-start | bytes 24584 | tf_op jit(solution)/shard_map/ppermute | solution.py:25
  54.9 6.5 %collective-permute-start.9 = (f32[4,1,512]{2,1,0:T(1,128)S(1)}, f32[4,1,512]{2,1,0:T(1,128)S(1)}, u32[]{:S(2)}, u32[]{:S(2)}) collective-permute-start(f32[4,1,512]{2,1,0:T(1,128)S(1)} %get-tuple-element.541), channel_id=1, source_target_pairs={{0,1},{1,2},{2,3},{3,0},{4,5},{5,6},{6,7},{7,4},{8,9},{9,10},{10,1... | collective-permute-start | bytes 24584 | tf_op jit(solution)/shard_map/ppermute | solution.py:24
  61.9 4.4 %collective-permute-start.12 = (f32[4,1,512]{2,1,0:T(1,128)S(1)}, f32[4,1,512]{2,1,0:T(1,128)S(1)}, u32[]{:S(2)}, u32[]{:S(2)}) collective-permute-start(f32[4,1,512]{2,1,0:T(1,128)S(1)} %get-tuple-element.530), channel_id=1, source_target_pairs={{1,0},{2,1},{3,2},{0,3},{5,4},{6,5},{7,6},{4,7},{9,8},{10,9},{11,1... | collective-permute-start | bytes 24584 | tf_op jit(solution)/shard_map/ppermute | solution.py:25
  63.9 6.5 %collective-permute-start.11 = (f32[4,1,512]{2,1,0:T(1,128)S(1)}, f32[4,1,512]{2,1,0:T(1,128)S(1)}, u32[]{:S(2)}, u32[]{:S(2)}) collective-permute-start(f32[4,1,512]{2,1,0:T(1,128)S(1)} %get-tuple-element.531), channel_id=1, source_target_pairs={{0,1},{1,2},{2,3},{3,0},{4,5},{5,6},{6,7},{7,4},{8,9},{9,10},{10,1... | collective-permute-start | bytes 24584 | tf_op jit(solution)/shard_map/ppermute | solution.py:24
  70.9 4.4 %collective-permute-start.14 = (f32[4,1,512]{2,1,0:T(1,128)S(1)}, f32[4,1,512]{2,1,0:T(1,128)S(1)}, u32[]{:S(2)}, u32[]{:S(2)}) collective-permute-start(f32[4,1,512]{2,1,0:T(1,128)S(1)} %get-tuple-element.520), channel_id=1, source_target_pairs={{1,0},{2,1},{3,2},{0,3},{5,4},{6,5},{7,6},{4,7},{9,8},{10,9},{11,1... | collective-permute-start | bytes 24584 | tf_op jit(solution)/shard_map/ppermute | solution.py:25
  72.9 6.5 %collective-permute-start.13 = (f32[4,1,512]{2,1,0:T(1,128)S(1)}, f32[4,1,512]{2,1,0:T(1,128)S(1)}, u32[]{:S(2)}, u32[]{:S(2)}) collective-permute-start(f32[4,1,512]{2,1,0:T(1,128)S(1)} %get-tuple-element.521), channel_id=1, source_target_pairs={{0,1},{1,2},{2,3},{3,0},{4,5},{5,6},{6,7},{7,4},{8,9},{9,10},{10,1... | collective-permute-start | bytes 24584 | tf_op jit(solution)/shard_map/ppermute | solution.py:24
  79.9 4.4 %collective-permute-start.16 = (f32[4,1,512]{2,1,0:T(1,128)S(1)}, f32[4,1,512]{2,1,0:T(1,128)S(1)}, u32[]{:S(2)}, u32[]{:S(2)}) collective-permute-start(f32[4,1,512]{2,1,0:T(1,128)S(1)} %get-tuple-element.510), channel_id=1, source_target_pairs={{1,0},{2,1},{3,2},{0,3},{5,4},{6,5},{7,6},{4,7},{9,8},{10,9},{11,1... | collective-permute-start | bytes 24584 | tf_op jit(solution)/shard_map/ppermute | solution.py:25
  81.9 6.5 %collective-permute-start.15 = (f32[4,1,512]{2,1,0:T(1,128)S(1)}, f32[4,1,512]{2,1,0:T(1,128)S(1)}, u32[]{:S(2)}, u32[]{:S(2)}) collective-permute-start(f32[4,1,512]{2,1,0:T(1,128)S(1)} %get-tuple-element.511), channel_id=1, source_target_pairs={{0,1},{1,2},{2,3},{3,0},{4,5},{5,6},{6,7},{7,4},{8,9},{9,10},{10,1... | collective-permute-start | bytes 24584 | tf_op jit(solution)/shard_map/ppermute | solution.py:24
  88.9 4.4 %collective-permute-start.18 = (f32[4,1,512]{2,1,0:T(1,128)S(1)}, f32[4,1,512]{2,1,0:T(1,128)S(1)}, u32[]{:S(2)}, u32[]{:S(2)}) collective-permute-start(f32[4,1,512]{2,1,0:T(1,128)S(1)} %get-tuple-element.500), channel_id=1, source_target_pairs={{1,0},{2,1},{3,2},{0,3},{5,4},{6,5},{7,6},{4,7},{9,8},{10,9},{11,1... | collective-permute-start | bytes 24584 | tf_op jit(solution)/shard_map/ppermute | solution.py:25
  90.9 6.5 %collective-permute-start.17 = (f32[4,1,512]{2,1,0:T(1,128)S(1)}, f32[4,1,512]{2,1,0:T(1,128)S(1)}, u32[]{:S(2)}, u32[]{:S(2)}) collective-permute-start(f32[4,1,512]{2,1,0:T(1,128)S(1)} %get-tuple-element.501), channel_id=1, source_target_pairs={{0,1},{1,2},{2,3},{3,0},{4,5},{5,6},{6,7},{7,4},{8,9},{9,10},{10,1... | collective-permute-start | bytes 24584 | tf_op jit(solution)/shard_map/ppermute | solution.py:24
  97.8 10.4 %collective-permute-start.19 = (f32[4,8,512]{2,1,0:T(8,128)S(1)}, f32[4,8,512]{2,1,0:T(8,128)S(1)}, u32[]{:S(2)}, u32[]{:S(2)}) collective-permute-start(f32[4,8,512]{2,1,0:T(8,128)S(1)} %pad_maximum_fusion.191), channel_id=1, source_target_pairs={{0,4},{4,8},{8,12},{12,16},{16,20},{20,24},{24,28},{28,32},{32,36}... | collective-permute-start | bytes 196616 | tf_op jit(solution)/shard_map/ppermute | solution.py:33
  108.3 4.4 %collective-permute-start.21 = (f32[4,1,512]{2,1,0:T(1,128)S(1)}, f32[4,1,512]{2,1,0:T(1,128)S(1)}, u32[]{:S(2)}, u32[]{:S(2)}) collective-permute-start(f32[4,1,512]{2,1,0:T(1,128)S(1)} %get-tuple-element.490), channel_id=1, source_target_pairs={{1,0},{2,1},{3,2},{0,3},{5,4},{6,5},{7,6},{4,7},{9,8},{10,9},{11,1... | collective-permute-start | bytes 24584 | tf_op jit(solution)/shard_map/ppermute | solution.py:25
  110.2 6.5 %collective-permute-start.20 = (f32[4,1,512]{2,1,0:T(1,128)S(1)}, f32[4,1,512]{2,1,0:T(1,128)S(1)}, u32[]{:S(2)}, u32[]{:S(2)}) collective-permute-start(f32[4,1,512]{2,1,0:T(1,128)S(1)} %get-tuple-element.491), channel_id=1, source_target_pairs={{0,1},{1,2},{2,3},{3,0},{4,5},{5,6},{6,7},{7,4},{8,9},{9,10},{10,1... | collective-permute-start | bytes 24584 | tf_op jit(solution)/shard_map/ppermute | solution.py:24
  117.5 4.4 %collective-permute-start.23 = (f32[4,1,512]{2,1,0:T(1,128)S(1)}, f32[4,1,512]{2,1,0:T(1,128)S(1)}, u32[]{:S(2)}, u32[]{:S(2)}) collective-permute-start(f32[4,1,512]{2,1,0:T(1,128)S(1)} %get-tuple-element.475), channel_id=1, source_target_pairs={{1,0},{2,1},{3,2},{0,3},{5,4},{6,5},{7,6},{4,7},{9,8},{10,9},{11,1... | collective-permute-start | bytes 24584 | tf_op jit(solution)/shard_map/ppermute | solution.py:25
  119.4 6.5 %collective-permute-start.22 = (f32[4,1,512]{2,1,0:T(1,128)S(1)}, f32[4,1,512]{2,1,0:T(1,128)S(1)}, u32[]{:S(2)}, u32[]{:S(2)}) collective-permute-start(f32[4,1,512]{2,1,0:T(1,128)S(1)} %get-tuple-element.476), channel_id=1, source_target_pairs={{0,1},{1,2},{2,3},{3,0},{4,5},{5,6},{6,7},{7,4},{8,9},{9,10},{10,1... | collective-permute-start | bytes 24584 | tf_op jit(solution)/shard_map/ppermute | solution.py:24
  126.5 4.4 %collective-permute-start.25 = (f32[4,1,512]{2,1,0:T(1,128)S(1)}, f32[4,1,512]{2,1,0:T(1,128)S(1)}, u32[]{:S(2)}, u32[]{:S(2)}) collective-permute-start(f32[4,1,512]{2,1,0:T(1,128)S(1)} %get-tuple-element.465), channel_id=1, source_target_pairs={{1,0},{2,1},{3,2},{0,3},{5,4},{6,5},{7,6},{4,7},{9,8},{10,9},{11,1... | collective-permute-start | bytes 24584 | tf_op jit(solution)/shard_map/ppermute | solution.py:25
  128.5 6.5 %collective-permute-start.24 = (f32[4,1,512]{2,1,0:T(1,128)S(1)}, f32[4,1,512]{2,1,0:T(1,128)S(1)}, u32[]{:S(2)}, u32[]{:S(2)}) collective-permute-start(f32[4,1,512]{2,1,0:T(1,128)S(1)} %get-tuple-element.466), channel_id=1, source_target_pairs={{0,1},{1,2},{2,3},{3,0},{4,5},{5,6},{6,7},{7,4},{8,9},{9,10},{10,1... | collective-permute-start | bytes 24584 | tf_op jit(solution)/shard_map/ppermute | solution.py:24
  135.5 4.4 %collective-permute-start.27 = (f32[4,1,512]{2,1,0:T(1,128)S(1)}, f32[4,1,512]{2,1,0:T(1,128)S(1)}, u32[]{:S(2)}, u32[]{:S(2)}) collective-permute-start(f32[4,1,512]{2,1,0:T(1,128)S(1)} %get-tuple-element.455), channel_id=1, source_target_pairs={{1,0},{2,1},{3,2},{0,3},{5,4},{6,5},{7,6},{4,7},{9,8},{10,9},{11,1... | collective-permute-start | bytes 24584 | tf_op jit(solution)/shard_map/ppermute | solution.py:25
  137.5 6.5 %collective-permute-start.26 = (f32[4,1,512]{2,1,0:T(1,128)S(1)}, f32[4,1,512]{2,1,0:T(1,128)S(1)}, u32[]{:S(2)}, u32[]{:S(2)}) collective-permute-start(f32[4,1,512]{2,1,0:T(1,128)S(1)} %get-tuple-element.456), channel_id=1, source_target_pairs={{0,1},{1,2},{2,3},{3,0},{4,5},{5,6},{6,7},{7,4},{8,9},{9,10},{10,1... | collective-permute-start | bytes 24584 | tf_op jit(solution)/shard_map/ppermute | solution.py:24
  144.5 4.4 %collective-permute-start.29 = (f32[4,1,512]{2,1,0:T(1,128)S(1)}, f32[4,1,512]{2,1,0:T(1,128)S(1)}, u32[]{:S(2)}, u32[]{:S(2)}) collective-permute-start(f32[4,1,512]{2,1,0:T(1,128)S(1)} %get-tuple-element.445), channel_id=1, source_target_pairs={{1,0},{2,1},{3,2},{0,3},{5,4},{6,5},{7,6},{4,7},{9,8},{10,9},{11,1... | collective-permute-start | bytes 24584 | tf_op jit(solution)/shard_map/ppermute | solution.py:25
  146.5 6.5 %collective-permute-start.28 = (f32[4,1,512]{2,1,0:T(1,128)S(1)}, f32[4,1,512]{2,1,0:T(1,128)S(1)}, u32[]{:S(2)}, u32[]{:S(2)}) collective-permute-start(f32[4,1,512]{2,1,0:T(1,128)S(1)} %get-tuple-element.446), channel_id=1, source_target_pairs={{0,1},{1,2},{2,3},{3,0},{4,5},{5,6},{6,7},{7,4},{8,9},{9,10},{10,1... | collective-permute-start | bytes 24584 | tf_op jit(solution)/shard_map/ppermute | solution.py:24
  153.5 4.4 %collective-permute-start.31 = (f32[4,1,512]{2,1,0:T(1,128)S(1)}, f32[4,1,512]{2,1,0:T(1,128)S(1)}, u32[]{:S(2)}, u32[]{:S(2)}) collective-permute-start(f32[4,1,512]{2,1,0:T(1,128)S(1)} %get-tuple-element.435), channel_id=1, source_target_pairs={{1,0},{2,1},{3,2},{0,3},{5,4},{6,5},{7,6},{4,7},{9,8},{10,9},{11,1... | collective-permute-start | bytes 24584 | tf_op jit(solution)/shard_map/ppermute | solution.py:25
  155.5 6.5 %collective-permute-start.30 = (f32[4,1,512]{2,1,0:T(1,128)S(1)}, f32[4,1,512]{2,1,0:T(1,128)S(1)}, u32[]{:S(2)}, u32[]{:S(2)}) collective-permute-start(f32[4,1,512]{2,1,0:T(1,128)S(1)} %get-tuple-element.436), channel_id=1, source_target_pairs={{0,1},{1,2},{2,3},{3,0},{4,5},{5,6},{6,7},{7,4},{8,9},{9,10},{10,1... | collective-permute-start | bytes 24584 | tf_op jit(solution)/shard_map/ppermute | solution.py:24
  162.5 4.4 %collective-permute-start.33 = (f32[4,1,512]{2,1,0:T(1,128)S(1)}, f32[4,1,512]{2,1,0:T(1,128)S(1)}, u32[]{:S(2)}, u32[]{:S(2)}) collective-permute-start(f32[4,1,512]{2,1,0:T(1,128)S(1)} %get-tuple-element.425), channel_id=1, source_target_pairs={{1,0},{2,1},{3,2},{0,3},{5,4},{6,5},{7,6},{4,7},{9,8},{10,9},{11,1... | collective-permute-start | bytes 24584 | tf_op jit(solution)/shard_map/ppermute | solution.py:25
  164.5 6.5 %collective-permute-start.32 = (f32[4,1,512]{2,1,0:T(1,128)S(1)}, f32[4,1,512]{2,1,0:T(1,128)S(1)}, u32[]{:S(2)}, u32[]{:S(2)}) collective-permute-start(f32[4,1,512]{2,1,0:T(1,128)S(1)} %get-tuple-element.426), channel_id=1, source_target_pairs={{0,1},{1,2},{2,3},{3,0},{4,5},{5,6},{6,7},{7,4},{8,9},{9,10},{10,1... | collective-permute-start | bytes 24584 | tf_op jit(solution)/shard_map/ppermute | solution.py:24
  171.5 4.4 %collective-permute-start.35 = (f32[4,1,512]{2,1,0:T(1,128)S(1)}, f32[4,1,512]{2,1,0:T(1,128)S(1)}, u32[]{:S(2)}, u32[]{:S(2)}) collective-permute-start(f32[4,1,512]{2,1,0:T(1,128)S(1)} %get-tuple-element.415), channel_id=1, source_target_pairs={{1,0},{2,1},{3,2},{0,3},{5,4},{6,5},{7,6},{4,7},{9,8},{10,9},{11,1... | collective-permute-start | bytes 24584 | tf_op jit(solution)/shard_map/ppermute | solution.py:25
  173.5 6.5 %collective-permute-start.34 = (f32[4,1,512]{2,1,0:T(1,128)S(1)}, f32[4,1,512]{2,1,0:T(1,128)S(1)}, u32[]{:S(2)}, u32[]{:S(2)}) collective-permute-start(f32[4,1,512]{2,1,0:T(1,128)S(1)} %get-tuple-element.416), channel_id=1, source_target_pairs={{0,1},{1,2},{2,3},{3,0},{4,5},{5,6},{6,7},{7,4},{8,9},{9,10},{10,1... | collective-permute-start | bytes 24584 | tf_op jit(solution)/shard_map/ppermute | solution.py:24
  180.4 10.4 %collective-permute-start.36 = (f32[4,8,512]{2,1,0:T(8,128)S(1)}, f32[4,8,512]{2,1,0:T(8,128)S(1)}, u32[]{:S(2)}, u32[]{:S(2)}) collective-permute-start(f32[4,8,512]{2,1,0:T(8,128)S(1)} %get-tuple-element.39), channel_id=1, source_target_pairs={{0,4},{4,8},{8,12},{12,16},{16,20},{20,24},{24,28},{28,32},{32,36}... | collective-permute-start | bytes 196616 | tf_op jit(solution)/shard_map/ppermute | solution.py:33
  191.0 4.4 %collective-permute-start.38 = (f32[4,1,512]{2,1,0:T(1,128)S(1)}, f32[4,1,512]{2,1,0:T(1,128)S(1)}, u32[]{:S(2)}, u32[]{:S(2)}) collective-permute-start(f32[4,1,512]{2,1,0:T(1,128)S(1)} %get-tuple-element.405), channel_id=1, source_target_pairs={{1,0},{2,1},{3,2},{0,3},{5,4},{6,5},{7,6},{4,7},{9,8},{10,9},{11,1... | collective-permute-start | bytes 24584 | tf_op jit(solution)/shard_map/ppermute | solution.py:25
  192.9 6.5 %collective-permute-start.37 = (f32[4,1,512]{2,1,0:T(1,128)S(1)}, f32[4,1,512]{2,1,0:T(1,128)S(1)}, u32[]{:S(2)}, u32[]{:S(2)}) collective-permute-start(f32[4,1,512]{2,1,0:T(1,128)S(1)} %get-tuple-element.406), channel_id=1, source_target_pairs={{0,1},{1,2},{2,3},{3,0},{4,5},{5,6},{6,7},{7,4},{8,9},{9,10},{10,1... | collective-permute-start | bytes 24584 | tf_op jit(solution)/shard_map/ppermute | solution.py:24
  199.9 10.4 %collective-permute-start.39 = (f32[4,8,512]{2,1,0:T(8,128)S(1)}, f32[4,8,512]{2,1,0:T(8,128)S(1)}, u32[]{:S(2)}, u32[]{:S(2)}) collective-permute-start(f32[4,8,512]{2,1,0:T(8,128)S(1)} %fusion.180), channel_id=1, source_target_pairs={{0,4},{4,8},{8,12},{12,16},{16,20},{20,24},{24,28},{28,32},{32,36}... | collective-permute-start | bytes 196616 | tf_op jit(solution)/shard_map/ppermute | solution.py:33
  210.4 4.4 %collective-permute-start.41 = (f32[4,1,512]{2,1,0:T(1,128)S(1)}, f32[4,1,512]{2,1,0:T(1,128)S(1)}, u32[]{:S(2)}, u32[]{:S(2)}) collective-permute-start(f32[4,1,512]{2,1,0:T(1,128)S(1)} %get-tuple-element.395), channel_id=1, source_target_pairs={{1,0},{2,1},{3,2},{0,3},{5,4},{6,5},{7,6},{4,7},{9,8},{10,9},{11,1... | collective-permute-start | bytes 24584 | tf_op jit(solution)/shard_map/ppermute | solution.py:25
  212.3 6.5 %collective-permute-start.40 = (f32[4,1,512]{2,1,0:T(1,128)S(1)}, f32[4,1,512]{2,1,0:T(1,128)S(1)}, u32[]{:S(2)}, u32[]{:S(2)}) collective-permute-start(f32[4,1,512]{2,1,0:T(1,128)S(1)} %get-tuple-element.396), channel_id=1, source_target_pairs={{0,1},{1,2},{2,3},{3,0},{4,5},{5,6},{6,7},{7,4},{8,9},{9,10},{10,1... | collective-permute-start | bytes 24584 | tf_op jit(solution)/shard_map/ppermute | solution.py:24
  219.3 10.4 %collective-permute-start.42 = (f32[4,8,512]{2,1,0:T(8,128)S(1)}, f32[4,8,512]{2,1,0:T(8,128)S(1)}, u32[]{:S(2)}, u32[]{:S(2)}) collective-permute-start(f32[4,8,512]{2,1,0:T(8,128)S(1)} %fusion.181), channel_id=1, source_target_pairs={{0,4},{4,8},{8,12},{12,16},{16,20},{20,24},{24,28},{28,32},{32,36}... | collective-permute-start | bytes 196616 | tf_op jit(solution)/shard_map/ppermute | solution.py:33
  229.8 4.4 %collective-permute-start.44 = (f32[4,1,512]{2,1,0:T(1,128)S(1)}, f32[4,1,512]{2,1,0:T(1,128)S(1)}, u32[]{:S(2)}, u32[]{:S(2)}) collective-permute-start(f32[4,1,512]{2,1,0:T(1,128)S(1)} %get-tuple-element.385), channel_id=1, source_target_pairs={{1,0},{2,1},{3,2},{0,3},{5,4},{6,5},{7,6},{4,7},{9,8},{10,9},{11,1... | collective-permute-start | bytes 24584 | tf_op jit(solution)/shard_map/ppermute | solution.py:25
  231.7 6.5 %collective-permute-start.43 = (f32[4,1,512]{2,1,0:T(1,128)S(1)}, f32[4,1,512]{2,1,0:T(1,128)S(1)}, u32[]{:S(2)}, u32[]{:S(2)}) collective-permute-start(f32[4,1,512]{2,1,0:T(1,128)S(1)} %get-tuple-element.386), channel_id=1, source_target_pairs={{0,1},{1,2},{2,3},{3,0},{4,5},{5,6},{6,7},{7,4},{8,9},{9,10},{10,1... | collective-permute-start | bytes 24584 | tf_op jit(solution)/shard_map/ppermute | solution.py:24
  238.7 10.4 %collective-permute-start.45 = (f32[4,8,512]{2,1,0:T(8,128)S(1)}, f32[4,8,512]{2,1,0:T(8,128)S(1)}, u32[]{:S(2)}, u32[]{:S(2)}) collective-permute-start(f32[4,8,512]{2,1,0:T(8,128)S(1)} %fusion.182), channel_id=1, source_target_pairs={{0,4},{4,8},{8,12},{12,16},{16,20},{20,24},{24,28},{28,32},{32,36}... | collective-permute-start | bytes 196616 | tf_op jit(solution)/shard_map/ppermute | solution.py:33
  249.2 4.4 %collective-permute-start.47 = (f32[4,1,512]{2,1,0:T(1,128)S(1)}, f32[4,1,512]{2,1,0:T(1,128)S(1)}, u32[]{:S(2)}, u32[]{:S(2)}) collective-permute-start(f32[4,1,512]{2,1,0:T(1,128)S(1)} %get-tuple-element.375), channel_id=1, source_target_pairs={{1,0},{2,1},{3,2},{0,3},{5,4},{6,5},{7,6},{4,7},{9,8},{10,9},{11,1... | collective-permute-start | bytes 24584 | tf_op jit(solution)/shard_map/ppermute | solution.py:25
  251.1 6.5 %collective-permute-start.46 = (f32[4,1,512]{2,1,0:T(1,128)S(1)}, f32[4,1,512]{2,1,0:T(1,128)S(1)}, u32[]{:S(2)}, u32[]{:S(2)}) collective-permute-start(f32[4,1,512]{2,1,0:T(1,128)S(1)} %get-tuple-element.376), channel_id=1, source_target_pairs={{0,1},{1,2},{2,3},{3,0},{4,5},{5,6},{6,7},{7,4},{8,9},{9,10},{10,1... | collective-permute-start | bytes 24584 | tf_op jit(solution)/shard_map/ppermute | solution.py:24
  258.1 10.4 %collective-permute-start.48 = (f32[4,8,512]{2,1,0:T(8,128)S(1)}, f32[4,8,512]{2,1,0:T(8,128)S(1)}, u32[]{:S(2)}, u32[]{:S(2)}) collective-permute-start(f32[4,8,512]{2,1,0:T(8,128)S(1)} %fusion.183), channel_id=1, source_target_pairs={{0,4},{4,8},{8,12},{12,16},{16,20},{20,24},{24,28},{28,32},{32,36}... | collective-permute-start | bytes 196616 | tf_op jit(solution)/shard_map/ppermute | solution.py:33
  268.6 4.4 %collective-permute-start.50 = (f32[4,1,512]{2,1,0:T(1,128)S(1)}, f32[4,1,512]{2,1,0:T(1,128)S(1)}, u32[]{:S(2)}, u32[]{:S(2)}) collective-permute-start(f32[4,1,512]{2,1,0:T(1,128)S(1)} %get-tuple-element.365), channel_id=1, source_target_pairs={{1,0},{2,1},{3,2},{0,3},{5,4},{6,5},{7,6},{4,7},{9,8},{10,9},{11,1... | collective-permute-start | bytes 24584 | tf_op jit(solution)/shard_map/ppermute | solution.py:25
  270.5 6.5 %collective-permute-start.49 = (f32[4,1,512]{2,1,0:T(1,128)S(1)}, f32[4,1,512]{2,1,0:T(1,128)S(1)}, u32[]{:S(2)}, u32[]{:S(2)}) collective-permute-start(f32[4,1,512]{2,1,0:T(1,128)S(1)} %get-tuple-element.366), channel_id=1, source_target_pairs={{0,1},{1,2},{2,3},{3,0},{4,5},{5,6},{6,7},{7,4},{8,9},{9,10},{10,1... | collective-permute-start | bytes 24584 | tf_op jit(solution)/shard_map/ppermute | solution.py:24
  277.5 10.4 %collective-permute-start.51 = (f32[4,8,512]{2,1,0:T(8,128)S(1)}, f32[4,8,512]{2,1,0:T(8,128)S(1)}, u32[]{:S(2)}, u32[]{:S(2)}) collective-permute-start(f32[4,8,512]{2,1,0:T(8,128)S(1)} %fusion.184), channel_id=1, source_target_pairs={{0,4},{4,8},{8,12},{12,16},{16,20},{20,24},{24,28},{28,32},{32,36}... | collective-permute-start | bytes 196616 | tf_op jit(solution)/shard_map/ppermute | solution.py:33
  288.0 4.4 %collective-permute-start.53 = (f32[4,1,512]{2,1,0:T(1,128)S(1)}, f32[4,1,512]{2,1,0:T(1,128)S(1)}, u32[]{:S(2)}, u32[]{:S(2)}) collective-permute-start(f32[4,1,512]{2,1,0:T(1,128)S(1)} %get-tuple-element.355), channel_id=1, source_target_pairs={{1,0},{2,1},{3,2},{0,3},{5,4},{6,5},{7,6},{4,7},{9,8},{10,9},{11,1... | collective-permute-start | bytes 24584 | tf_op jit(solution)/shard_map/ppermute | solution.py:25
  289.9 6.5 %collective-permute-start.52 = (f32[4,1,512]{2,1,0:T(1,128)S(1)}, f32[4,1,512]{2,1,0:T(1,128)S(1)}, u32[]{:S(2)}, u32[]{:S(2)}) collective-permute-start(f32[4,1,512]{2,1,0:T(1,128)S(1)} %get-tuple-element.356), channel_id=1, source_target_pairs={{0,1},{1,2},{2,3},{3,0},{4,5},{5,6},{6,7},{7,4},{8,9},{9,10},{10,1... | collective-permute-start | bytes 24584 | tf_op jit(solution)/shard_map/ppermute | solution.py:24
  296.9 10.4 %collective-permute-start.54 = (f32[4,8,512]{2,1,0:T(8,128)S(1)}, f32[4,8,512]{2,1,0:T(8,128)S(1)}, u32[]{:S(2)}, u32[]{:S(2)}) collective-permute-start(f32[4,8,512]{2,1,0:T(8,128)S(1)} %fusion.185), channel_id=1, source_target_pairs={{0,4},{4,8},{8,12},{12,16},{16,20},{20,24},{24,28},{28,32},{32,36}... | collective-permute-start | bytes 196616 | tf_op jit(solution)/shard_map/ppermute | solution.py:33
  307.4 4.4 %collective-permute-start.56 = (f32[4,1,512]{2,1,0:T(1,128)S(1)}, f32[4,1,512]{2,1,0:T(1,128)S(1)}, u32[]{:S(2)}, u32[]{:S(2)}) collective-permute-start(f32[4,1,512]{2,1,0:T(1,128)S(1)} %get-tuple-element.345), channel_id=1, source_target_pairs={{1,0},{2,1},{3,2},{0,3},{5,4},{6,5},{7,6},{4,7},{9,8},{10,9},{11,1... | collective-permute-start | bytes 24584 | tf_op jit(solution)/shard_map/ppermute | solution.py:25
  309.3 6.5 %collective-permute-start.55 = (f32[4,1,512]{2,1,0:T(1,128)S(1)}, f32[4,1,512]{2,1,0:T(1,128)S(1)}, u32[]{:S(2)}, u32[]{:S(2)}) collective-permute-start(f32[4,1,512]{2,1,0:T(1,128)S(1)} %get-tuple-element.346), channel_id=1, source_target_pairs={{0,1},{1,2},{2,3},{3,0},{4,5},{5,6},{6,7},{7,4},{8,9},{9,10},{10,1... | collective-permute-start | bytes 24584 | tf_op jit(solution)/shard_map/ppermute | solution.py:24
where the time goes:
time: 319 us; the launch traced here: 317 us
  waiting for transfers between devices  172 us (54%)
  starting transfers between devices  126 us (39%)
  local copies, waits for them, and re-layouts  8.21 us (3%)
  other arithmetic  8.05 us (3%)
    ppermute x24, waiting for transfers between devices, with_halo(): before = lax.ppermute(last, axis, up)  92.1 us
    ppermute x9, waiting for transfers between devices, from_behind(): lax.ppermute(value, axis, [(source, source + steps) for source in range(i...  79.7 us
    ppermute x24, starting transfers between devices, with_halo(): before = lax.ppermute(last, axis, up)  56.8 us
    ppermute x24, starting transfers between devices, with_halo(): after = lax.ppermute(initial, axis, down)  50.3 us
    ppermute x9, starting transfers between devices, from_behind(): lax.ppermute(value, axis, [(source, source + steps) for source in range(i...  19.2 us
  transfers between devices with their start and end apart: 57, of which 32 were waited for; matrix products, arithmetic and copies ran while one was open for 1% of the time, Pallas kernels for 0%

commit v1 on v0

v1 whole, which is shorter than its diff:
```python
import jax
import jax.numpy as jnp
from jax import lax
from jax.experimental import pallas as pl
from jax.experimental.pallas import tpu as pltpu
from jax.sharding import PartitionSpec as P

FINE_STEPS = 8
FINE = (0.0375, 0.025)
COARSE = (0.3, 0.2)
FIELDS = 4
TILE = (8, 128)
AXES = ("tm", "rows")


def east(x):
    return pltpu.roll(x, 127, 1)


def west(x):
    return pltpu.roll(x, 1, 1)


def north(tiles):
    return [*tiles[1:], pltpu.roll(tiles[0], 7, 0)]


def south(tiles):
    return [pltpu.roll(tiles[3], 1, 0), *tiles[:3]]


def advance(state, statics, ratio, viscous):
    slope_e, slope_n, wet = statics
    half = 0.5 * ratio
    h, p, s, m = state
    inverse = [1.0 / a for a in h]
    u = [a * b for a, b in zip(p, inverse)]
    v = [a * b for a, b in zip(s, inverse)]
    hu = [half * a for a in u]
    hv = [half * a for a in v]
    pressure = [(0.5 * half) * (a * a) for a in h]
    cross = [a * b for a, b in zip(s, hu)]
    east_flux = (
        [half * a for a in p],
        [a * b + c for a, b, c in zip(p, hu, pressure)],
        cross,
        [a * b for a, b in zip(m, hu)],
    )
    north_flux = (
        [half * a for a in s],
        cross,
        [a * b + c for a, b, c in zip(s, hv, pressure)],
        [a * b for a, b in zip(m, hv)],
    )
    moved = []
    for field in range(FIELDS):
        q = state[field]
        near = [viscous * a for a in q]
        up = north([a - b for a, b in zip(near, north_flux[field])])
        down = south([a + b for a, b in zip(near, north_flux[field])])
        tiles = []
        for k in range(4):
            lanes = east(near[k] - east_flux[field][k]) + west(near[k] + east_flux[field][k])
            tiles.append((1.0 - 4.0 * viscous) * q[k] + (lanes + (up[k] + down[k])))
        moved.append(tiles)
    new_p, new_s, new_m = [], [], []
    for k in range(4):
        square = u[k] * u[k] + v[k] * v[k]
        drag = (0.02 * ratio) * jnp.sqrt(square)
        new_p.append(wet[k] * (moved[1][k] - (h[k] * slope_e[k] + drag * u[k])))
        new_s.append(wet[k] * (moved[2][k] - (h[k] * slope_n[k] + drag * v[k])))
        new_m.append(
            moved[3][k] + ((0.05 * ratio) * square - (0.3 * ratio) * (m[k] * inverse[k]))
        )
    return [moved[0], new_p, new_s, new_m]


def scaled(slopes, ratio):
    slope_e, slope_n, wet = slopes
    return [ratio * a for a in slope_e], [ratio * a for a in slope_n], wet


def flat(nested):
    return jax.tree.leaves(nested)


def combine(function, a, b):
    return jax.tree.map(function, a, b)


def read_tiles(ref, *lead):
    return [[ref[(*lead, field, k)] for k in range(4)] for field in range(FIELDS)]


def write_tiles(ref, state, *lead):
    for field in range(FIELDS):
        for k in range(4):
            ref[(*lead, field, k)] = state[field][k]


def lane_index():
    return lax.broadcasted_iota(jnp.int32, TILE, 1)


def pack_kernel(start_ref, guess_ref, mask_ref, class_ref, table_ref, out_ref):
    time_index = lax.axis_index("tm")
    lanes = lane_index()
    use_start = time_index >= lax.axis_size("tm") - 2
    odd = time_index % 2 == 1

    def windows(plane, chunks):
        ahead = [pltpu.roll(a, 32, 1) for a in chunks]
        behind = [pltpu.roll(a, 96, 1) for a in chunks]
        for c in range(4):
            out_ref[2 * c, plane] = jnp.where(lanes < 32, ahead[c - 1], ahead[c])
            out_ref[2 * c + 1, plane] = jnp.where(lanes < 96, behind[c], behind[(c + 1) % 4])

    cuts = [pl.ds(128 * c, 128) for c in range(4)]
    for field in range(FIELDS):
        windows(
            field,
            [jnp.where(use_start, start_ref[field, :, cut], guess_ref[0, field, :, cut]) for cut in cuts],
        )
    static = []
    for cut in cuts:
        classes = class_ref[:, cut]
        bed = jnp.zeros(TILE, jnp.float32)
        for index in range(table_ref.shape[0]):
            bed = jnp.where(classes == index, table_ref[index], bed)
        static.append(jnp.where(odd, mask_ref[:, cut].astype(jnp.float32), bed))
    windows(FIELDS, static)


def forcing_kernel(in_ref, forcing_ref, chain_ref, before_ref, slope_ref, rows_ref):
    group = lax.axis_index("tm") // 2
    last = group == lax.axis_size("tm") // 2 - 1
    for pair in range(2):
        for r in range(4):
            for plane in range(FIELDS + 1):
                rows_ref[pair, plane, pl.ds(8 * r, 8), :] = in_ref[4 * pair + r, plane]

    def strided(pair, plane):
        return [rows_ref[pair, plane, pl.ds(k, 8, 4), :] for k in range(4)]

    bed, wet = strided(0, FIELDS), strided(1, FIELDS)
    slope_e = [0.5 * (east(a) - west(a)) for a in bed]
    slope_n = [0.5 * (a - b) for a, b in zip(north(bed), south(bed))]
    slopes = (slope_e, slope_n, wet)
    for index, tiles in enumerate(slopes):
        for k in range(4):
            slope_ref[index, k] = tiles[k]
    fine, coarse = scaled(slopes, FINE[0]), scaled(slopes, COARSE[0])
    first = [[strided(pair, field) for field in range(FIELDS)] for pair in range(2)]
    shape = jax.tree.structure(first)

    def propagate(states):
        def body(_, leaves):
            pairs = jax.tree.unflatten(shape, leaves)
            return tuple(flat([advance(state, fine, *FINE) for state in pairs]))

        return jax.tree.unflatten(shape, lax.fori_loop(0, FINE_STEPS, body, tuple(flat(states))))

    before = propagate(first)
    before[0] = combine(lambda a, b: jnp.where(last, a, b), first[0], before[0])
    write_tiles(before_ref, before[0])
    reached = propagate(before)
    forcing = [
        combine(jnp.subtract, reached[pair], advance(before[pair], coarse, *COARSE))
        for pair in range(2)
    ]
    for pair in range(2):
        write_tiles(forcing_ref, forcing[pair], pair)
    write_tiles(chain_ref, combine(jnp.add, advance(reached[0], coarse, *COARSE), forcing[1]))


def two_steps(opening, forcing_ref, slope_ref):
    slopes = [[slope_ref[index, k] for k in range(4)] for index in range(3)]
    coarse = scaled(slopes, COARSE[0])
    values = []
    for pair in range(2):
        opening = combine(
            jnp.add, advance(opening, coarse, *COARSE), read_tiles(forcing_ref, pair)
        )
        values.append(opening)
    return values


def first_chain_kernel(in_ref, forcing_ref, slope_ref, out_ref):
    write_tiles(out_ref, two_steps(read_tiles(in_ref), forcing_ref, slope_ref)[1])


def second_chain_kernel(in_ref, before_ref, forcing_ref, slope_ref, out_ref):
    group = lax.axis_index("tm") // 2
    last = group == lax.axis_size("tm") // 2 - 1
    opening = combine(lambda a, b: jnp.where(last, a, b), read_tiles(before_ref), read_tiles(in_ref))
    for pair, value in enumerate(two_steps(opening, forcing_ref, slope_ref)):
        write_tiles(out_ref, value, pair)


def last_chain_kernel(in_ref, forcing_ref, slope_ref, out_ref, rows_ref):
    lanes = lane_index()
    states = [read_tiles(in_ref, 0), read_tiles(in_ref, 1)]
    states += two_steps(states[1], forcing_ref, slope_ref)
    for position in range(4):
        for field in range(FIELDS):
            shift = 96 if field % 2 == 0 else 32
            for k in range(4):
                rows_ref[position, field, pl.ds(k, 8, 4), :] = pltpu.roll(
                    states[position][field][k], shift, 1
                )
        for r in range(4):
            for half in range(2):
                low = rows_ref[position, 2 * half, pl.ds(8 * r, 8), :]
                high = rows_ref[position, 2 * half + 1, pl.ds(8 * r, 8), :]
                out_ref[4 * position + r, half] = jnp.where(lanes < 64, low, high)


def unpack_kernel(in_ref, out_ref):
    lanes = lane_index()
    for half in range(2):
        for c in range(4):
            left, right = in_ref[2 * c, half], in_ref[2 * c + 1, half]
            cut = pl.ds(128 * c, 128)
            out_ref[0, 2 * half, :, cut] = jnp.where(lanes < 64, left, pltpu.roll(right, 64, 1))
            out_ref[0, 2 * half + 1, :, cut] = jnp.where(lanes < 64, pltpu.roll(left, 64, 1), right)


def call(kernel, shapes, name, specs=None, scratch=()):
    outs = [jax.ShapeDtypeStruct(shape, jnp.float32) for shape in shapes]
    vmem = pl.BlockSpec(memory_space=pltpu.VMEM)
    single = len(outs) == 1

    def run(*args):
        return pl.pallas_call(
            kernel,
            out_shape=outs[0] if single else outs,
            in_specs=specs or [vmem] * len(args),
            out_specs=vmem if single else [vmem] * len(outs),
            scratch_shapes=scratch,
            name=name,
        )(*args)

    return run


def groups(count, row_devices, size):
    return [
        [(size * g + q) * row_devices + r for q in range(size) for r in range(row_devices)]
        for g in range(count // size)
    ]


def on_device(start_state, initial_guess, land_mask, bed_class, bed_table):
    count, row_devices = lax.axis_size("tm"), lax.axis_size("rows")
    vmem = pl.BlockSpec(memory_space=pltpu.VMEM)
    smem = pl.BlockSpec(memory_space=pltpu.SMEM)
    packed = call(
        pack_kernel, [(8, FIELDS + 1, *TILE)], "pack", [vmem] * 4 + [smem]
    )(start_state, initial_guess, land_mask, bed_class, bed_table)
    arrived = lax.all_to_all(packed, AXES, 0, 0, axis_index_groups=groups(count, row_devices, 2))
    state = (FIELDS, 4, *TILE)
    forcing, chain, before, slopes = call(
        forcing_kernel,
        [(2, *state), state, state, (3, 4, *TILE)],
        "forcing",
        scratch=[pltpu.VMEM((2, FIELDS + 1, 32, 128), jnp.float32)],
    )(arrived)
    to_even = [(i, (i + 2) % count) for i in range(count) if i % 4 >= 2]
    to_odd = [(i, i + 2) for i in range(count) if i % 4 < 2]
    chain = lax.ppermute(chain, "tm", to_even)
    chain = call(first_chain_kernel, [state], "chain1")(chain, forcing, slopes)
    chain = lax.ppermute(chain, "tm", to_odd)
    values = call(second_chain_kernel, [(2, *state)], "chain2")(chain, before, forcing, slopes)
    values = lax.ppermute(values, "tm", to_even)
    packed = call(
        last_chain_kernel,
        [(16, 2, *TILE)],
        "chain3",
        scratch=[pltpu.VMEM((4, FIELDS, 32, 128), jnp.float32)],
    )(values, forcing, slopes)
    arrived = lax.all_to_all(packed, AXES, 0, 0, axis_index_groups=groups(count, row_devices, 4))
    return call(unpack_kernel, [initial_guess.shape], "unpack")(arrived)


def solution(mesh):
    in_specs = (
        P(None, "rows", None),
        P("tm", None, "rows", None),
        P("rows", None),
        P("rows", None),
        P(),
    )
    out_specs = P("tm", None, "rows", None)
    return jax.shard_map(
        on_device, mesh=mesh, in_specs=in_specs, out_specs=out_specs, check_vma=False
    )
```

time: 319 us -> 74.3 us (0.23)
  the two profiles are of different devices: /device:TPU:6 before, /device:TPU:1 now
where the time goes in v1:
time: 74.3 us; the launch traced here: 73.9 us
  blocking collectives  34.2 us (46%)
  waiting for transfers between devices  21 us (28%)
  Pallas kernels  12.9 us (17%)
  starting transfers between devices  3.84 us (5%)
  local copies, waits for them, and re-layouts  1.9 us (3%)
    all_to_all x2, blocking collectives, on_device(): lax.all_to_all(packed, AXES, 0, 0, axis_index_groups=groups(count, row_de...  34.2 us
    pallas_call x6, Pallas kernels, run(): pl.pallas_call(kernel, out_shape=outs[0] if single else outs, in_specs=sp...  12.9 us
    ppermute x1, waiting for transfers between devices, on_device(): values = lax.ppermute(values, 'tm', to_even)  9.74 us
    ppermute x1, waiting for transfers between devices, on_device(): chain = lax.ppermute(chain, 'tm', to_even)  9.63 us
    unnamed x6, local copies, waits for them, and re-layouts  1.9 us
    ppermute x1, waiting for transfers between devices, on_device(): chain = lax.ppermute(chain, 'tm', to_odd)  1.63 us
  transfers between devices with their start and end apart: 3, of which 3 were waited for; matrix products, arithmetic and copies ran while one was open for 0% of the time, Pallas kernels for 0%

profile of v1, /device:TPU:1, one launch (start us, length us, event | category | flops | bytes accessed | tf_op | source)
XLA Modules:
  0.0 73.9 jit_solution(11553842240867854052)
XLA Ops:
  0.0 1.7 %pack.1 = f32[8,5,8,128]{3,2,1,0:T(8,128)} custom-call(f32[4,8,512]{2,1,0:T(8,128)} %start_ref.1, f32[1,4,8,512]{3,2,1,0:T(8,128)} %guess_ref.1, s32[8,512]{1,0:T(8,128)} %mask_ref.1, s32[8,512]{1,0:T(8,128)} %class_ref.1, f32[16]{0:T(128)} %table_ref.1), custom_call_target="tpu_custom_call" | custom-call | tf_op jit(solution)/shard_map/pack/pallas_call | solution.py:234
  1.7 16.8 %all_to_all.10.in_ref = f32[8,5,8,128]{3,2,1,0:T(8,128)} all-to-all(f32[8,5,8,128]{3,2,1,0:T(8,128)} %pack.1), channel_id=1, replica_groups={{0,1,2,3,4,5,6,7},{8,9,10,11,12,13,14,15},{16,17,18,19,20,21,22,23},{24..., dimensions={0} | all-to-all | bytes 327680 | tf_op jit(solution)/shard_map/all_to_all | solution.py:260
  18.5 4.1 %forcing.1 = (f32[2,4,4,8,128]{4,3,2,1,0:T(8,128)}, f32[4,4,8,128]{3,2,1,0:T(8,128)}, f32[4,4,8,128]{3,2,1,0:T(8,128)}, f32[3,4,8,128]{3,2,1,0:T(8,128)}) custom-call(f32[8,5,8,128]{3,2,1,0:T(8,128)} %all_to_all.10.in_ref), custom_call_target="tpu_custom_call" | custom-call | tf_op jit(solution)/shard_map/forcing/pallas_call | solution.py:234
  22.6 1.3 %collective-permute-start = (f32[4,4,8,128]{3,2,1,0:T(8,128)}, f32[4,4,8,128]{3,2,1,0:T(8,128)S(1)}, u32[]{:S(2)}, u32[]{:S(2)}) collective-permute-start(f32[4,4,8,128]{3,2,1,0:T(8,128)} %get-tuple-element.9), channel_id=1, source_target_pairs={{8,16},{12,20},{24,32},{28,36},{40,48},{44,52},{56,64},{60,68},{72... | collective-permute-start | bytes 196616 | tf_op jit(solution)/shard_map/ppermute | solution.py:270
  23.9 9.6 %collective-permute-done.in_ref = f32[4,4,8,128]{3,2,1,0:T(8,128)S(1)} collective-permute-done((f32[4,4,8,128]{3,2,1,0:T(8,128)}, f32[4,4,8,128]{3,2,1,0:T(8,128)S(1)}, u32[]{:S(2)}, u32[]{:S(2)}) %collective-permute-start) | collective-permute-done | bytes 65568 | tf_op jit(solution)/shard_map/ppermute | solution.py:270
  33.5 0.0 copy-start.2
  33.5 0.6 copy-done.2
  34.1 1.7 %chain1.1 = f32[4,4,8,128]{3,2,1,0:T(8,128)} custom-call(f32[4,4,8,128]{3,2,1,0:T(8,128)} %copy-done.2, f32[2,4,4,8,128]{4,3,2,1,0:T(8,128)} %get-tuple-element.10.forcing_ref, f32[3,4,8,128]{3,2,1,0:T(8,128)} %get-tuple-element.11.slope_ref), custom_call_target="tpu_custom_call" | custom-call | tf_op jit(solution)/shard_map/chain1/pallas_call | solution.py:234
  35.9 1.3 %collective-permute-start.1 = (f32[4,4,8,128]{3,2,1,0:T(8,128)}, f32[4,4,8,128]{3,2,1,0:T(8,128)S(1)}, u32[]{:S(2)}, u32[]{:S(2)}) collective-permute-start(f32[4,4,8,128]{3,2,1,0:T(8,128)} %chain1.1), channel_id=1, source_target_pairs={{0,8},{4,12},{16,24},{20,28},{32,40},{36,44},{48,56},{52,60},{64,7... | collective-permute-start | bytes 196616 | tf_op jit(solution)/shard_map/ppermute | solution.py:272
  37.2 1.6 %collective-permute-done.1.in_ref = f32[4,4,8,128]{3,2,1,0:T(8,128)S(1)} collective-permute-done((f32[4,4,8,128]{3,2,1,0:T(8,128)}, f32[4,4,8,128]{3,2,1,0:T(8,128)S(1)}, u32[]{:S(2)}, u32[]{:S(2)}) %collective-permute-start.1) | collective-permute-done | bytes 65568 | tf_op jit(solution)/shard_map/ppermute | solution.py:272
  38.8 0.0 copy-start.1
  38.8 0.6 copy-done.1
  39.4 1.8 %chain2.1 = f32[2,4,4,8,128]{4,3,2,1,0:T(8,128)} custom-call(f32[4,4,8,128]{3,2,1,0:T(8,128)} %copy-done.1, f32[4,4,8,128]{3,2,1,0:T(8,128)} %get-tuple-element.12.before_ref, f32[2,4,4,8,128]{4,3,2,1,0:T(8,128)} %get-tuple-element.10.forcing_ref, f32[3,4,8,128]{3,2,1,0:T(8,128)} %get-tuple-element.11.slope_ref), custom_call_target="tpu_custom_call" | custom-call | tf_op jit(solution)/shard_map/chain2/pallas_call | solution.py:234
  41.3 1.3 %collective-permute-start.2 = (f32[2,4,4,8,128]{4,3,2,1,0:T(8,128)}, f32[2,4,4,8,128]{4,3,2,1,0:T(8,128)S(1)}, u32[]{:S(2)}, u32[]{:S(2)}) collective-permute-start(f32[2,4,4,8,128]{4,3,2,1,0:T(8,128)} %chain2.1), channel_id=1, source_target_pairs={{8,16},{12,20},{24,32},{28,36},{40,48},{44,52},{56,64},{60,68},{72... | collective-permute-start | bytes 393224 | tf_op jit(solution)/shard_map/ppermute | solution.py:274
  42.5 9.7 %collective-permute-done.2.in_ref = f32[2,4,4,8,128]{4,3,2,1,0:T(8,128)S(1)} collective-permute-done((f32[2,4,4,8,128]{4,3,2,1,0:T(8,128)}, f32[2,4,4,8,128]{4,3,2,1,0:T(8,128)S(1)}, u32[]{:S(2)}, u32[]{:S(2)}) %collective-permute-start.2) | collective-permute-done | bytes 131104 | tf_op jit(solution)/shard_map/ppermute | solution.py:274
  52.3 0.0 copy-start
  52.3 0.6 copy-done
  52.9 1.9 %chain3.1 = f32[16,2,8,128]{3,2,1,0:T(8,128)} custom-call(f32[2,4,4,8,128]{4,3,2,1,0:T(8,128)} %copy-done, f32[2,4,4,8,128]{4,3,2,1,0:T(8,128)} %get-tuple-element.10.forcing_ref, f32[3,4,8,128]{3,2,1,0:T(8,128)} %get-tuple-element.11.slope_ref), custom_call_target="tpu_custom_call" | custom-call | tf_op jit(solution)/shard_map/chain3/pallas_call | solution.py:234
  54.8 17.4 %all_to_all.11.in_ref = f32[16,2,8,128]{3,2,1,0:T(8,128)} all-to-all(f32[16,2,8,128]{3,2,1,0:T(8,128)} %chain3.1), channel_id=1, replica_groups={{0,1,2,3,4,5,6,7,8,9,10,11,12,13,14,15},{16,17,18,19,20,21,22,23,24,25,..., dimensions={0} | all-to-all | bytes 262144 | tf_op jit(solution)/shard_map/all_to_all | solution.py:281
  72.2 1.6 %unpack.1 = f32[1,4,8,512]{3,2,1,0:T(8,128)} custom-call(f32[16,2,8,128]{3,2,1,0:T(8,128)} %all_to_all.11.in_ref), custom_call_target="tpu_custom_call" | custom-call | tf_op jit(solution)/shard_map/unpack/pallas_call | solution.py:234
Async XLA Ops:
  22.6 10.9 %collective-permute-start = (f32[4,4,8,128]{3,2,1,0:T(8,128)}, f32[4,4,8,128]{3,2,1,0:T(8,128)S(1)}, u32[]{:S(2)}, u32[]{:S(2)}) collective-permute-start(f32[4,4,8,128]{3,2,1,0:T(8,128)} %get-tuple-element.9), channel_id=1, source_target_pairs={{8,16},{12,20},{24,32},{28,36},{40,48},{44,52},{56,64},{60,68},{72... | collective-permute-start | bytes 196616 | tf_op jit(solution)/shard_map/ppermute | solution.py:270
  33.5 0.6 copy-start.2
  35.9 2.9 %collective-permute-start.1 = (f32[4,4,8,128]{3,2,1,0:T(8,128)}, f32[4,4,8,128]{3,2,1,0:T(8,128)S(1)}, u32[]{:S(2)}, u32[]{:S(2)}) collective-permute-start(f32[4,4,8,128]{3,2,1,0:T(8,128)} %chain1.1), channel_id=1, source_target_pairs={{0,8},{4,12},{16,24},{20,28},{32,40},{36,44},{48,56},{52,60},{64,7... | collective-permute-start | bytes 196616 | tf_op jit(solution)/shard_map/ppermute | solution.py:272
  38.8 0.6 copy-start.1
  41.3 11.0 %collective-permute-start.2 = (f32[2,4,4,8,128]{4,3,2,1,0:T(8,128)}, f32[2,4,4,8,128]{4,3,2,1,0:T(8,128)S(1)}, u32[]{:S(2)}, u32[]{:S(2)}) collective-permute-start(f32[2,4,4,8,128]{4,3,2,1,0:T(8,128)} %chain2.1), channel_id=1, source_target_pairs={{8,16},{12,20},{24,32},{28,36},{40,48},{44,52},{56,64},{60,68},{72... | collective-permute-start | bytes 393224 | tf_op jit(solution)/shard_map/ppermute | solution.py:274
  52.3 0.6 copy-start

commit v2 on v1

--- a/solution.py
+++ b/solution.py
@@ -225,12 +225,15 @@
             out_ref[0, 2 * half + 1, :, cut] = jnp.where(lanes < 64, pltpu.roll(left, 64, 1), right)
 
 
-def call(kernel, shapes, name, specs=None, scratch=()):
-    outs = [jax.ShapeDtypeStruct(shape, jnp.float32) for shape in shapes]
+def call(kernel, shapes, name, specs=None, scratch=(), in_vmem=True, out_vmem=True):
+    kind = pltpu.VMEM if out_vmem else jax.ShapeDtypeStruct
+    outs = [kind(shape, jnp.float32) for shape in shapes]
     vmem = pl.BlockSpec(memory_space=pltpu.VMEM)
     single = len(outs) == 1
 
     def run(*args):
+        if in_vmem:
+            args = [pltpu.with_memory_space_constraint(a, pltpu.VMEM) for a in args]
         return pl.pallas_call(
             kernel,
             out_shape=outs[0] if single else outs,
@@ -255,7 +258,7 @@
     vmem = pl.BlockSpec(memory_space=pltpu.VMEM)
     smem = pl.BlockSpec(memory_space=pltpu.SMEM)
     packed = call(
-        pack_kernel, [(8, FIELDS + 1, *TILE)], "pack", [vmem] * 4 + [smem]
+        pack_kernel, [(8, FIELDS + 1, *TILE)], "pack", [vmem] * 4 + [smem], in_vmem=False
     )(start_state, initial_guess, land_mask, bed_class, bed_table)
     arrived = lax.all_to_all(packed, AXES, 0, 0, axis_index_groups=groups(count, row_devices, 2))
     state = (FIELDS, 4, *TILE)
@@ -279,7 +282,7 @@
         scratch=[pltpu.VMEM((4, FIELDS, 32, 128), jnp.float32)],
     )(values, forcing, slopes)
     arrived = lax.all_to_all(packed, AXES, 0, 0, axis_index_groups=groups(count, row_devices, 4))
-    return call(unpack_kernel, [initial_guess.shape], "unpack")(arrived)
+    return call(unpack_kernel, [initial_guess.shape], "unpack", out_vmem=False)(arrived)
 
 
 def solution(mesh):

time: 74.3 us -> 62.9 us (0.85)
  Pallas kernels: 12.9 us -> 4.93 us
  blocking collectives: 34.2 us -> 32.3 us
  local copies, waits for them, and re-layouts: 1.9 us -> 0 us
    pallas_call x6, Pallas kernels: 12.9 us -> 4.93 us  [run(): pl.pallas_call(kernel, out_shape=outs[0] if single else outs, in_specs=sp...]
    all_to_all x2, blocking collectives: 34.2 us -> 32.3 us  [on_device(): lax.all_to_all(packed, AXES, 0, 0, axis_index_groups=groups(count, row_de...]
    unnamed x6 -> x0, local copies, waits for them, and re-layouts: 1.9 us -> none
    ppermute x1, waiting for transfers between devices: 9.63 us -> 10.7 us  [on_device(): chain = lax.ppermute(chain, 'tm', to_even)]
where the time goes in v2:
time: 62.9 us; the launch traced here: 62.7 us
  blocking collectives  32.3 us (51%)
  waiting for transfers between devices  21.5 us (34%)
  Pallas kernels  4.93 us (8%)
  starting transfers between devices  3.88 us (6%)
    all_to_all x2, blocking collectives, on_device(): lax.all_to_all(packed, AXES, 0, 0, axis_index_groups=groups(count, row_de...  32.3 us
    ppermute x1, waiting for transfers between devices, on_device(): chain = lax.ppermute(chain, 'tm', to_even)  10.7 us
    ppermute x1, waiting for transfers between devices, on_device(): values = lax.ppermute(values, 'tm', to_even)  9.53 us
    pallas_call x6, Pallas kernels, run(): pl.pallas_call(kernel, out_shape=outs[0] if single else outs, in_specs=sp...  4.93 us
    ppermute x1, waiting for transfers between devices, on_device(): chain = lax.ppermute(chain, 'tm', to_odd)  1.31 us
    ppermute x1, starting transfers between devices, on_device(): chain = lax.ppermute(chain, 'tm', to_odd)  1.29 us
    ppermute x1, starting transfers between devices, on_device(): values = lax.ppermute(values, 'tm', to_even)  1.29 us
    ppermute x1, starting transfers between devices, on_device(): chain = lax.ppermute(chain, 'tm', to_even)  1.29 us
  transfers between devices with their start and end apart: 3, of which 3 were waited for; matrix products, arithmetic and copies ran while one was open for 0% of the time, Pallas kernels for 0%

profile of v2, /device:TPU:1, one launch (start us, length us, event | category | flops | bytes accessed | tf_op | source)
XLA Modules:
  0.0 62.7 jit_solution(2977455543106044552)
XLA Ops:
  0.0 1.0 %pack.1 = f32[8,5,8,128]{3,2,1,0:T(8,128)S(1)} custom-call(f32[4,8,512]{2,1,0:T(8,128)} %start_ref.1, f32[1,4,8,512]{3,2,1,0:T(8,128)} %guess_ref.1, s32[8,512]{1,0:T(8,128)} %mask_ref.1, s32[8,512]{1,0:T(8,128)} %class_ref.1, f32[16]{0:T(128)} %table_ref.1), custom_call_target="tpu_custom_call" | custom-call | tf_op jit(solution)/shard_map/pack/pallas_call | solution.py:237
  1.0 15.2 %all_to_all.10.in_ref = f32[8,5,8,128]{3,2,1,0:T(8,128)S(1)} all-to-all(f32[8,5,8,128]{3,2,1,0:T(8,128)S(1)} %pack.1), channel_id=1, replica_groups={{0,1,2,3,4,5,6,7},{8,9,10,11,12,13,14,15},{16,17,18,19,20,21,22,23},{24..., dimensions={0} | all-to-all | bytes 327680 | tf_op jit(solution)/shard_map/all_to_all | solution.py:263
  16.2 2.5 %forcing.1 = (f32[2,4,4,8,128]{4,3,2,1,0:T(8,128)S(1)}, f32[4,4,8,128]{3,2,1,0:T(8,128)S(1)}, f32[4,4,8,128]{3,2,1,0:T(8,128)S(1)}, f32[3,4,8,128]{3,2,1,0:T(8,128)S(1)}) custom-call(f32[8,5,8,128]{3,2,1,0:T(8,128)S(1)} %all_to_all.10.in_ref), custom_call_target="tpu_custom_call" | custom-call | tf_op jit(solution)/shard_map/forcing/pallas_call | solution.py:237
  18.7 1.3 %collective-permute-start = (f32[4,4,8,128]{3,2,1,0:T(8,128)S(1)}, f32[4,4,8,128]{3,2,1,0:T(8,128)S(1)}, u32[]{:S(2)}, u32[]{:S(2)}) collective-permute-start(f32[4,4,8,128]{3,2,1,0:T(8,128)S(1)} %get-tuple-element.9), channel_id=1, source_target_pairs={{8,16},{12,20},{24,32},{28,36},{40,48},{44,52},{56,64},{60,68},{72... | collective-permute-start | bytes 196616 | tf_op jit(solution)/shard_map/ppermute | solution.py:273
  20.0 10.7 %collective-permute-done.in_ref = f32[4,4,8,128]{3,2,1,0:T(8,128)S(1)} collective-permute-done((f32[4,4,8,128]{3,2,1,0:T(8,128)S(1)}, f32[4,4,8,128]{3,2,1,0:T(8,128)S(1)}, u32[]{:S(2)}, u32[]{:S(2)}) %collective-permute-start) | collective-permute-done | bytes 65568 | tf_op jit(solution)/shard_map/ppermute | solution.py:273
  30.7 0.2 chain1.1
  30.9 1.3 %collective-permute-start.1 = (f32[4,4,8,128]{3,2,1,0:T(8,128)S(1)}, f32[4,4,8,128]{3,2,1,0:T(8,128)S(1)}, u32[]{:S(2)}, u32[]{:S(2)}) collective-permute-start(f32[4,4,8,128]{3,2,1,0:T(8,128)S(1)} %chain1.1), channel_id=1, source_target_pairs={{0,8},{4,12},{16,24},{20,28},{32,40},{36,44},{48,56},{52,60},{64,7... | collective-permute-start | bytes 196616 | tf_op jit(solution)/shard_map/ppermute | solution.py:275
  32.2 1.3 %collective-permute-done.1.in_ref = f32[4,4,8,128]{3,2,1,0:T(8,128)S(1)} collective-permute-done((f32[4,4,8,128]{3,2,1,0:T(8,128)S(1)}, f32[4,4,8,128]{3,2,1,0:T(8,128)S(1)}, u32[]{:S(2)}, u32[]{:S(2)}) %collective-permute-start.1) | collective-permute-done | bytes 65568 | tf_op jit(solution)/shard_map/ppermute | solution.py:275
  33.5 0.2 chain2.1
  33.7 1.3 %collective-permute-start.2 = (f32[2,4,4,8,128]{4,3,2,1,0:T(8,128)S(1)}, f32[2,4,4,8,128]{4,3,2,1,0:T(8,128)S(1)}, u32[]{:S(2)}, u32[]{:S(2)}) collective-permute-start(f32[2,4,4,8,128]{4,3,2,1,0:T(8,128)S(1)} %chain2.1), channel_id=1, source_target_pairs={{8,16},{12,20},{24,32},{28,36},{40,48},{44,52},{56,64},{60,68},{72... | collective-permute-start | bytes 393224 | tf_op jit(solution)/shard_map/ppermute | solution.py:277
  35.0 9.5 %collective-permute-done.2.in_ref = f32[2,4,4,8,128]{4,3,2,1,0:T(8,128)S(1)} collective-permute-done((f32[2,4,4,8,128]{4,3,2,1,0:T(8,128)S(1)}, f32[2,4,4,8,128]{4,3,2,1,0:T(8,128)S(1)}, u32[]{:S(2)}, u32[]{:S(2)}) %collective-permute-start.2) | collective-permute-done | bytes 131104 | tf_op jit(solution)/shard_map/ppermute | solution.py:277
  44.6 0.3 chain3.1
  44.8 17.1 %all_to_all.11.in_ref = f32[16,2,8,128]{3,2,1,0:T(8,128)S(1)} all-to-all(f32[16,2,8,128]{3,2,1,0:T(8,128)S(1)} %chain3.1), channel_id=1, replica_groups={{0,1,2,3,4,5,6,7,8,9,10,11,12,13,14,15},{16,17,18,19,20,21,22,23,24,25,..., dimensions={0} | all-to-all | bytes 262144 | tf_op jit(solution)/shard_map/all_to_all | solution.py:284
  61.9 0.7 %unpack.1 = f32[1,4,8,512]{3,2,1,0:T(8,128)} custom-call(f32[16,2,8,128]{3,2,1,0:T(8,128)S(1)} %all_to_all.11.in_ref), custom_call_target="tpu_custom_call" | custom-call | tf_op jit(solution)/shard_map/unpack/pallas_call | solution.py:237
Async XLA Ops:
  18.7 12.0 %collective-permute-start = (f32[4,4,8,128]{3,2,1,0:T(8,128)S(1)}, f32[4,4,8,128]{3,2,1,0:T(8,128)S(1)}, u32[]{:S(2)}, u32[]{:S(2)}) collective-permute-start(f32[4,4,8,128]{3,2,1,0:T(8,128)S(1)} %get-tuple-element.9), channel_id=1, source_target_pairs={{8,16},{12,20},{24,32},{28,36},{40,48},{44,52},{56,64},{60,68},{72... | collective-permute-start | bytes 196616 | tf_op jit(solution)/shard_map/ppermute | solution.py:273
  30.9 2.6 %collective-permute-start.1 = (f32[4,4,8,128]{3,2,1,0:T(8,128)S(1)}, f32[4,4,8,128]{3,2,1,0:T(8,128)S(1)}, u32[]{:S(2)}, u32[]{:S(2)}) collective-permute-start(f32[4,4,8,128]{3,2,1,0:T(8,128)S(1)} %chain1.1), channel_id=1, source_target_pairs={{0,8},{4,12},{16,24},{20,28},{32,40},{36,44},{48,56},{52,60},{64,7... | collective-permute-start | bytes 196616 | tf_op jit(solution)/shard_map/ppermute | solution.py:275
  33.7 10.8 %collective-permute-start.2 = (f32[2,4,4,8,128]{4,3,2,1,0:T(8,128)S(1)}, f32[2,4,4,8,128]{4,3,2,1,0:T(8,128)S(1)}, u32[]{:S(2)}, u32[]{:S(2)}) collective-permute-start(f32[2,4,4,8,128]{4,3,2,1,0:T(8,128)S(1)} %chain2.1), channel_id=1, source_target_pairs={{8,16},{12,20},{24,32},{28,36},{40,48},{44,52},{56,64},{60,68},{72... | collective-permute-start | bytes 393224 | tf_op jit(solution)/shard_map/ppermute | solution.py:277

commit v3 on v2

--- a/solution.py
+++ b/solution.py
@@ -131,7 +131,40 @@
     windows(FIELDS, static)
 
 
-def forcing_kernel(in_ref, forcing_ref, chain_ref, before_ref, slope_ref, rows_ref):
+def fold(ref, state, *lead):
+    lanes = lane_index()
+    for half in range(2):
+        for k in range(4):
+            low = pltpu.roll(state[2 * half][k], 96, 1)
+            high = pltpu.roll(state[2 * half + 1][k], 32, 1)
+            ref[(*lead, 4 * half + k)] = jnp.where(lanes < 64, low, high)
+        edge = None
+        for slot in range(8):
+            tile = state[2 * half + slot // 4][slot % 4]
+            left = pltpu.roll(tile, (16 * slot - 24) % 128, 1)
+            right = pltpu.roll(tile, (16 * slot + 8 - 96) % 128, 1)
+            both = jnp.where(lanes < 16 * slot + 8, left, right)
+            edge = both if edge is None else jnp.where(lanes < 16 * slot, edge, both)
+        ref[(*lead, 8 + half)] = edge
+
+
+def unfold(ref, *lead):
+    lanes = lane_index()
+    state = [[None] * 4 for _ in range(FIELDS)]
+    for half in range(2):
+        edge = ref[(*lead, 8 + half)]
+        for slot in range(8):
+            k = slot % 4
+            own = pltpu.roll(ref[(*lead, 4 * half + k)], 32 if slot < 4 else 96, 1)
+            left = pltpu.roll(edge, (24 - 16 * slot) % 128, 1)
+            right = pltpu.roll(edge, (96 - 16 * slot - 8) % 128, 1)
+            state[2 * half + slot // 4][k] = jnp.where(
+                lanes < 32, left, jnp.where(lanes < 96, own, right)
+            )
+    return state
+
+
+def forcing_kernel(in_ref, forcing_ref, chain_ref, pass_ref, slope_ref, rows_ref):
     group = lax.axis_index("tm") // 2
     last = group == lax.axis_size("tm") // 2 - 1
     for pair in range(2):
@@ -160,54 +193,57 @@
 
         return jax.tree.unflatten(shape, lax.fori_loop(0, FINE_STEPS, body, tuple(flat(states))))
 
+    def choose(a, b):
+        return combine(lambda x, y: jnp.where(last, x, y), a, b)
+
     before = propagate(first)
-    before[0] = combine(lambda a, b: jnp.where(last, a, b), first[0], before[0])
-    write_tiles(before_ref, before[0])
+    before[0] = choose(first[0], before[0])
     reached = propagate(before)
     forcing = [
         combine(jnp.subtract, reached[pair], advance(before[pair], coarse, *COARSE))
         for pair in range(2)
     ]
+    second = combine(jnp.add, advance(reached[0], coarse, *COARSE), forcing[1])
+    fold(chain_ref, second)
+    fold(pass_ref, choose(reached[0], forcing[0]), 0)
+    fold(pass_ref, choose(second, forcing[1]), 1)
     for pair in range(2):
         write_tiles(forcing_ref, forcing[pair], pair)
-    write_tiles(chain_ref, combine(jnp.add, advance(reached[0], coarse, *COARSE), forcing[1]))
-
-
-def two_steps(opening, forcing_ref, slope_ref):
-    slopes = [[slope_ref[index, k] for k in range(4)] for index in range(3)]
-    coarse = scaled(slopes, COARSE[0])
-    values = []
+
+
+def coarse_of(slope_ref):
+    return scaled([[slope_ref[index, k] for k in range(4)] for index in range(3)], COARSE[0])
+
+
+def relax(opening, forcing, coarse):
+    return combine(jnp.add, advance(opening, coarse, *COARSE), forcing)
+
+
+def chain_kernel(in_ref, forcing_ref, slope_ref, out_ref):
+    coarse = coarse_of(slope_ref)
+    value = unfold(in_ref)
     for pair in range(2):
-        opening = combine(
-            jnp.add, advance(opening, coarse, *COARSE), read_tiles(forcing_ref, pair)
-        )
-        values.append(opening)
-    return values
-
-
-def first_chain_kernel(in_ref, forcing_ref, slope_ref, out_ref):
-    write_tiles(out_ref, two_steps(read_tiles(in_ref), forcing_ref, slope_ref)[1])
-
-
-def second_chain_kernel(in_ref, before_ref, forcing_ref, slope_ref, out_ref):
-    group = lax.axis_index("tm") // 2
-    last = group == lax.axis_size("tm") // 2 - 1
-    opening = combine(lambda a, b: jnp.where(last, a, b), read_tiles(before_ref), read_tiles(in_ref))
-    for pair, value in enumerate(two_steps(opening, forcing_ref, slope_ref)):
-        write_tiles(out_ref, value, pair)
-
-
-def last_chain_kernel(in_ref, forcing_ref, slope_ref, out_ref, rows_ref):
-    lanes = lane_index()
-    states = [read_tiles(in_ref, 0), read_tiles(in_ref, 1)]
-    states += two_steps(states[1], forcing_ref, slope_ref)
+        value = relax(value, read_tiles(forcing_ref, pair), coarse)
+    fold(out_ref, value)
+
+
+def last_kernel(in_ref, pass_ref, forcing_ref, slope_ref, out_ref, rows_ref):
+    lanes = lane_index()
+    opens = lax.axis_index("tm") < 2
+    coarse = coarse_of(slope_ref)
+    value = unfold(in_ref)
     for position in range(4):
+        if position < 2:
+            given = unfold(pass_ref, position)
+            value = combine(
+                lambda a, b: jnp.where(opens, a, b), given, relax(value, given, coarse)
+            )
+        else:
+            value = relax(value, read_tiles(forcing_ref, position - 2), coarse)
         for field in range(FIELDS):
             shift = 96 if field % 2 == 0 else 32
             for k in range(4):
-                rows_ref[position, field, pl.ds(k, 8, 4), :] = pltpu.roll(
-                    states[position][field][k], shift, 1
-                )
+                rows_ref[position, field, pl.ds(k, 8, 4), :] = pltpu.roll(value[field][k], shift, 1)
         for r in range(4):
             for half in range(2):
                 low = rows_ref[position, 2 * half, pl.ds(8 * r, 8), :]
@@ -262,25 +298,24 @@
     )(start_state, initial_guess, land_mask, bed_class, bed_table)
     arrived = lax.all_to_all(packed, AXES, 0, 0, axis_index_groups=groups(count, row_devices, 2))
     state = (FIELDS, 4, *TILE)
-    forcing, chain, before, slopes = call(
+    forcing, chain, passed, slopes = call(
         forcing_kernel,
-        [(2, *state), state, state, (3, 4, *TILE)],
+        [(2, *state), (10, *TILE), (2, 10, *TILE), (3, 4, *TILE)],
         "forcing",
         scratch=[pltpu.VMEM((2, FIELDS + 1, 32, 128), jnp.float32)],
     )(arrived)
     to_even = [(i, (i + 2) % count) for i in range(count) if i % 4 >= 2]
-    to_odd = [(i, i + 2) for i in range(count) if i % 4 < 2]
+    to_next = [(i, i + 4) for i in range(count - 4) if i % 4 < 2]
     chain = lax.ppermute(chain, "tm", to_even)
-    chain = call(first_chain_kernel, [state], "chain1")(chain, forcing, slopes)
-    chain = lax.ppermute(chain, "tm", to_odd)
-    values = call(second_chain_kernel, [(2, *state)], "chain2")(chain, before, forcing, slopes)
-    values = lax.ppermute(values, "tm", to_even)
+    passed = lax.ppermute(passed, "tm", to_even)
+    chain = call(chain_kernel, [(10, *TILE)], "chain")(chain, forcing, slopes)
+    chain = lax.ppermute(chain, "tm", to_next)
     packed = call(
-        last_chain_kernel,
+        last_kernel,
         [(16, 2, *TILE)],
-        "chain3",
+        "last",
         scratch=[pltpu.VMEM((4, FIELDS, 32, 128), jnp.float32)],
-    )(values, forcing, slopes)
+    )(chain, passed, forcing, slopes)
     arrived = lax.all_to_all(packed, AXES, 0, 0, axis_index_groups=groups(count, row_devices, 4))
     return call(unpack_kernel, [initial_guess.shape], "unpack", out_vmem=False)(arrived)
 

time: 62.9 us -> 59.4 us (0.944)
  the two profiles are of different devices: /device:TPU:1 before, /device:TPU:2 now
where the time goes in v3:
time: 59.4 us; the launch traced here: 59.2 us
  blocking collectives  24.8 us (42%)
  waiting for transfers between devices  24.4 us (41%)
  Pallas kernels  5.43 us (9%)
  starting transfers between devices  4.5 us (8%)
    all_to_all x2, blocking collectives, on_device(): lax.all_to_all(packed, AXES, 0, 0, axis_index_groups=groups(count, row_de...  24.8 us
    ppermute x1, waiting for transfers between devices, on_device(): chain = lax.ppermute(chain, 'tm', to_even)  13.3 us
    ppermute x1, waiting for transfers between devices, on_device(): chain = lax.ppermute(chain, 'tm', to_next)  11.1 us
    pallas_call x5, Pallas kernels, run(): pl.pallas_call(kernel, out_shape=outs[0] if single else outs, in_specs=sp...  5.43 us
    ppermute x1, starting transfers between devices, on_device(): chain = lax.ppermute(chain, 'tm', to_next)  1.92 us
    ppermute x1, starting transfers between devices, on_device(): chain = lax.ppermute(chain, 'tm', to_even)  1.29 us
    ppermute x1, starting transfers between devices, on_device(): passed = lax.ppermute(passed, 'tm', to_even)  1.29 us
  transfers between devices with their start and end apart: 3, of which 2 were waited for; matrix products, arithmetic and copies ran while one was open for 0% of the time, Pallas kernels for 1%

profile of v3, /device:TPU:2, one launch (start us, length us, event | category | flops | bytes accessed | tf_op | source)
XLA Modules:
  0.0 59.2 jit_solution(7703875058987935450)
XLA Ops:
  0.0 1.0 %pack.1 = f32[8,5,8,128]{3,2,1,0:T(8,128)S(1)} custom-call(f32[4,8,512]{2,1,0:T(8,128)} %start_ref.1, f32[1,4,8,512]{3,2,1,0:T(8,128)} %guess_ref.1, s32[8,512]{1,0:T(8,128)} %mask_ref.1, s32[8,512]{1,0:T(8,128)} %class_ref.1, f32[16]{0:T(128)} %table_ref.1), custom_call_target="tpu_custom_call" | custom-call | tf_op jit(solution)/shard_map/pack/pallas_call | solution.py:273
  1.0 11.5 %all_to_all.10.in_ref = f32[8,5,8,128]{3,2,1,0:T(8,128)S(1)} all-to-all(f32[8,5,8,128]{3,2,1,0:T(8,128)S(1)} %pack.1), channel_id=1, replica_groups={{0,1,2,3,4,5,6,7},{8,9,10,11,12,13,14,15},{16,17,18,19,20,21,22,23},{24..., dimensions={0} | all-to-all | bytes 327680 | tf_op jit(solution)/shard_map/all_to_all | solution.py:299
  12.5 2.7 %forcing.1 = (f32[2,4,4,8,128]{4,3,2,1,0:T(8,128)S(1)}, f32[10,8,128]{2,1,0:T(8,128)S(1)}, f32[2,10,8,128]{3,2,1,0:T(8,128)S(1)}, f32[3,4,8,128]{3,2,1,0:T(8,128)S(1)}) custom-call(f32[8,5,8,128]{3,2,1,0:T(8,128)S(1)} %all_to_all.10.in_ref), custom_call_target="tpu_custom_call" | custom-call | tf_op jit(solution)/shard_map/forcing/pallas_call | solution.py:273
  15.2 1.3 %collective-permute-start = (f32[10,8,128]{2,1,0:T(8,128)S(1)}, f32[10,8,128]{2,1,0:T(8,128)S(1)}, u32[]{:S(2)}, u32[]{:S(2)}) collective-permute-start(f32[10,8,128]{2,1,0:T(8,128)S(1)} %get-tuple-element.9), channel_id=1, source_target_pairs={{8,16},{12,20},{24,32},{28,36},{40,48},{44,52},{56,64},{60,68},{72... | collective-permute-start | bytes 122888 | tf_op jit(solution)/shard_map/ppermute | solution.py:309
  16.5 1.3 %collective-permute-start.2 = (f32[2,10,8,128]{3,2,1,0:T(8,128)S(1)}, f32[2,10,8,128]{3,2,1,0:T(8,128)S(1)}, u32[]{:S(2)}, u32[]{:S(2)}) collective-permute-start(f32[2,10,8,128]{3,2,1,0:T(8,128)S(1)} %get-tuple-element.12), channel_id=1, source_target_pairs={{8,16},{12,20},{24,32},{28,36},{40,48},{44,52},{56,64},{60,68},{72... | collective-permute-start | bytes 245768 | tf_op jit(solution)/shard_map/ppermute | solution.py:310
  17.8 13.3 %collective-permute-done.in_ref = f32[10,8,128]{2,1,0:T(8,128)S(1)} collective-permute-done((f32[10,8,128]{2,1,0:T(8,128)S(1)}, f32[10,8,128]{2,1,0:T(8,128)S(1)}, u32[]{:S(2)}, u32[]{:S(2)}) %collective-permute-start) | collective-permute-done | bytes 40992 | tf_op jit(solution)/shard_map/ppermute | solution.py:309
  31.1 0.4 chain.1
  31.5 1.9 %collective-permute-start.1 = (f32[10,8,128]{2,1,0:T(8,128)S(1)}, f32[10,8,128]{2,1,0:T(8,128)S(1)}, u32[]{:S(2)}, u32[]{:S(2)}) collective-permute-start(f32[10,8,128]{2,1,0:T(8,128)S(1)} %chain.1), channel_id=1, source_target_pairs={{0,16},{4,20},{16,32},{20,36},{32,48},{36,52},{48,64},{52,68},{64,... | collective-permute-start | bytes 122888 | tf_op jit(solution)/shard_map/ppermute | solution.py:312
  33.4 0.0 collective-permute-done.2.pass_ref
  33.4 11.1 %collective-permute-done.1.in_ref = f32[10,8,128]{2,1,0:T(8,128)S(1)} collective-permute-done((f32[10,8,128]{2,1,0:T(8,128)S(1)}, f32[10,8,128]{2,1,0:T(8,128)S(1)}, u32[]{:S(2)}, u32[]{:S(2)}) %collective-permute-start.1) | collective-permute-done | bytes 40992 | tf_op jit(solution)/shard_map/ppermute | solution.py:312
  44.5 0.6 %last.1 = f32[16,2,8,128]{3,2,1,0:T(8,128)S(1)} custom-call(f32[10,8,128]{2,1,0:T(8,128)S(1)} %collective-permute-done.1.in_ref, f32[2,10,8,128]{3,2,1,0:T(8,128)S(1)} %collective-permute-done.2.pass_ref, f32[2,4,4,8,128]{4,3,2,1,0:T(8,128)S(1)} %get-tuple-element.10.forcing_ref, f32[3,4,8,128]{3,2,1,0:T(8,128)S(1)} %get-tuple-element.11.slope_ref), custom_call_target="tpu_custom_call" | custom-call | tf_op jit(solution)/shard_map/last/pallas_call | solution.py:273
  45.1 13.3 %all_to_all.11.in_ref = f32[16,2,8,128]{3,2,1,0:T(8,128)S(1)} all-to-all(f32[16,2,8,128]{3,2,1,0:T(8,128)S(1)} %last.1), channel_id=1, replica_groups={{0,1,2,3,4,5,6,7,8,9,10,11,12,13,14,15},{16,17,18,19,20,21,22,23,24,25,..., dimensions={0} | all-to-all | bytes 262144 | tf_op jit(solution)/shard_map/all_to_all | solution.py:319
  58.4 0.7 %unpack.1 = f32[1,4,8,512]{3,2,1,0:T(8,128)} custom-call(f32[16,2,8,128]{3,2,1,0:T(8,128)S(1)} %all_to_all.11.in_ref), custom_call_target="tpu_custom_call" | custom-call | tf_op jit(solution)/shard_map/unpack/pallas_call | solution.py:273
Async XLA Ops:
  15.2 15.9 %collective-permute-start = (f32[10,8,128]{2,1,0:T(8,128)S(1)}, f32[10,8,128]{2,1,0:T(8,128)S(1)}, u32[]{:S(2)}, u32[]{:S(2)}) collective-permute-start(f32[10,8,128]{2,1,0:T(8,128)S(1)} %get-tuple-element.9), channel_id=1, source_target_pairs={{8,16},{12,20},{24,32},{28,36},{40,48},{44,52},{56,64},{60,68},{72... | collective-permute-start | bytes 122888 | tf_op jit(solution)/shard_map/ppermute | solution.py:309
  16.5 16.9 %collective-permute-start.2 = (f32[2,10,8,128]{3,2,1,0:T(8,128)S(1)}, f32[2,10,8,128]{3,2,1,0:T(8,128)S(1)}, u32[]{:S(2)}, u32[]{:S(2)}) collective-permute-start(f32[2,10,8,128]{3,2,1,0:T(8,128)S(1)} %get-tuple-element.12), channel_id=1, source_target_pairs={{8,16},{12,20},{24,32},{28,36},{40,48},{44,52},{56,64},{60,68},{72... | collective-permute-start | bytes 245768 | tf_op jit(solution)/shard_map/ppermute | solution.py:310
  31.5 13.0 %collective-permute-start.1 = (f32[10,8,128]{2,1,0:T(8,128)S(1)}, f32[10,8,128]{2,1,0:T(8,128)S(1)}, u32[]{:S(2)}, u32[]{:S(2)}) collective-permute-start(f32[10,8,128]{2,1,0:T(8,128)S(1)} %chain.1), channel_id=1, source_target_pairs={{0,16},{4,20},{16,32},{20,36},{32,48},{36,52},{48,64},{52,68},{64,... | collective-permute-start | bytes 122888 | tf_op jit(solution)/shard_map/ppermute | solution.py:312

commit v4 on v3

--- a/solution.py
+++ b/solution.py
@@ -5,12 +5,14 @@
 from jax.experimental.pallas import tpu as pltpu
 from jax.sharding import PartitionSpec as P
 
+
 FINE_STEPS = 8
 FINE = (0.0375, 0.025)
 COARSE = (0.3, 0.2)
 FIELDS = 4
 TILE = (8, 128)
 AXES = ("tm", "rows")
+RING = 16
 
 
 def east(x):
@@ -227,11 +229,22 @@
     fold(out_ref, value)
 
 
-def last_kernel(in_ref, pass_ref, forcing_ref, slope_ref, out_ref, rows_ref):
+def late_chain_kernel(in_ref, forcing_ref, slope_ref, order_ref, out_ref):
+    del order_ref
+    chain_kernel(in_ref, forcing_ref, slope_ref, out_ref)
+
+
+def last_kernel(
+    in_ref, late_ref, across_ref, pass_ref, forcing_ref, slope_ref, out_ref, join_ref, rows_ref
+):
     lanes = lane_index()
     opens = lax.axis_index("tm") < 2
     coarse = coarse_of(slope_ref)
-    value = unfold(in_ref)
+    place = lax.axis_index("tm") % RING // 2
+    for tile in range(10):
+        joined = jnp.where(place == 2, late_ref[tile], in_ref[tile])
+        join_ref[tile] = jnp.where(place == 0, across_ref[tile], joined)
+    value = unfold(join_ref)
     for position in range(4):
         if position < 2:
             given = unfold(pass_ref, position)
@@ -261,7 +274,7 @@
             out_ref[0, 2 * half + 1, :, cut] = jnp.where(lanes < 64, pltpu.roll(left, 64, 1), right)
 
 
-def call(kernel, shapes, name, specs=None, scratch=(), in_vmem=True, out_vmem=True):
+def call(kernel, shapes, specs=None, scratch=(), in_vmem=True, out_vmem=True):
     kind = pltpu.VMEM if out_vmem else jax.ShapeDtypeStruct
     outs = [kind(shape, jnp.float32) for shape in shapes]
     vmem = pl.BlockSpec(memory_space=pltpu.VMEM)
@@ -276,7 +289,6 @@
             in_specs=specs or [vmem] * len(args),
             out_specs=vmem if single else [vmem] * len(outs),
             scratch_shapes=scratch,
-            name=name,
         )(*args)
 
     return run
@@ -294,30 +306,37 @@
     vmem = pl.BlockSpec(memory_space=pltpu.VMEM)
     smem = pl.BlockSpec(memory_space=pltpu.SMEM)
     packed = call(
-        pack_kernel, [(8, FIELDS + 1, *TILE)], "pack", [vmem] * 4 + [smem], in_vmem=False
+        pack_kernel, [(8, FIELDS + 1, *TILE)], [vmem] * 4 + [smem], in_vmem=False
     )(start_state, initial_guess, land_mask, bed_class, bed_table)
     arrived = lax.all_to_all(packed, AXES, 0, 0, axis_index_groups=groups(count, row_devices, 2))
     state = (FIELDS, 4, *TILE)
     forcing, chain, passed, slopes = call(
         forcing_kernel,
         [(2, *state), (10, *TILE), (2, 10, *TILE), (3, 4, *TILE)],
-        "forcing",
         scratch=[pltpu.VMEM((2, FIELDS + 1, 32, 128), jnp.float32)],
     )(arrived)
     to_even = [(i, (i + 2) % count) for i in range(count) if i % 4 >= 2]
     to_next = [(i, i + 4) for i in range(count - 4) if i % 4 < 2]
-    chain = lax.ppermute(chain, "tm", to_even)
+    inside = [(i, j) for i, j in to_even if i % RING < RING - 2]
+    crossing = [(i, j) for i, j in to_even if i % RING >= RING - 2]
+    handed_across = [(i, j) for i, j in to_next if i % RING >= RING - 4]
+    handed_late = [(i, j) for i, j in to_next if i % RING < 2]
+    handed_inside = [(i, j) for i, j in to_next if 2 <= i % RING < RING - 4]
+    first = lax.ppermute(chain, "tm", inside)
+    second = lax.ppermute(chain, "tm", crossing)
     passed = lax.ppermute(passed, "tm", to_even)
-    chain = call(chain_kernel, [(10, *TILE)], "chain")(chain, forcing, slopes)
-    chain = lax.ppermute(chain, "tm", to_next)
+    first = call(chain_kernel, [(10, *TILE)])(first, forcing, slopes)
+    second = call(late_chain_kernel, [(10, *TILE)])(second, forcing, slopes, first)
+    across = lax.ppermute(first, "tm", handed_across)
+    second = lax.ppermute(second, "tm", handed_late)
+    first = lax.ppermute(first, "tm", handed_inside)
     packed = call(
         last_kernel,
         [(16, 2, *TILE)],
-        "last",
-        scratch=[pltpu.VMEM((4, FIELDS, 32, 128), jnp.float32)],
-    )(chain, passed, forcing, slopes)
+        scratch=[pltpu.VMEM((10, *TILE), jnp.float32), pltpu.VMEM((4, FIELDS, 32, 128), jnp.float32)],
+    )(first, second, across, passed, forcing, slopes)
     arrived = lax.all_to_all(packed, AXES, 0, 0, axis_index_groups=groups(count, row_devices, 4))
-    return call(unpack_kernel, [initial_guess.shape], "unpack", out_vmem=False)(arrived)
+    return call(unpack_kernel, [initial_guess.shape], out_vmem=False)(arrived)
 
 
 def solution(mesh):

time: 59.4 us -> 61.4 us (1.034)
  starting transfers between devices: 4.5 us -> 6.5 us
  waiting for transfers between devices: 24.4 us -> 23.7 us
    ppermute x2 -> x5, starting transfers between devices: 3.21 us -> 5.2 us  [the longest x1 1.29 us: on_device(): second = lax.ppermute(chain, 'tm', crossing)]
    ppermute x2 -> x5, waiting for transfers between devices: 24.4 us -> 23.7 us  [the longest x1 12.9 us: on_device(): second = lax.ppermute(chain, 'tm', crossing)]
    pallas_call x5 -> x6, Pallas kernels: 5.43 us -> 5.83 us  [run(): pl.pallas_call(kernel, out_shape=outs[0] if single else outs, in_specs=sp...]
  transfers between devices with their start and end apart: 3 -> 6, of which waited for: 2 -> 2; matrix products, arithmetic and copies ran while one was open for 0% -> 0% of each run, Pallas kernels for 1% -> 1%
where the time goes in v4:
time: 61.4 us; the launch traced here: 61.1 us
  blocking collectives  25 us (41%)
  waiting for transfers between devices  23.7 us (39%)
  starting transfers between devices  6.5 us (11%)
  Pallas kernels  5.83 us (9%)
    all_to_all x2, blocking collectives, on_device(): lax.all_to_all(packed, AXES, 0, 0, axis_index_groups=groups(count, row_de...  25 us
    ppermute x1, waiting for transfers between devices, on_device(): second = lax.ppermute(chain, 'tm', crossing)  12.9 us
    ppermute x1, waiting for transfers between devices, on_device(): across = lax.ppermute(first, 'tm', handed_across)  10.8 us
    pallas_call x6, Pallas kernels, run(): pl.pallas_call(kernel, out_shape=outs[0] if single else outs, in_specs=sp...  5.83 us
    ppermute x1, starting transfers between devices, on_device(): second = lax.ppermute(chain, 'tm', crossing)  1.29 us
    ppermute x1, starting transfers between devices, on_device(): passed = lax.ppermute(passed, 'tm', to_even)  1.29 us
    ppermute x1, starting transfers between devices, on_device(): second = lax.ppermute(second, 'tm', handed_late)  1.29 us
    ppermute x1, starting transfers between devices, on_device(): across = lax.ppermute(first, 'tm', handed_across)  1.29 us
  transfers between devices with their start and end apart: 6, of which 2 were waited for; matrix products, arithmetic and copies ran while one was open for 0% of the time, Pallas kernels for 1%

profile of v4, /device:TPU:2, one launch (start us, length us, event | category | flops | bytes accessed | tf_op | source)
XLA Modules:
  0.0 61.1 jit_solution(15853715891732432581)
XLA Ops:
  0.0 1.0 %shard_map.55 = f32[8,5,8,128]{3,2,1,0:T(8,128)S(1)} custom-call(f32[4,8,512]{2,1,0:T(8,128)} %start_ref.1, f32[1,4,8,512]{3,2,1,0:T(8,128)} %guess_ref.1, s32[8,512]{1,0:T(8,128)} %mask_ref.1, s32[8,512]{1,0:T(8,128)} %class_ref.1, f32[16]{0:T(128)} %table_ref.1), custom_call_target="tpu_custom_call" | custom-call | tf_op jit(solution)/shard_map/pallas_call | solution.py:286
  1.0 11.5 %all_to_all.10.in_ref = f32[8,5,8,128]{3,2,1,0:T(8,128)S(1)} all-to-all(f32[8,5,8,128]{3,2,1,0:T(8,128)S(1)} %shard_map.55), channel_id=1, replica_groups={{0,1,2,3,4,5,6,7},{8,9,10,11,12,13,14,15},{16,17,18,19,20,21,22,23},{24..., dimensions={0} | all-to-all | bytes 327680 | tf_op jit(solution)/shard_map/all_to_all | solution.py:311
  12.5 2.7 %shard_map.56 = (f32[2,4,4,8,128]{4,3,2,1,0:T(8,128)S(1)}, f32[10,8,128]{2,1,0:T(8,128)S(1)}, f32[2,10,8,128]{3,2,1,0:T(8,128)S(1)}, f32[3,4,8,128]{3,2,1,0:T(8,128)S(1)}) custom-call(f32[8,5,8,128]{3,2,1,0:T(8,128)S(1)} %all_to_all.10.in_ref), custom_call_target="tpu_custom_call" | custom-call | tf_op jit(solution)/shard_map/pallas_call | solution.py:286
  15.2 0.7 %collective-permute-start = (f32[10,8,128]{2,1,0:T(8,128)S(1)}, f32[10,8,128]{2,1,0:T(8,128)S(1)}, u32[]{:S(2)}, u32[]{:S(2)}) collective-permute-start(f32[10,8,128]{2,1,0:T(8,128)S(1)} %get-tuple-element.9), channel_id=1, source_target_pairs={{8,16},{12,20},{24,32},{28,36},{40,48},{44,52},{72,80},{76,84},{88... | collective-permute-start | bytes 122888 | tf_op jit(solution)/shard_map/ppermute | solution.py:325
  15.9 1.3 %collective-permute-start.2 = (f32[10,8,128]{2,1,0:T(8,128)S(1)}, f32[10,8,128]{2,1,0:T(8,128)S(1)}, u32[]{:S(2)}, u32[]{:S(2)}) collective-permute-start(f32[10,8,128]{2,1,0:T(8,128)S(1)} %get-tuple-element.9), channel_id=1, source_target_pairs={{56,64},{60,68},{120,128},{124,132},{184,192},{188,196},{248,256},... | collective-permute-start | bytes 122888 | tf_op jit(solution)/shard_map/ppermute | solution.py:326
  17.2 1.3 %collective-permute-start.5 = (f32[2,10,8,128]{3,2,1,0:T(8,128)S(1)}, f32[2,10,8,128]{3,2,1,0:T(8,128)S(1)}, u32[]{:S(2)}, u32[]{:S(2)}) collective-permute-start(f32[2,10,8,128]{3,2,1,0:T(8,128)S(1)} %get-tuple-element.12), channel_id=1, source_target_pairs={{8,16},{12,20},{24,32},{28,36},{40,48},{44,52},{56,64},{60,68},{72... | collective-permute-start | bytes 245768 | tf_op jit(solution)/shard_map/ppermute | solution.py:327
  18.5 0.0 collective-permute-done.in_ref
  18.5 0.4 shard_map.57.order_ref
  18.9 12.9 %collective-permute-done.2.in_ref = f32[10,8,128]{2,1,0:T(8,128)S(1)} collective-permute-done((f32[10,8,128]{2,1,0:T(8,128)S(1)}, f32[10,8,128]{2,1,0:T(8,128)S(1)}, u32[]{:S(2)}, u32[]{:S(2)}) %collective-permute-start.2) | collective-permute-done | bytes 40992 | tf_op jit(solution)/shard_map/ppermute | solution.py:326
  31.8 0.4 shard_map.58
  32.2 1.3 %collective-permute-start.3 = (f32[10,8,128]{2,1,0:T(8,128)S(1)}, f32[10,8,128]{2,1,0:T(8,128)S(1)}, u32[]{:S(2)}, u32[]{:S(2)}) collective-permute-start(f32[10,8,128]{2,1,0:T(8,128)S(1)} %shard_map.58), channel_id=1, source_target_pairs={{0,16},{4,20},{64,80},{68,84},{128,144},{132,148},{192,208},{196,2... | collective-permute-start | bytes 122888 | tf_op jit(solution)/shard_map/ppermute | solution.py:331
  33.5 1.3 %collective-permute-start.4 = (f32[10,8,128]{2,1,0:T(8,128)S(1)}, f32[10,8,128]{2,1,0:T(8,128)S(1)}, u32[]{:S(2)}, u32[]{:S(2)}) collective-permute-start(f32[10,8,128]{2,1,0:T(8,128)S(1)} %shard_map.57.order_ref), channel_id=1, source_target_pairs={{48,64},{52,68},{112,128},{116,132},{176,192},{180,196},{240,256},... | collective-permute-start | bytes 122888 | tf_op jit(solution)/shard_map/ppermute | solution.py:330
  34.8 0.7 %collective-permute-start.1 = (f32[10,8,128]{2,1,0:T(8,128)S(1)}, f32[10,8,128]{2,1,0:T(8,128)S(1)}, u32[]{:S(2)}, u32[]{:S(2)}) collective-permute-start(f32[10,8,128]{2,1,0:T(8,128)S(1)} %shard_map.57.order_ref), channel_id=1, source_target_pairs={{16,32},{20,36},{32,48},{36,52},{80,96},{84,100},{96,112},{100,116... | collective-permute-start | bytes 122888 | tf_op jit(solution)/shard_map/ppermute | solution.py:332
  35.4 0.0 collective-permute-done.5.pass_ref
  35.5 0.0 collective-permute-done.3.late_ref
  35.5 10.8 %collective-permute-done.4.across_ref = f32[10,8,128]{2,1,0:T(8,128)S(1)} collective-permute-done((f32[10,8,128]{2,1,0:T(8,128)S(1)}, f32[10,8,128]{2,1,0:T(8,128)S(1)}, u32[]{:S(2)}, u32[]{:S(2)}) %collective-permute-start.4) | collective-permute-done | bytes 40992 | tf_op jit(solution)/shard_map/ppermute | solution.py:330
  46.3 0.0 collective-permute-done.1.in_ref
  46.3 0.6 %shard_map.59 = f32[16,2,8,128]{3,2,1,0:T(8,128)S(1)} custom-call(f32[10,8,128]{2,1,0:T(8,128)S(1)} %collective-permute-done.1.in_ref, f32[10,8,128]{2,1,0:T(8,128)S(1)} %collective-permute-done.3.late_ref, f32[10,8,128]{2,1,0:T(8,128)S(1)} %collective-permute-done.4.across_ref, f32[2,10,8,128]{3,2,1,0:T(8,128)S(1)} %collective-permute-done.5.pass_ref, ...), custom_call_target="tpu_custom_call" | custom-call | tf_op jit(solution)/shard_map/pallas_call | solution.py:286
  46.9 13.5 %all_to_all.11.in_ref = f32[16,2,8,128]{3,2,1,0:T(8,128)S(1)} all-to-all(f32[16,2,8,128]{3,2,1,0:T(8,128)S(1)} %shard_map.59), channel_id=1, replica_groups={{0,1,2,3,4,5,6,7,8,9,10,11,12,13,14,15},{16,17,18,19,20,21,22,23,24,25,..., dimensions={0} | all-to-all | bytes 262144 | tf_op jit(solution)/shard_map/all_to_all | solution.py:338
  60.4 0.7 %shard_map.60 = f32[1,4,8,512]{3,2,1,0:T(8,128)} custom-call(f32[16,2,8,128]{3,2,1,0:T(8,128)S(1)} %all_to_all.11.in_ref), custom_call_target="tpu_custom_call" | custom-call | tf_op jit(solution)/shard_map/pallas_call | solution.py:286
Async XLA Ops:
  15.2 3.3 %collective-permute-start = (f32[10,8,128]{2,1,0:T(8,128)S(1)}, f32[10,8,128]{2,1,0:T(8,128)S(1)}, u32[]{:S(2)}, u32[]{:S(2)}) collective-permute-start(f32[10,8,128]{2,1,0:T(8,128)S(1)} %get-tuple-element.9), channel_id=1, source_target_pairs={{8,16},{12,20},{24,32},{28,36},{40,48},{44,52},{72,80},{76,84},{88... | collective-permute-start | bytes 122888 | tf_op jit(solution)/shard_map/ppermute | solution.py:325
  15.9 15.9 %collective-permute-start.2 = (f32[10,8,128]{2,1,0:T(8,128)S(1)}, f32[10,8,128]{2,1,0:T(8,128)S(1)}, u32[]{:S(2)}, u32[]{:S(2)}) collective-permute-start(f32[10,8,128]{2,1,0:T(8,128)S(1)} %get-tuple-element.9), channel_id=1, source_target_pairs={{56,64},{60,68},{120,128},{124,132},{184,192},{188,196},{248,256},... | collective-permute-start | bytes 122888 | tf_op jit(solution)/shard_map/ppermute | solution.py:326
  17.2 18.3 %collective-permute-start.5 = (f32[2,10,8,128]{3,2,1,0:T(8,128)S(1)}, f32[2,10,8,128]{3,2,1,0:T(8,128)S(1)}, u32[]{:S(2)}, u32[]{:S(2)}) collective-permute-start(f32[2,10,8,128]{3,2,1,0:T(8,128)S(1)} %get-tuple-element.12), channel_id=1, source_target_pairs={{8,16},{12,20},{24,32},{28,36},{40,48},{44,52},{56,64},{60,68},{72... | collective-permute-start | bytes 245768 | tf_op jit(solution)/shard_map/ppermute | solution.py:327
  32.2 3.3 %collective-permute-start.3 = (f32[10,8,128]{2,1,0:T(8,128)S(1)}, f32[10,8,128]{2,1,0:T(8,128)S(1)}, u32[]{:S(2)}, u32[]{:S(2)}) collective-permute-start(f32[10,8,128]{2,1,0:T(8,128)S(1)} %shard_map.58), channel_id=1, source_target_pairs={{0,16},{4,20},{64,80},{68,84},{128,144},{132,148},{192,208},{196,2... | collective-permute-start | bytes 122888 | tf_op jit(solution)/shard_map/ppermute | solution.py:331
  33.5 12.8 %collective-permute-start.4 = (f32[10,8,128]{2,1,0:T(8,128)S(1)}, f32[10,8,128]{2,1,0:T(8,128)S(1)}, u32[]{:S(2)}, u32[]{:S(2)}) collective-permute-start(f32[10,8,128]{2,1,0:T(8,128)S(1)} %shard_map.57.order_ref), channel_id=1, source_target_pairs={{48,64},{52,68},{112,128},{116,132},{176,192},{180,196},{240,256},... | collective-permute-start | bytes 122888 | tf_op jit(solution)/shard_map/ppermute | solution.py:330
  34.8 11.5 %collective-permute-start.1 = (f32[10,8,128]{2,1,0:T(8,128)S(1)}, f32[10,8,128]{2,1,0:T(8,128)S(1)}, u32[]{:S(2)}, u32[]{:S(2)}) collective-permute-start(f32[10,8,128]{2,1,0:T(8,128)S(1)} %shard_map.57.order_ref), channel_id=1, source_target_pairs={{16,32},{20,36},{32,48},{36,52},{80,96},{84,100},{96,112},{100,116... | collective-permute-start | bytes 122888 | tf_op jit(solution)/shard_map/ppermute | solution.py:332

commit v5 on v3

--- a/solution.py
+++ b/solution.py
@@ -5,12 +5,14 @@
 from jax.experimental.pallas import tpu as pltpu
 from jax.sharding import PartitionSpec as P
 
+
 FINE_STEPS = 8
 FINE = (0.0375, 0.025)
 COARSE = (0.3, 0.2)
 FIELDS = 4
 TILE = (8, 128)
 AXES = ("tm", "rows")
+RING = 16
 
 
 def east(x):
@@ -219,19 +221,23 @@
     return combine(jnp.add, advance(opening, coarse, *COARSE), forcing)
 
 
-def chain_kernel(in_ref, forcing_ref, slope_ref, out_ref):
-    coarse = coarse_of(slope_ref)
-    value = unfold(in_ref)
-    for pair in range(2):
-        value = relax(value, read_tiles(forcing_ref, pair), coarse)
-    fold(out_ref, value)
-
-
-def last_kernel(in_ref, pass_ref, forcing_ref, slope_ref, out_ref, rows_ref):
+def last_kernel(
+    far_ref, far_across_ref, middle_ref, middle_across_ref, pass_ref, forcing_ref, slope_ref,
+    out_ref, far_join_ref, middle_join_ref, rows_ref,
+):
+    starts = lax.axis_index("tm") % RING < 2
+    for tile in range(10):
+        far_join_ref[tile] = jnp.where(starts, far_across_ref[tile], far_ref[tile])
+        for pair in range(2):
+            middle_join_ref[pair, tile] = jnp.where(
+                starts, middle_across_ref[pair, tile], middle_ref[pair, tile]
+            )
     lanes = lane_index()
     opens = lax.axis_index("tm") < 2
     coarse = coarse_of(slope_ref)
-    value = unfold(in_ref)
+    value = unfold(far_join_ref)
+    for pair in range(2):
+        value = relax(value, unfold(middle_join_ref, pair), coarse)
     for position in range(4):
         if position < 2:
             given = unfold(pass_ref, position)
@@ -261,7 +267,7 @@
             out_ref[0, 2 * half + 1, :, cut] = jnp.where(lanes < 64, pltpu.roll(left, 64, 1), right)
 
 
-def call(kernel, shapes, name, specs=None, scratch=(), in_vmem=True, out_vmem=True):
+def call(kernel, shapes, specs=None, scratch=(), in_vmem=True, out_vmem=True):
     kind = pltpu.VMEM if out_vmem else jax.ShapeDtypeStruct
     outs = [kind(shape, jnp.float32) for shape in shapes]
     vmem = pl.BlockSpec(memory_space=pltpu.VMEM)
@@ -276,7 +282,6 @@
             in_specs=specs or [vmem] * len(args),
             out_specs=vmem if single else [vmem] * len(outs),
             scratch_shapes=scratch,
-            name=name,
         )(*args)
 
     return run
@@ -294,30 +299,40 @@
     vmem = pl.BlockSpec(memory_space=pltpu.VMEM)
     smem = pl.BlockSpec(memory_space=pltpu.SMEM)
     packed = call(
-        pack_kernel, [(8, FIELDS + 1, *TILE)], "pack", [vmem] * 4 + [smem], in_vmem=False
+        pack_kernel, [(8, FIELDS + 1, *TILE)], [vmem] * 4 + [smem], in_vmem=False
     )(start_state, initial_guess, land_mask, bed_class, bed_table)
     arrived = lax.all_to_all(packed, AXES, 0, 0, axis_index_groups=groups(count, row_devices, 2))
     state = (FIELDS, 4, *TILE)
     forcing, chain, passed, slopes = call(
         forcing_kernel,
         [(2, *state), (10, *TILE), (2, 10, *TILE), (3, 4, *TILE)],
-        "forcing",
         scratch=[pltpu.VMEM((2, FIELDS + 1, 32, 128), jnp.float32)],
     )(arrived)
-    to_even = [(i, (i + 2) % count) for i in range(count) if i % 4 >= 2]
-    to_next = [(i, i + 4) for i in range(count - 4) if i % 4 < 2]
-    chain = lax.ppermute(chain, "tm", to_even)
-    passed = lax.ppermute(passed, "tm", to_even)
-    chain = call(chain_kernel, [(10, *TILE)], "chain")(chain, forcing, slopes)
-    chain = lax.ppermute(chain, "tm", to_next)
+    even = [i for i in range(count) if i % 4 < 2]
+    odd = [i for i in range(count) if i % 4 >= 2]
+    two = [(i, (i + 2) % count) for i in odd]
+    four = [(i, i + 4) for i in even if i + 4 < count]
+    six = [(i, (i + 6) % count) for i in odd if i < count - 6 or i >= count - 2]
+
+    def send(value, pairs):
+        return lax.ppermute(value, "tm", pairs)
+
+    far_across = send(chain, [(i, j) for i, j in six if j % RING < 2])
+    middle_across = send(passed, [(i, j) for i, j in four if j % RING < 2])
+    near = send(passed, two)
+    far = send(chain, [(i, j) for i, j in six if j % RING >= 2])
+    middle = send(passed, [(i, j) for i, j in four if j % RING >= 2])
     packed = call(
         last_kernel,
         [(16, 2, *TILE)],
-        "last",
-        scratch=[pltpu.VMEM((4, FIELDS, 32, 128), jnp.float32)],
-    )(chain, passed, forcing, slopes)
+        scratch=[
+            pltpu.VMEM((10, *TILE), jnp.float32),
+            pltpu.VMEM((2, 10, *TILE), jnp.float32),
+            pltpu.VMEM((4, FIELDS, 32, 128), jnp.float32),
+        ],
+    )(far, far_across, middle, middle_across, near, forcing, slopes)
     arrived = lax.all_to_all(packed, AXES, 0, 0, axis_index_groups=groups(count, row_devices, 4))
-    return call(unpack_kernel, [initial_guess.shape], "unpack", out_vmem=False)(arrived)
+    return call(unpack_kernel, [initial_guess.shape], out_vmem=False)(arrived)
 
 
 def solution(mesh):

time: 59.4 us -> 57.6 us (0.970)
  waiting for transfers between devices: 24.4 us -> 14.6 us
  starting transfers between devices: 4.5 us -> 13 us
    ppermute x3 -> x5, waiting for transfers between devices: 24.4 us -> 14.6 us  [send(): return lax.ppermute(value, 'tm', pairs)]
    ppermute x3 -> x5, starting transfers between devices: 4.5 us -> 13 us  [send(): return lax.ppermute(value, 'tm', pairs)]
    pallas_call x5 -> x4, Pallas kernels: 5.43 us -> 5.27 us  [run(): pl.pallas_call(kernel, out_shape=outs[0] if single else outs, in_specs=sp...]
  transfers between devices with their start and end apart: 3 -> 5, of which waited for: 2 -> 1; matrix products, arithmetic and copies ran while one was open for 0% -> 0% of each run, Pallas kernels for 1% -> 0%
where the time goes in v5:
time: 57.6 us; the launch traced here: 57.3 us
  blocking collectives  24.3 us (42%)
  waiting for transfers between devices  14.6 us (25%)
  starting transfers between devices  13 us (23%)
  Pallas kernels  5.27 us (9%)
    all_to_all x2, blocking collectives, on_device(): lax.all_to_all(packed, AXES, 0, 0, axis_index_groups=groups(count, row_de...  24.3 us
    ppermute x5, waiting for transfers between devices, send(): return lax.ppermute(value, 'tm', pairs)  14.6 us
    ppermute x5, starting transfers between devices, send(): return lax.ppermute(value, 'tm', pairs)  13 us
    pallas_call x4, Pallas kernels, run(): pl.pallas_call(kernel, out_shape=outs[0] if single else outs, in_specs=sp...  5.27 us
  transfers between devices with their start and end apart: 5, of which 1 were waited for; matrix products, arithmetic and copies ran while one was open for 0% of the time, Pallas kernels for 0%

profile of v5, /device:TPU:2, one launch (start us, length us, event | category | flops | bytes accessed | tf_op | source)
XLA Modules:
  0.0 57.3 jit_solution(16375488478772743714)
XLA Ops:
  0.0 1.0 %shard_map.55 = f32[8,5,8,128]{3,2,1,0:T(8,128)S(1)} custom-call(f32[4,8,512]{2,1,0:T(8,128)} %start_ref.1, f32[1,4,8,512]{3,2,1,0:T(8,128)} %guess_ref.1, s32[8,512]{1,0:T(8,128)} %mask_ref.1, s32[8,512]{1,0:T(8,128)} %class_ref.1, f32[16]{0:T(128)} %table_ref.1), custom_call_target="tpu_custom_call" | custom-call | tf_op jit(solution)/shard_map/pallas_call | solution.py:279
  1.0 11.5 %all_to_all.10.in_ref = f32[8,5,8,128]{3,2,1,0:T(8,128)S(1)} all-to-all(f32[8,5,8,128]{3,2,1,0:T(8,128)S(1)} %shard_map.55), channel_id=1, replica_groups={{0,1,2,3,4,5,6,7},{8,9,10,11,12,13,14,15},{16,17,18,19,20,21,22,23},{24..., dimensions={0} | all-to-all | bytes 327680 | tf_op jit(solution)/shard_map/all_to_all | solution.py:304
  12.5 2.7 %shard_map.56 = (f32[2,4,4,8,128]{4,3,2,1,0:T(8,128)S(1)}, f32[10,8,128]{2,1,0:T(8,128)S(1)}, f32[2,10,8,128]{3,2,1,0:T(8,128)S(1)}, f32[3,4,8,128]{3,2,1,0:T(8,128)S(1)}) custom-call(f32[8,5,8,128]{3,2,1,0:T(8,128)S(1)} %all_to_all.10.in_ref), custom_call_target="tpu_custom_call" | custom-call | tf_op jit(solution)/shard_map/pallas_call | solution.py:279
  15.2 1.3 %collective-permute-start.4 = (f32[2,10,8,128]{3,2,1,0:T(8,128)S(1)}, f32[2,10,8,128]{3,2,1,0:T(8,128)S(1)}, u32[]{:S(2)}, u32[]{:S(2)}) collective-permute-start(f32[2,10,8,128]{3,2,1,0:T(8,128)S(1)} %get-tuple-element.10), channel_id=1, source_target_pairs={{8,16},{12,20},{24,32},{28,36},{40,48},{44,52},{56,64},{60,68},{72... | collective-permute-start | bytes 245768 | tf_op jit(solution)/shard_map/ppermute | solution.py:318
  16.5 1.3 %collective-permute-start.3 = (f32[2,10,8,128]{3,2,1,0:T(8,128)S(1)}, f32[2,10,8,128]{3,2,1,0:T(8,128)S(1)}, u32[]{:S(2)}, u32[]{:S(2)}) collective-permute-start(f32[2,10,8,128]{3,2,1,0:T(8,128)S(1)} %get-tuple-element.10), channel_id=1, source_target_pairs={{48,64},{52,68},{112,128},{116,132},{176,192},{180,196},{240,256},... | collective-permute-start | bytes 245768 | tf_op jit(solution)/shard_map/ppermute | solution.py:318
  17.8 8.5 %collective-permute-start.2 = (f32[2,10,8,128]{3,2,1,0:T(8,128)S(1)}, f32[2,10,8,128]{3,2,1,0:T(8,128)S(1)}, u32[]{:S(2)}, u32[]{:S(2)}) collective-permute-start(f32[2,10,8,128]{3,2,1,0:T(8,128)S(1)} %get-tuple-element.10), channel_id=1, source_target_pairs={{0,16},{4,20},{16,32},{20,36},{32,48},{36,52},{64,80},{68,84},{80,... | collective-permute-start | bytes 245768 | tf_op jit(solution)/shard_map/ppermute | solution.py:318
  26.3 1.3 %collective-permute-start.1 = (f32[10,8,128]{2,1,0:T(8,128)S(1)}, f32[10,8,128]{2,1,0:T(8,128)S(1)}, u32[]{:S(2)}, u32[]{:S(2)}) collective-permute-start(f32[10,8,128]{2,1,0:T(8,128)S(1)} %get-tuple-element.9), channel_id=1, source_target_pairs={{40,64},{44,68},{104,128},{108,132},{168,192},{172,196},{232,256},... | collective-permute-start | bytes 122888 | tf_op jit(solution)/shard_map/ppermute | solution.py:318
  27.6 0.7 %collective-permute-start = (f32[10,8,128]{2,1,0:T(8,128)S(1)}, f32[10,8,128]{2,1,0:T(8,128)S(1)}, u32[]{:S(2)}, u32[]{:S(2)}) collective-permute-start(f32[10,8,128]{2,1,0:T(8,128)S(1)} %get-tuple-element.9), channel_id=1, source_target_pairs={{8,32},{12,36},{24,48},{28,52},{56,80},{60,84},{72,96},{76,100},{8... | collective-permute-start | bytes 122888 | tf_op jit(solution)/shard_map/ppermute | solution.py:318
  28.3 14.6 %collective-permute-done.1.far_across_ref = f32[10,8,128]{2,1,0:T(8,128)S(1)} collective-permute-done((f32[10,8,128]{2,1,0:T(8,128)S(1)}, f32[10,8,128]{2,1,0:T(8,128)S(1)}, u32[]{:S(2)}, u32[]{:S(2)}) %collective-permute-start.1) | collective-permute-done | bytes 40992 | tf_op jit(solution)/shard_map/ppermute | solution.py:318
  42.9 0.0 collective-permute-done.far_ref
  42.9 0.0 collective-permute-done.4.pass_ref
  42.9 0.0 collective-permute-done.3.middle_across_ref
  42.9 0.0 collective-permute-done.2.middle_ref
  42.9 0.8 %shard_map.57 = f32[16,2,8,128]{3,2,1,0:T(8,128)S(1)} custom-call(f32[10,8,128]{2,1,0:T(8,128)S(1)} %collective-permute-done.far_ref, f32[10,8,128]{2,1,0:T(8,128)S(1)} %collective-permute-done.1.far_across_ref, f32[2,10,8,128]{3,2,1,0:T(8,128)S(1)} %collective-permute-done.2.middle_ref, f32[2,10,8,128]{3,2,1,0:T(8,128)S(1)} %collective-permute-done.3.middle_across_ref, ...), custom_call_target="tpu_custom_call" | custom-call | tf_op jit(solution)/shard_map/pallas_call | solution.py:279
  43.7 12.9 %all_to_all.11.in_ref = f32[16,2,8,128]{3,2,1,0:T(8,128)S(1)} all-to-all(f32[16,2,8,128]{3,2,1,0:T(8,128)S(1)} %shard_map.57), channel_id=1, replica_groups={{0,1,2,3,4,5,6,7,8,9,10,11,12,13,14,15},{16,17,18,19,20,21,22,23,24,25,..., dimensions={0} | all-to-all | bytes 262144 | tf_op jit(solution)/shard_map/all_to_all | solution.py:334
  56.6 0.7 %shard_map.58 = f32[1,4,8,512]{3,2,1,0:T(8,128)} custom-call(f32[16,2,8,128]{3,2,1,0:T(8,128)S(1)} %all_to_all.11.in_ref), custom_call_target="tpu_custom_call" | custom-call | tf_op jit(solution)/shard_map/pallas_call | solution.py:279
Async XLA Ops:
  15.2 27.7 %collective-permute-start.4 = (f32[2,10,8,128]{3,2,1,0:T(8,128)S(1)}, f32[2,10,8,128]{3,2,1,0:T(8,128)S(1)}, u32[]{:S(2)}, u32[]{:S(2)}) collective-permute-start(f32[2,10,8,128]{3,2,1,0:T(8,128)S(1)} %get-tuple-element.10), channel_id=1, source_target_pairs={{8,16},{12,20},{24,32},{28,36},{40,48},{44,52},{56,64},{60,68},{72... | collective-permute-start | bytes 245768 | tf_op jit(solution)/shard_map/ppermute | solution.py:318
  16.5 26.4 %collective-permute-start.3 = (f32[2,10,8,128]{3,2,1,0:T(8,128)S(1)}, f32[2,10,8,128]{3,2,1,0:T(8,128)S(1)}, u32[]{:S(2)}, u32[]{:S(2)}) collective-permute-start(f32[2,10,8,128]{3,2,1,0:T(8,128)S(1)} %get-tuple-element.10), channel_id=1, source_target_pairs={{48,64},{52,68},{112,128},{116,132},{176,192},{180,196},{240,256},... | collective-permute-start | bytes 245768 | tf_op jit(solution)/shard_map/ppermute | solution.py:318
  17.8 25.1 %collective-permute-start.2 = (f32[2,10,8,128]{3,2,1,0:T(8,128)S(1)}, f32[2,10,8,128]{3,2,1,0:T(8,128)S(1)}, u32[]{:S(2)}, u32[]{:S(2)}) collective-permute-start(f32[2,10,8,128]{3,2,1,0:T(8,128)S(1)} %get-tuple-element.10), channel_id=1, source_target_pairs={{0,16},{4,20},{16,32},{20,36},{32,48},{36,52},{64,80},{68,84},{80,... | collective-permute-start | bytes 245768 | tf_op jit(solution)/shard_map/ppermute | solution.py:318
  26.3 16.6 %collective-permute-start.1 = (f32[10,8,128]{2,1,0:T(8,128)S(1)}, f32[10,8,128]{2,1,0:T(8,128)S(1)}, u32[]{:S(2)}, u32[]{:S(2)}) collective-permute-start(f32[10,8,128]{2,1,0:T(8,128)S(1)} %get-tuple-element.9), channel_id=1, source_target_pairs={{40,64},{44,68},{104,128},{108,132},{168,192},{172,196},{232,256},... | collective-permute-start | bytes 122888 | tf_op jit(solution)/shard_map/ppermute | solution.py:318
  27.6 15.3 %collective-permute-start = (f32[10,8,128]{2,1,0:T(8,128)S(1)}, f32[10,8,128]{2,1,0:T(8,128)S(1)}, u32[]{:S(2)}, u32[]{:S(2)}) collective-permute-start(f32[10,8,128]{2,1,0:T(8,128)S(1)} %get-tuple-element.9), channel_id=1, source_target_pairs={{8,32},{12,36},{24,48},{28,52},{56,80},{60,84},{72,96},{76,100},{8... | collective-permute-start | bytes 122888 | tf_op jit(solution)/shard_map/ppermute | solution.py:318

commit v6 on v5

--- a/solution.py
+++ b/solution.py
@@ -12,6 +12,7 @@
 FIELDS = 4
 TILE = (8, 128)
 AXES = ("tm", "rows")
+SMALLEST = 1.1754944e-38
 RING = 16
 
 
@@ -35,24 +36,22 @@
     slope_e, slope_n, wet = statics
     half = 0.5 * ratio
     h, p, s, m = state
-    inverse = [1.0 / a for a in h]
+    inverse = [half / a for a in h]
     u = [a * b for a, b in zip(p, inverse)]
     v = [a * b for a, b in zip(s, inverse)]
-    hu = [half * a for a in u]
-    hv = [half * a for a in v]
     pressure = [(0.5 * half) * (a * a) for a in h]
-    cross = [a * b for a, b in zip(s, hu)]
+    cross = [a * b for a, b in zip(s, u)]
     east_flux = (
         [half * a for a in p],
-        [a * b + c for a, b, c in zip(p, hu, pressure)],
+        [a * b + c for a, b, c in zip(p, u, pressure)],
         cross,
-        [a * b for a, b in zip(m, hu)],
+        [a * b for a, b in zip(m, u)],
     )
     north_flux = (
         [half * a for a in s],
         cross,
-        [a * b + c for a, b, c in zip(s, hv, pressure)],
-        [a * b for a, b in zip(m, hv)],
+        [a * b + c for a, b, c in zip(s, v, pressure)],
+        [a * b for a, b in zip(m, v)],
     )
     moved = []
     for field in range(FIELDS):
@@ -68,12 +67,12 @@
     new_p, new_s, new_m = [], [], []
     for k in range(4):
         square = u[k] * u[k] + v[k] * v[k]
-        drag = (0.02 * ratio) * jnp.sqrt(square)
+        root = square * lax.rsqrt(jnp.maximum(square, SMALLEST))
+        drag = (0.02 * ratio / half**2) * root
         new_p.append(wet[k] * (moved[1][k] - (h[k] * slope_e[k] + drag * u[k])))
         new_s.append(wet[k] * (moved[2][k] - (h[k] * slope_n[k] + drag * v[k])))
-        new_m.append(
-            moved[3][k] + ((0.05 * ratio) * square - (0.3 * ratio) * (m[k] * inverse[k]))
-        )
+        settled = (0.3 * ratio / half) * (m[k] * inverse[k])
+        new_m.append(moved[3][k] + ((0.05 * ratio / half**2) * square - settled))
     return [moved[0], new_p, new_s, new_m]
 
 
@@ -133,36 +132,57 @@
     windows(FIELDS, static)
 
 
-def fold(ref, state, *lead):
-    lanes = lane_index()
-    for half in range(2):
-        for k in range(4):
-            low = pltpu.roll(state[2 * half][k], 96, 1)
-            high = pltpu.roll(state[2 * half + 1][k], 32, 1)
-            ref[(*lead, 4 * half + k)] = jnp.where(lanes < 64, low, high)
-        edge = None
-        for slot in range(8):
-            tile = state[2 * half + slot // 4][slot % 4]
-            left = pltpu.roll(tile, (16 * slot - 24) % 128, 1)
-            right = pltpu.roll(tile, (16 * slot + 8 - 96) % 128, 1)
-            both = jnp.where(lanes < 16 * slot + 8, left, right)
-            edge = both if edge is None else jnp.where(lanes < 16 * slot, edge, both)
-        ref[(*lead, 8 + half)] = edge
-
-
-def unfold(ref, *lead):
-    lanes = lane_index()
+SLOTS = {5: 11, 7: 8}
+DIVIDE = {5: 205, 7: 147}
+
+
+def payload(states, width):
+    return 8 * states - (-16 * states // SLOTS[width])
+
+
+def slot_of_lane(width):
+    lanes = lane_index()
+    right = ((lanes - 64) * DIVIDE[width]) >> 10
+    left = (lanes * DIVIDE[width]) >> 10
+    inside = jnp.where(lanes < 64, left + 1, right)
+    return jnp.where(lanes >= 128 - width, 0, inside)
+
+
+def fold(ref, states, width):
+    lanes, slots = lane_index(), slot_of_lane(width)
+    edges = [None] * (payload(len(states), width) - 8 * len(states))
+    for index, state in enumerate(states):
+        for k in range(4):
+            for half in range(2):
+                low = pltpu.roll(state[2 * half][k], 96, 1)
+                high = pltpu.roll(state[2 * half + 1][k], 32, 1)
+                ref[8 * index + 4 * half + k] = jnp.where(lanes < 64, low, high)
+                for part, turned in enumerate((low, high)):
+                    number = 16 * index + 4 * (2 * half + part) + k
+                    edge, slot = divmod(number, SLOTS[width])
+                    shift = (64 * part + width * slot) % 128
+                    moved = pltpu.roll(turned, shift, 1) if shift else turned
+                    edges[edge] = (
+                        moved
+                        if edges[edge] is None
+                        else jnp.where(slots == slot, moved, edges[edge])
+                    )
+    for index, edge in enumerate(edges):
+        ref[8 * len(states) + index] = edge
+
+
+def unfold(ref, states, width, index=0):
+    lanes = lane_index()
+    own_lanes = (lanes >= 32) & (lanes < 96)
     state = [[None] * 4 for _ in range(FIELDS)]
-    for half in range(2):
-        edge = ref[(*lead, 8 + half)]
-        for slot in range(8):
-            k = slot % 4
-            own = pltpu.roll(ref[(*lead, 4 * half + k)], 32 if slot < 4 else 96, 1)
-            left = pltpu.roll(edge, (24 - 16 * slot) % 128, 1)
-            right = pltpu.roll(edge, (96 - 16 * slot - 8) % 128, 1)
-            state[2 * half + slot // 4][k] = jnp.where(
-                lanes < 32, left, jnp.where(lanes < 96, own, right)
-            )
+    for field in range(FIELDS):
+        for k in range(4):
+            main = ref[8 * index + 4 * (field // 2) + k]
+            own = pltpu.roll(main, 32 if field % 2 == 0 else 96, 1)
+            edge, slot = divmod(16 * index + 4 * field + k, SLOTS[width])
+            edge = ref[8 * states + edge]
+            shift = (32 - width * slot) % 128
+            state[field][k] = jnp.where(own_lanes, own, pltpu.roll(edge, shift, 1))
     return state
 
 
@@ -193,7 +213,7 @@
             pairs = jax.tree.unflatten(shape, leaves)
             return tuple(flat([advance(state, fine, *FINE) for state in pairs]))
 
-        return jax.tree.unflatten(shape, lax.fori_loop(0, FINE_STEPS, body, tuple(flat(states))))
+        return jax.tree.unflatten(shape, lax.fori_loop(0, FINE_STEPS, body, tuple(flat(states)), unroll=8))
 
     def choose(a, b):
         return combine(lambda x, y: jnp.where(last, x, y), a, b)
@@ -206,9 +226,8 @@
         for pair in range(2)
     ]
     second = combine(jnp.add, advance(reached[0], coarse, *COARSE), forcing[1])
-    fold(chain_ref, second)
-    fold(pass_ref, choose(reached[0], forcing[0]), 0)
-    fold(pass_ref, choose(second, forcing[1]), 1)
+    fold(chain_ref, [second], 7)
+    fold(pass_ref, [choose(reached[0], forcing[0]), choose(second, forcing[1])], 5)
     for pair in range(2):
         write_tiles(forcing_ref, forcing[pair], pair)
 
@@ -226,21 +245,19 @@
     out_ref, far_join_ref, middle_join_ref, rows_ref,
 ):
     starts = lax.axis_index("tm") % RING < 2
-    for tile in range(10):
+    for tile in range(far_ref.shape[0]):
         far_join_ref[tile] = jnp.where(starts, far_across_ref[tile], far_ref[tile])
-        for pair in range(2):
-            middle_join_ref[pair, tile] = jnp.where(
-                starts, middle_across_ref[pair, tile], middle_ref[pair, tile]
-            )
+    for tile in range(middle_ref.shape[0]):
+        middle_join_ref[tile] = jnp.where(starts, middle_across_ref[tile], middle_ref[tile])
     lanes = lane_index()
     opens = lax.axis_index("tm") < 2
     coarse = coarse_of(slope_ref)
-    value = unfold(far_join_ref)
+    value = unfold(far_join_ref, 1, 7)
     for pair in range(2):
-        value = relax(value, unfold(middle_join_ref, pair), coarse)
+        value = relax(value, unfold(middle_join_ref, 2, 5, pair), coarse)
     for position in range(4):
         if position < 2:
-            given = unfold(pass_ref, position)
+            given = unfold(pass_ref, 2, 5, position)
             value = combine(
                 lambda a, b: jnp.where(opens, a, b), given, relax(value, given, coarse)
             )
@@ -305,7 +322,7 @@
     state = (FIELDS, 4, *TILE)
     forcing, chain, passed, slopes = call(
         forcing_kernel,
-        [(2, *state), (10, *TILE), (2, 10, *TILE), (3, 4, *TILE)],
+        [(2, *state), (payload(1, 7), *TILE), (payload(2, 5), *TILE), (3, 4, *TILE)],
         scratch=[pltpu.VMEM((2, FIELDS + 1, 32, 128), jnp.float32)],
     )(arrived)
     even = [i for i in range(count) if i % 4 < 2]
@@ -326,8 +343,8 @@
         last_kernel,
         [(16, 2, *TILE)],
         scratch=[
-            pltpu.VMEM((10, *TILE), jnp.float32),
-            pltpu.VMEM((2, 10, *TILE), jnp.float32),
+            pltpu.VMEM((payload(1, 7), *TILE), jnp.float32),
+            pltpu.VMEM((payload(2, 5), *TILE), jnp.float32),
             pltpu.VMEM((4, FIELDS, 32, 128), jnp.float32),
         ],
     )(far, far_across, middle, middle_across, near, forcing, slopes)

time: 57.6 us -> 57.1 us (level)
  no operation moved by 1% of the time
where the time goes in v6:
time: 57.1 us; the launch traced here: 56.8 us
  blocking collectives  24.3 us (43%)
  waiting for transfers between devices  14.5 us (25%)
  starting transfers between devices  13 us (23%)
  Pallas kernels  4.93 us (9%)
    all_to_all x2, blocking collectives, on_device(): lax.all_to_all(packed, AXES, 0, 0, axis_index_groups=groups(count, row_de...  24.3 us
    ppermute x5, waiting for transfers between devices, send(): return lax.ppermute(value, 'tm', pairs)  14.5 us
    ppermute x5, starting transfers between devices, send(): return lax.ppermute(value, 'tm', pairs)  13 us
    pallas_call x4, Pallas kernels, run(): pl.pallas_call(kernel, out_shape=outs[0] if single else outs, in_specs=sp...  4.93 us
  transfers between devices with their start and end apart: 5, of which 1 were waited for; matrix products, arithmetic and copies ran while one was open for 0% of the time, Pallas kernels for 0%

profile of v6, /device:TPU:2, one launch (start us, length us, event | category | flops | bytes accessed | tf_op | source)
XLA Modules:
  0.0 56.8 jit_solution(17930452666878469633)
XLA Ops:
  0.0 1.0 %shard_map.55 = f32[8,5,8,128]{3,2,1,0:T(8,128)S(1)} custom-call(f32[4,8,512]{2,1,0:T(8,128)} %start_ref.1, f32[1,4,8,512]{3,2,1,0:T(8,128)} %guess_ref.1, s32[8,512]{1,0:T(8,128)} %mask_ref.1, s32[8,512]{1,0:T(8,128)} %class_ref.1, f32[16]{0:T(128)} %table_ref.1), custom_call_target="tpu_custom_call" | custom-call | tf_op jit(solution)/shard_map/pallas_call | solution.py:296
  1.0 11.5 %all_to_all.10.in_ref = f32[8,5,8,128]{3,2,1,0:T(8,128)S(1)} all-to-all(f32[8,5,8,128]{3,2,1,0:T(8,128)S(1)} %shard_map.55), channel_id=1, replica_groups={{0,1,2,3,4,5,6,7},{8,9,10,11,12,13,14,15},{16,17,18,19,20,21,22,23},{24..., dimensions={0} | all-to-all | bytes 327680 | tf_op jit(solution)/shard_map/all_to_all | solution.py:321
  12.5 2.4 %shard_map.56 = (f32[2,4,4,8,128]{4,3,2,1,0:T(8,128)S(1)}, f32[10,8,128]{2,1,0:T(8,128)S(1)}, f32[19,8,128]{2,1,0:T(8,128)S(1)}, f32[3,4,8,128]{3,2,1,0:T(8,128)S(1)}) custom-call(f32[8,5,8,128]{3,2,1,0:T(8,128)S(1)} %all_to_all.10.in_ref), custom_call_target="tpu_custom_call" | custom-call | tf_op jit(solution)/shard_map/pallas_call | solution.py:296
  14.9 1.3 %collective-permute-start.4 = (f32[19,8,128]{2,1,0:T(8,128)S(1)}, f32[19,8,128]{2,1,0:T(8,128)S(1)}, u32[]{:S(2)}, u32[]{:S(2)}) collective-permute-start(f32[19,8,128]{2,1,0:T(8,128)S(1)} %get-tuple-element.10), channel_id=1, source_target_pairs={{8,16},{12,20},{24,32},{28,36},{40,48},{44,52},{56,64},{60,68},{72... | collective-permute-start | bytes 233480 | tf_op jit(solution)/shard_map/ppermute | solution.py:335
  16.2 1.3 %collective-permute-start.3 = (f32[19,8,128]{2,1,0:T(8,128)S(1)}, f32[19,8,128]{2,1,0:T(8,128)S(1)}, u32[]{:S(2)}, u32[]{:S(2)}) collective-permute-start(f32[19,8,128]{2,1,0:T(8,128)S(1)} %get-tuple-element.10), channel_id=1, source_target_pairs={{48,64},{52,68},{112,128},{116,132},{176,192},{180,196},{240,256},... | collective-permute-start | bytes 233480 | tf_op jit(solution)/shard_map/ppermute | solution.py:335
  17.5 8.5 %collective-permute-start.2 = (f32[19,8,128]{2,1,0:T(8,128)S(1)}, f32[19,8,128]{2,1,0:T(8,128)S(1)}, u32[]{:S(2)}, u32[]{:S(2)}) collective-permute-start(f32[19,8,128]{2,1,0:T(8,128)S(1)} %get-tuple-element.10), channel_id=1, source_target_pairs={{0,16},{4,20},{16,32},{20,36},{32,48},{36,52},{64,80},{68,84},{80,... | collective-permute-start | bytes 233480 | tf_op jit(solution)/shard_map/ppermute | solution.py:335
  26.0 1.3 %collective-permute-start.1 = (f32[10,8,128]{2,1,0:T(8,128)S(1)}, f32[10,8,128]{2,1,0:T(8,128)S(1)}, u32[]{:S(2)}, u32[]{:S(2)}) collective-permute-start(f32[10,8,128]{2,1,0:T(8,128)S(1)} %get-tuple-element.9), channel_id=1, source_target_pairs={{40,64},{44,68},{104,128},{108,132},{168,192},{172,196},{232,256},... | collective-permute-start | bytes 122888 | tf_op jit(solution)/shard_map/ppermute | solution.py:335
  27.3 0.7 %collective-permute-start = (f32[10,8,128]{2,1,0:T(8,128)S(1)}, f32[10,8,128]{2,1,0:T(8,128)S(1)}, u32[]{:S(2)}, u32[]{:S(2)}) collective-permute-start(f32[10,8,128]{2,1,0:T(8,128)S(1)} %get-tuple-element.9), channel_id=1, source_target_pairs={{8,32},{12,36},{24,48},{28,52},{56,80},{60,84},{72,96},{76,100},{8... | collective-permute-start | bytes 122888 | tf_op jit(solution)/shard_map/ppermute | solution.py:335
  27.9 14.5 %collective-permute-done.1.far_across_ref = f32[10,8,128]{2,1,0:T(8,128)S(1)} collective-permute-done((f32[10,8,128]{2,1,0:T(8,128)S(1)}, f32[10,8,128]{2,1,0:T(8,128)S(1)}, u32[]{:S(2)}, u32[]{:S(2)}) %collective-permute-start.1) | collective-permute-done | bytes 40992 | tf_op jit(solution)/shard_map/ppermute | solution.py:335
  42.4 0.0 collective-permute-done.far_ref
  42.4 0.0 collective-permute-done.4.pass_ref
  42.4 0.0 collective-permute-done.3.middle_across_ref
  42.4 0.0 collective-permute-done.2.middle_ref
  42.4 0.8 %shard_map.57 = f32[16,2,8,128]{3,2,1,0:T(8,128)S(1)} custom-call(f32[10,8,128]{2,1,0:T(8,128)S(1)} %collective-permute-done.far_ref, f32[10,8,128]{2,1,0:T(8,128)S(1)} %collective-permute-done.1.far_across_ref, f32[19,8,128]{2,1,0:T(8,128)S(1)} %collective-permute-done.2.middle_ref, f32[19,8,128]{2,1,0:T(8,128)S(1)} %collective-permute-done.3.middle_across_ref, ...), custom_call_target="tpu_custom_call" | custom-call | tf_op jit(solution)/shard_map/pallas_call | solution.py:296
  43.3 12.8 %all_to_all.11.in_ref = f32[16,2,8,128]{3,2,1,0:T(8,128)S(1)} all-to-all(f32[16,2,8,128]{3,2,1,0:T(8,128)S(1)} %shard_map.57), channel_id=1, replica_groups={{0,1,2,3,4,5,6,7,8,9,10,11,12,13,14,15},{16,17,18,19,20,21,22,23,24,25,..., dimensions={0} | all-to-all | bytes 262144 | tf_op jit(solution)/shard_map/all_to_all | solution.py:351
  56.1 0.7 %shard_map.58 = f32[1,4,8,512]{3,2,1,0:T(8,128)} custom-call(f32[16,2,8,128]{3,2,1,0:T(8,128)S(1)} %all_to_all.11.in_ref), custom_call_target="tpu_custom_call" | custom-call | tf_op jit(solution)/shard_map/pallas_call | solution.py:296
Async XLA Ops:
  14.9 27.5 %collective-permute-start.4 = (f32[19,8,128]{2,1,0:T(8,128)S(1)}, f32[19,8,128]{2,1,0:T(8,128)S(1)}, u32[]{:S(2)}, u32[]{:S(2)}) collective-permute-start(f32[19,8,128]{2,1,0:T(8,128)S(1)} %get-tuple-element.10), channel_id=1, source_target_pairs={{8,16},{12,20},{24,32},{28,36},{40,48},{44,52},{56,64},{60,68},{72... | collective-permute-start | bytes 233480 | tf_op jit(solution)/shard_map/ppermute | solution.py:335
  16.2 26.2 %collective-permute-start.3 = (f32[19,8,128]{2,1,0:T(8,128)S(1)}, f32[19,8,128]{2,1,0:T(8,128)S(1)}, u32[]{:S(2)}, u32[]{:S(2)}) collective-permute-start(f32[19,8,128]{2,1,0:T(8,128)S(1)} %get-tuple-element.10), channel_id=1, source_target_pairs={{48,64},{52,68},{112,128},{116,132},{176,192},{180,196},{240,256},... | collective-permute-start | bytes 233480 | tf_op jit(solution)/shard_map/ppermute | solution.py:335
  17.5 24.9 %collective-permute-start.2 = (f32[19,8,128]{2,1,0:T(8,128)S(1)}, f32[19,8,128]{2,1,0:T(8,128)S(1)}, u32[]{:S(2)}, u32[]{:S(2)}) collective-permute-start(f32[19,8,128]{2,1,0:T(8,128)S(1)} %get-tuple-element.10), channel_id=1, source_target_pairs={{0,16},{4,20},{16,32},{20,36},{32,48},{36,52},{64,80},{68,84},{80,... | collective-permute-start | bytes 233480 | tf_op jit(solution)/shard_map/ppermute | solution.py:335
  26.0 16.5 %collective-permute-start.1 = (f32[10,8,128]{2,1,0:T(8,128)S(1)}, f32[10,8,128]{2,1,0:T(8,128)S(1)}, u32[]{:S(2)}, u32[]{:S(2)}) collective-permute-start(f32[10,8,128]{2,1,0:T(8,128)S(1)} %get-tuple-element.9), channel_id=1, source_target_pairs={{40,64},{44,68},{104,128},{108,132},{168,192},{172,196},{232,256},... | collective-permute-start | bytes 122888 | tf_op jit(solution)/shard_map/ppermute | solution.py:335
  27.3 15.2 %collective-permute-start = (f32[10,8,128]{2,1,0:T(8,128)S(1)}, f32[10,8,128]{2,1,0:T(8,128)S(1)}, u32[]{:S(2)}, u32[]{:S(2)}) collective-permute-start(f32[10,8,128]{2,1,0:T(8,128)S(1)} %get-tuple-element.9), channel_id=1, source_target_pairs={{8,32},{12,36},{24,48},{28,52},{56,80},{60,84},{72,96},{76,100},{8... | collective-permute-start | bytes 122888 | tf_op jit(solution)/shard_map/ppermute | solution.py:335

commit v7 on v6

--- a/solution.py
+++ b/solution.py
@@ -241,14 +241,16 @@
 
 
 def last_kernel(
-    far_ref, far_across_ref, middle_ref, middle_across_ref, pass_ref, forcing_ref, slope_ref,
-    out_ref, far_join_ref, middle_join_ref, rows_ref,
+    far_ref, far_across_ref, middle_ref, middle_across_ref, near_ref, near_across_ref, forcing_ref,
+    slope_ref, out_ref, far_join_ref, middle_join_ref, near_join_ref, rows_ref,
 ):
     starts = lax.axis_index("tm") % RING < 2
+    early = starts | (lax.axis_index("tm") % RING >= RING - 4)
     for tile in range(far_ref.shape[0]):
-        far_join_ref[tile] = jnp.where(starts, far_across_ref[tile], far_ref[tile])
+        far_join_ref[tile] = jnp.where(early, far_across_ref[tile], far_ref[tile])
     for tile in range(middle_ref.shape[0]):
         middle_join_ref[tile] = jnp.where(starts, middle_across_ref[tile], middle_ref[tile])
+        near_join_ref[tile] = jnp.where(starts, near_across_ref[tile], near_ref[tile])
     lanes = lane_index()
     opens = lax.axis_index("tm") < 2
     coarse = coarse_of(slope_ref)
@@ -257,7 +259,7 @@
         value = relax(value, unfold(middle_join_ref, 2, 5, pair), coarse)
     for position in range(4):
         if position < 2:
-            given = unfold(pass_ref, 2, 5, position)
+            given = unfold(near_join_ref, 2, 5, position)
             value = combine(
                 lambda a, b: jnp.where(opens, a, b), given, relax(value, given, coarse)
             )
@@ -334,10 +336,11 @@
     def send(value, pairs):
         return lax.ppermute(value, "tm", pairs)
 
-    far_across = send(chain, [(i, j) for i, j in six if j % RING < 2])
+    far_across = send(chain, [(i, j) for i, j in six if j % RING < 2 or j % RING >= RING - 4])
     middle_across = send(passed, [(i, j) for i, j in four if j % RING < 2])
-    near = send(passed, two)
-    far = send(chain, [(i, j) for i, j in six if j % RING >= 2])
+    near_across = send(passed, [(i, j) for i, j in two if j % RING < 2])
+    near = send(passed, [(i, j) for i, j in two if j % RING >= 2])
+    far = send(chain, [(i, j) for i, j in six if 2 <= j % RING < RING - 4])
     middle = send(passed, [(i, j) for i, j in four if j % RING >= 2])
     packed = call(
         last_kernel,
@@ -345,9 +348,10 @@
         scratch=[
             pltpu.VMEM((payload(1, 7), *TILE), jnp.float32),
             pltpu.VMEM((payload(2, 5), *TILE), jnp.float32),
+            pltpu.VMEM((payload(2, 5), *TILE), jnp.float32),
             pltpu.VMEM((4, FIELDS, 32, 128), jnp.float32),
         ],
-    )(far, far_across, middle, middle_across, near, forcing, slopes)
+    )(far, far_across, middle, middle_across, near, near_across, forcing, slopes)
     arrived = lax.all_to_all(packed, AXES, 0, 0, axis_index_groups=groups(count, row_devices, 4))
     return call(unpack_kernel, [initial_guess.shape], out_vmem=False)(arrived)
 

time: 57.1 us -> 57 us (level)
  the two profiles are of different devices: /device:TPU:2 before, /device:TPU:128 now
where the time goes in v7:
time: 57 us; the launch traced here: 56.7 us
  blocking collectives  24.4 us (43%)
  waiting for transfers between devices  14.5 us (25%)
  starting transfers between devices  12.8 us (22%)
  Pallas kernels  4.93 us (9%)
    all_to_all x2, blocking collectives, on_device(): lax.all_to_all(packed, AXES, 0, 0, axis_index_groups=groups(count, row_de...  24.4 us
    ppermute x6, waiting for transfers between devices, send(): return lax.ppermute(value, 'tm', pairs)  14.5 us
    ppermute x6, starting transfers between devices, send(): return lax.ppermute(value, 'tm', pairs)  12.8 us
    pallas_call x4, Pallas kernels, run(): pl.pallas_call(kernel, out_shape=outs[0] if single else outs, in_specs=sp...  4.93 us
  transfers between devices with their start and end apart: 6, of which 1 were waited for; matrix products, arithmetic and copies ran while one was open for 0% of the time, Pallas kernels for 0%

profile of v7, /device:TPU:128, one launch (start us, length us, event | category | flops | bytes accessed | tf_op | source)
XLA Modules:
  0.0 56.7 jit_solution(354167565649336145)
XLA Ops:
  0.0 1.0 %shard_map.55 = f32[8,5,8,128]{3,2,1,0:T(8,128)S(1)} custom-call(f32[4,8,512]{2,1,0:T(8,128)} %start_ref.1, f32[1,4,8,512]{3,2,1,0:T(8,128)} %guess_ref.1, s32[8,512]{1,0:T(8,128)} %mask_ref.1, s32[8,512]{1,0:T(8,128)} %class_ref.1, f32[16]{0:T(128)} %table_ref.1), custom_call_target="tpu_custom_call" | custom-call | tf_op jit(solution)/shard_map/pallas_call | solution.py:298
  1.0 12.4 %all_to_all.10.in_ref = f32[8,5,8,128]{3,2,1,0:T(8,128)S(1)} all-to-all(f32[8,5,8,128]{3,2,1,0:T(8,128)S(1)} %shard_map.55), channel_id=1, replica_groups={{0,1,2,3,4,5,6,7},{8,9,10,11,12,13,14,15},{16,17,18,19,20,21,22,23},{24..., dimensions={0} | all-to-all | bytes 327680 | tf_op jit(solution)/shard_map/all_to_all | solution.py:323
  13.4 2.4 %shard_map.56 = (f32[2,4,4,8,128]{4,3,2,1,0:T(8,128)S(1)}, f32[10,8,128]{2,1,0:T(8,128)S(1)}, f32[19,8,128]{2,1,0:T(8,128)S(1)}, f32[3,4,8,128]{3,2,1,0:T(8,128)S(1)}) custom-call(f32[8,5,8,128]{3,2,1,0:T(8,128)S(1)} %all_to_all.10.in_ref), custom_call_target="tpu_custom_call" | custom-call | tf_op jit(solution)/shard_map/pallas_call | solution.py:298
  15.8 0.7 %collective-permute-start.1 = (f32[10,8,128]{2,1,0:T(8,128)S(1)}, f32[10,8,128]{2,1,0:T(8,128)S(1)}, u32[]{:S(2)}, u32[]{:S(2)}) collective-permute-start(f32[10,8,128]{2,1,0:T(8,128)S(1)} %get-tuple-element.9), channel_id=1, source_target_pairs={{24,48},{28,52},{40,64},{44,68},{88,112},{92,116},{104,128},{108,1... | collective-permute-start | bytes 122888 | tf_op jit(solution)/shard_map/ppermute | solution.py:337
  16.4 0.7 %collective-permute-start.5 = (f32[19,8,128]{2,1,0:T(8,128)S(1)}, f32[19,8,128]{2,1,0:T(8,128)S(1)}, u32[]{:S(2)}, u32[]{:S(2)}) collective-permute-start(f32[19,8,128]{2,1,0:T(8,128)S(1)} %get-tuple-element.10), channel_id=1, source_target_pairs={{56,64},{60,68},{120,128},{124,132},{184,192},{188,196},{248,256},... | collective-permute-start | bytes 233480 | tf_op jit(solution)/shard_map/ppermute | solution.py:337
  17.1 1.3 %collective-permute-start.4 = (f32[19,8,128]{2,1,0:T(8,128)S(1)}, f32[19,8,128]{2,1,0:T(8,128)S(1)}, u32[]{:S(2)}, u32[]{:S(2)}) collective-permute-start(f32[19,8,128]{2,1,0:T(8,128)S(1)} %get-tuple-element.10), channel_id=1, source_target_pairs={{8,16},{12,20},{24,32},{28,36},{40,48},{44,52},{72,80},{76,84},{88... | collective-permute-start | bytes 233480 | tf_op jit(solution)/shard_map/ppermute | solution.py:337
  18.4 0.7 %collective-permute-start.3 = (f32[19,8,128]{2,1,0:T(8,128)S(1)}, f32[19,8,128]{2,1,0:T(8,128)S(1)}, u32[]{:S(2)}, u32[]{:S(2)}) collective-permute-start(f32[19,8,128]{2,1,0:T(8,128)S(1)} %get-tuple-element.10), channel_id=1, source_target_pairs={{48,64},{52,68},{112,128},{116,132},{176,192},{180,196},{240,256},... | collective-permute-start | bytes 233480 | tf_op jit(solution)/shard_map/ppermute | solution.py:337
  19.1 8.2 %collective-permute-start.2 = (f32[19,8,128]{2,1,0:T(8,128)S(1)}, f32[19,8,128]{2,1,0:T(8,128)S(1)}, u32[]{:S(2)}, u32[]{:S(2)}) collective-permute-start(f32[19,8,128]{2,1,0:T(8,128)S(1)} %get-tuple-element.10), channel_id=1, source_target_pairs={{0,16},{4,20},{16,32},{20,36},{32,48},{36,52},{64,80},{68,84},{80,... | collective-permute-start | bytes 233480 | tf_op jit(solution)/shard_map/ppermute | solution.py:337
  27.3 0.0 collective-permute-done.1.far_across_ref
  27.3 1.3 %collective-permute-start = (f32[10,8,128]{2,1,0:T(8,128)S(1)}, f32[10,8,128]{2,1,0:T(8,128)S(1)}, u32[]{:S(2)}, u32[]{:S(2)}) collective-permute-start(f32[10,8,128]{2,1,0:T(8,128)S(1)} %get-tuple-element.9), channel_id=1, source_target_pairs={{8,32},{12,36},{56,80},{60,84},{72,96},{76,100},{120,144},{124,148... | collective-permute-start | bytes 122888 | tf_op jit(solution)/shard_map/ppermute | solution.py:337
  28.6 14.5 %collective-permute-done.far_ref = f32[10,8,128]{2,1,0:T(8,128)S(1)} collective-permute-done((f32[10,8,128]{2,1,0:T(8,128)S(1)}, f32[10,8,128]{2,1,0:T(8,128)S(1)}, u32[]{:S(2)}, u32[]{:S(2)}) %collective-permute-start) | collective-permute-done | bytes 40992 | tf_op jit(solution)/shard_map/ppermute | solution.py:337
  43.1 0.0 collective-permute-done.5.near_across_ref
  43.1 0.0 collective-permute-done.4.near_ref
  43.1 0.0 collective-permute-done.3.middle_across_ref
  43.1 0.0 collective-permute-done.2.middle_ref
  43.1 0.8 %shard_map.57 = f32[16,2,8,128]{3,2,1,0:T(8,128)S(1)} custom-call(f32[10,8,128]{2,1,0:T(8,128)S(1)} %collective-permute-done.far_ref, f32[10,8,128]{2,1,0:T(8,128)S(1)} %collective-permute-done.1.far_across_ref, f32[19,8,128]{2,1,0:T(8,128)S(1)} %collective-permute-done.2.middle_ref, f32[19,8,128]{2,1,0:T(8,128)S(1)} %collective-permute-done.3.middle_across_ref, ...), custom_call_target="tpu_custom_call" | custom-call | tf_op jit(solution)/shard_map/pallas_call | solution.py:298
  44.0 12.0 %all_to_all.11.in_ref = f32[16,2,8,128]{3,2,1,0:T(8,128)S(1)} all-to-all(f32[16,2,8,128]{3,2,1,0:T(8,128)S(1)} %shard_map.57), channel_id=1, replica_groups={{0,1,2,3,4,5,6,7,8,9,10,11,12,13,14,15},{16,17,18,19,20,21,22,23,24,25,..., dimensions={0} | all-to-all | bytes 262144 | tf_op jit(solution)/shard_map/all_to_all | solution.py:355
  56.0 0.7 %shard_map.58 = f32[1,4,8,512]{3,2,1,0:T(8,128)} custom-call(f32[16,2,8,128]{3,2,1,0:T(8,128)S(1)} %all_to_all.11.in_ref), custom_call_target="tpu_custom_call" | custom-call | tf_op jit(solution)/shard_map/pallas_call | solution.py:298
Async XLA Ops:
  15.8 11.5 %collective-permute-start.1 = (f32[10,8,128]{2,1,0:T(8,128)S(1)}, f32[10,8,128]{2,1,0:T(8,128)S(1)}, u32[]{:S(2)}, u32[]{:S(2)}) collective-permute-start(f32[10,8,128]{2,1,0:T(8,128)S(1)} %get-tuple-element.9), channel_id=1, source_target_pairs={{24,48},{28,52},{40,64},{44,68},{88,112},{92,116},{104,128},{108,1... | collective-permute-start | bytes 122888 | tf_op jit(solution)/shard_map/ppermute | solution.py:337
  16.4 26.7 %collective-permute-start.5 = (f32[19,8,128]{2,1,0:T(8,128)S(1)}, f32[19,8,128]{2,1,0:T(8,128)S(1)}, u32[]{:S(2)}, u32[]{:S(2)}) collective-permute-start(f32[19,8,128]{2,1,0:T(8,128)S(1)} %get-tuple-element.10), channel_id=1, source_target_pairs={{56,64},{60,68},{120,128},{124,132},{184,192},{188,196},{248,256},... | collective-permute-start | bytes 233480 | tf_op jit(solution)/shard_map/ppermute | solution.py:337
  17.1 26.0 %collective-permute-start.4 = (f32[19,8,128]{2,1,0:T(8,128)S(1)}, f32[19,8,128]{2,1,0:T(8,128)S(1)}, u32[]{:S(2)}, u32[]{:S(2)}) collective-permute-start(f32[19,8,128]{2,1,0:T(8,128)S(1)} %get-tuple-element.10), channel_id=1, source_target_pairs={{8,16},{12,20},{24,32},{28,36},{40,48},{44,52},{72,80},{76,84},{88... | collective-permute-start | bytes 233480 | tf_op jit(solution)/shard_map/ppermute | solution.py:337
  18.4 24.7 %collective-permute-start.3 = (f32[19,8,128]{2,1,0:T(8,128)S(1)}, f32[19,8,128]{2,1,0:T(8,128)S(1)}, u32[]{:S(2)}, u32[]{:S(2)}) collective-permute-start(f32[19,8,128]{2,1,0:T(8,128)S(1)} %get-tuple-element.10), channel_id=1, source_target_pairs={{48,64},{52,68},{112,128},{116,132},{176,192},{180,196},{240,256},... | collective-permute-start | bytes 233480 | tf_op jit(solution)/shard_map/ppermute | solution.py:337
  19.1 24.1 %collective-permute-start.2 = (f32[19,8,128]{2,1,0:T(8,128)S(1)}, f32[19,8,128]{2,1,0:T(8,128)S(1)}, u32[]{:S(2)}, u32[]{:S(2)}) collective-permute-start(f32[19,8,128]{2,1,0:T(8,128)S(1)} %get-tuple-element.10), channel_id=1, source_target_pairs={{0,16},{4,20},{16,32},{20,36},{32,48},{36,52},{64,80},{68,84},{80,... | collective-permute-start | bytes 233480 | tf_op jit(solution)/shard_map/ppermute | solution.py:337
  27.3 15.8 %collective-permute-start = (f32[10,8,128]{2,1,0:T(8,128)S(1)}, f32[10,8,128]{2,1,0:T(8,128)S(1)}, u32[]{:S(2)}, u32[]{:S(2)}) collective-permute-start(f32[10,8,128]{2,1,0:T(8,128)S(1)} %get-tuple-element.9), channel_id=1, source_target_pairs={{8,32},{12,36},{56,80},{60,84},{72,96},{76,100},{120,144},{124,148... | collective-permute-start | bytes 122888 | tf_op jit(solution)/shard_map/ppermute | solution.py:337

commit v8 on v7

--- a/solution.py
+++ b/solution.py
@@ -245,7 +245,7 @@
     slope_ref, out_ref, far_join_ref, middle_join_ref, near_join_ref, rows_ref,
 ):
     starts = lax.axis_index("tm") % RING < 2
-    early = starts | (lax.axis_index("tm") % RING >= RING - 4)
+    early = starts
     for tile in range(far_ref.shape[0]):
         far_join_ref[tile] = jnp.where(early, far_across_ref[tile], far_ref[tile])
     for tile in range(middle_ref.shape[0]):
@@ -336,11 +336,11 @@
     def send(value, pairs):
         return lax.ppermute(value, "tm", pairs)
 
-    far_across = send(chain, [(i, j) for i, j in six if j % RING < 2 or j % RING >= RING - 4])
+    far_across = send(chain, [(i, j) for i, j in six if j % RING < 2])
     middle_across = send(passed, [(i, j) for i, j in four if j % RING < 2])
     near_across = send(passed, [(i, j) for i, j in two if j % RING < 2])
     near = send(passed, [(i, j) for i, j in two if j % RING >= 2])
-    far = send(chain, [(i, j) for i, j in six if 2 <= j % RING < RING - 4])
+    far = send(chain, [(i, j) for i, j in six if j % RING >= 2])
     middle = send(passed, [(i, j) for i, j in four if j % RING >= 2])
     packed = call(
         last_kernel,

time: 57 us -> 57 us (level)
  no operation moved by 1% of the time
where the time goes in v8:
time: 57 us; the launch traced here: 56.7 us
  blocking collectives  24.4 us (43%)
  waiting for transfers between devices  14.5 us (25%)
  starting transfers between devices  12.8 us (22%)
  Pallas kernels  4.93 us (9%)
    all_to_all x2, blocking collectives, on_device(): lax.all_to_all(packed, AXES, 0, 0, axis_index_groups=groups(count, row_de...  24.4 us
    ppermute x6, waiting for transfers between devices, send(): return lax.ppermute(value, 'tm', pairs)  14.5 us
    ppermute x6, starting transfers between devices, send(): return lax.ppermute(value, 'tm', pairs)  12.8 us
    pallas_call x4, Pallas kernels, run(): pl.pallas_call(kernel, out_shape=outs[0] if single else outs, in_specs=sp...  4.93 us
  transfers between devices with their start and end apart: 6, of which 1 were waited for; matrix products, arithmetic and copies ran while one was open for 0% of the time, Pallas kernels for 0%

profile of v8, /device:TPU:128, one launch (start us, length us, event | category | flops | bytes accessed | tf_op | source)
XLA Modules:
  0.0 56.7 jit_solution(16948098365771932664)
XLA Ops:
  0.0 1.0 %shard_map.55 = f32[8,5,8,128]{3,2,1,0:T(8,128)S(1)} custom-call(f32[4,8,512]{2,1,0:T(8,128)} %start_ref.1, f32[1,4,8,512]{3,2,1,0:T(8,128)} %guess_ref.1, s32[8,512]{1,0:T(8,128)} %mask_ref.1, s32[8,512]{1,0:T(8,128)} %class_ref.1, f32[16]{0:T(128)} %table_ref.1), custom_call_target="tpu_custom_call" | custom-call | tf_op jit(solution)/shard_map/pallas_call | solution.py:298
  1.0 12.4 %all_to_all.10.in_ref = f32[8,5,8,128]{3,2,1,0:T(8,128)S(1)} all-to-all(f32[8,5,8,128]{3,2,1,0:T(8,128)S(1)} %shard_map.55), channel_id=1, replica_groups={{0,1,2,3,4,5,6,7},{8,9,10,11,12,13,14,15},{16,17,18,19,20,21,22,23},{24..., dimensions={0} | all-to-all | bytes 327680 | tf_op jit(solution)/shard_map/all_to_all | solution.py:323
  13.4 2.4 %shard_map.56 = (f32[2,4,4,8,128]{4,3,2,1,0:T(8,128)S(1)}, f32[10,8,128]{2,1,0:T(8,128)S(1)}, f32[19,8,128]{2,1,0:T(8,128)S(1)}, f32[3,4,8,128]{3,2,1,0:T(8,128)S(1)}) custom-call(f32[8,5,8,128]{3,2,1,0:T(8,128)S(1)} %all_to_all.10.in_ref), custom_call_target="tpu_custom_call" | custom-call | tf_op jit(solution)/shard_map/pallas_call | solution.py:298
  15.8 0.7 %collective-permute-start.1 = (f32[10,8,128]{2,1,0:T(8,128)S(1)}, f32[10,8,128]{2,1,0:T(8,128)S(1)}, u32[]{:S(2)}, u32[]{:S(2)}) collective-permute-start(f32[10,8,128]{2,1,0:T(8,128)S(1)} %get-tuple-element.9), channel_id=1, source_target_pairs={{40,64},{44,68},{104,128},{108,132},{168,192},{172,196},{232,256},... | collective-permute-start | bytes 122888 | tf_op jit(solution)/shard_map/ppermute | solution.py:337
  16.4 0.7 %collective-permute-start.5 = (f32[19,8,128]{2,1,0:T(8,128)S(1)}, f32[19,8,128]{2,1,0:T(8,128)S(1)}, u32[]{:S(2)}, u32[]{:S(2)}) collective-permute-start(f32[19,8,128]{2,1,0:T(8,128)S(1)} %get-tuple-element.10), channel_id=1, source_target_pairs={{56,64},{60,68},{120,128},{124,132},{184,192},{188,196},{248,256},... | collective-permute-start | bytes 233480 | tf_op jit(solution)/shard_map/ppermute | solution.py:337
  17.1 1.3 %collective-permute-start.4 = (f32[19,8,128]{2,1,0:T(8,128)S(1)}, f32[19,8,128]{2,1,0:T(8,128)S(1)}, u32[]{:S(2)}, u32[]{:S(2)}) collective-permute-start(f32[19,8,128]{2,1,0:T(8,128)S(1)} %get-tuple-element.10), channel_id=1, source_target_pairs={{8,16},{12,20},{24,32},{28,36},{40,48},{44,52},{72,80},{76,84},{88... | collective-permute-start | bytes 233480 | tf_op jit(solution)/shard_map/ppermute | solution.py:337
  18.4 0.7 %collective-permute-start.3 = (f32[19,8,128]{2,1,0:T(8,128)S(1)}, f32[19,8,128]{2,1,0:T(8,128)S(1)}, u32[]{:S(2)}, u32[]{:S(2)}) collective-permute-start(f32[19,8,128]{2,1,0:T(8,128)S(1)} %get-tuple-element.10), channel_id=1, source_target_pairs={{48,64},{52,68},{112,128},{116,132},{176,192},{180,196},{240,256},... | collective-permute-start | bytes 233480 | tf_op jit(solution)/shard_map/ppermute | solution.py:337
  19.1 8.2 %collective-permute-start.2 = (f32[19,8,128]{2,1,0:T(8,128)S(1)}, f32[19,8,128]{2,1,0:T(8,128)S(1)}, u32[]{:S(2)}, u32[]{:S(2)}) collective-permute-start(f32[19,8,128]{2,1,0:T(8,128)S(1)} %get-tuple-element.10), channel_id=1, source_target_pairs={{0,16},{4,20},{16,32},{20,36},{32,48},{36,52},{64,80},{68,84},{80,... | collective-permute-start | bytes 233480 | tf_op jit(solution)/shard_map/ppermute | solution.py:337
  27.3 0.0 collective-permute-done.1.far_across_ref
  27.3 1.3 %collective-permute-start = (f32[10,8,128]{2,1,0:T(8,128)S(1)}, f32[10,8,128]{2,1,0:T(8,128)S(1)}, u32[]{:S(2)}, u32[]{:S(2)}) collective-permute-start(f32[10,8,128]{2,1,0:T(8,128)S(1)} %get-tuple-element.9), channel_id=1, source_target_pairs={{8,32},{12,36},{24,48},{28,52},{56,80},{60,84},{72,96},{76,100},{8... | collective-permute-start | bytes 122888 | tf_op jit(solution)/shard_map/ppermute | solution.py:337
  28.6 14.5 %collective-permute-done.far_ref = f32[10,8,128]{2,1,0:T(8,128)S(1)} collective-permute-done((f32[10,8,128]{2,1,0:T(8,128)S(1)}, f32[10,8,128]{2,1,0:T(8,128)S(1)}, u32[]{:S(2)}, u32[]{:S(2)}) %collective-permute-start) | collective-permute-done | bytes 40992 | tf_op jit(solution)/shard_map/ppermute | solution.py:337
  43.1 0.0 collective-permute-done.5.near_across_ref
  43.1 0.0 collective-permute-done.4.near_ref
  43.1 0.0 collective-permute-done.3.middle_across_ref
  43.1 0.0 collective-permute-done.2.middle_ref
  43.1 0.8 %shard_map.57 = f32[16,2,8,128]{3,2,1,0:T(8,128)S(1)} custom-call(f32[10,8,128]{2,1,0:T(8,128)S(1)} %collective-permute-done.far_ref, f32[10,8,128]{2,1,0:T(8,128)S(1)} %collective-permute-done.1.far_across_ref, f32[19,8,128]{2,1,0:T(8,128)S(1)} %collective-permute-done.2.middle_ref, f32[19,8,128]{2,1,0:T(8,128)S(1)} %collective-permute-done.3.middle_across_ref, ...), custom_call_target="tpu_custom_call" | custom-call | tf_op jit(solution)/shard_map/pallas_call | solution.py:298
  44.0 12.0 %all_to_all.11.in_ref = f32[16,2,8,128]{3,2,1,0:T(8,128)S(1)} all-to-all(f32[16,2,8,128]{3,2,1,0:T(8,128)S(1)} %shard_map.57), channel_id=1, replica_groups={{0,1,2,3,4,5,6,7,8,9,10,11,12,13,14,15},{16,17,18,19,20,21,22,23,24,25,..., dimensions={0} | all-to-all | bytes 262144 | tf_op jit(solution)/shard_map/all_to_all | solution.py:355
  56.0 0.7 %shard_map.58 = f32[1,4,8,512]{3,2,1,0:T(8,128)} custom-call(f32[16,2,8,128]{3,2,1,0:T(8,128)S(1)} %all_to_all.11.in_ref), custom_call_target="tpu_custom_call" | custom-call | tf_op jit(solution)/shard_map/pallas_call | solution.py:298
Async XLA Ops:
  15.8 11.5 %collective-permute-start.1 = (f32[10,8,128]{2,1,0:T(8,128)S(1)}, f32[10,8,128]{2,1,0:T(8,128)S(1)}, u32[]{:S(2)}, u32[]{:S(2)}) collective-permute-start(f32[10,8,128]{2,1,0:T(8,128)S(1)} %get-tuple-element.9), channel_id=1, source_target_pairs={{40,64},{44,68},{104,128},{108,132},{168,192},{172,196},{232,256},... | collective-permute-start | bytes 122888 | tf_op jit(solution)/shard_map/ppermute | solution.py:337
  16.4 26.7 %collective-permute-start.5 = (f32[19,8,128]{2,1,0:T(8,128)S(1)}, f32[19,8,128]{2,1,0:T(8,128)S(1)}, u32[]{:S(2)}, u32[]{:S(2)}) collective-permute-start(f32[19,8,128]{2,1,0:T(8,128)S(1)} %get-tuple-element.10), channel_id=1, source_target_pairs={{56,64},{60,68},{120,128},{124,132},{184,192},{188,196},{248,256},... | collective-permute-start | bytes 233480 | tf_op jit(solution)/shard_map/ppermute | solution.py:337
  17.1 26.0 %collective-permute-start.4 = (f32[19,8,128]{2,1,0:T(8,128)S(1)}, f32[19,8,128]{2,1,0:T(8,128)S(1)}, u32[]{:S(2)}, u32[]{:S(2)}) collective-permute-start(f32[19,8,128]{2,1,0:T(8,128)S(1)} %get-tuple-element.10), channel_id=1, source_target_pairs={{8,16},{12,20},{24,32},{28,36},{40,48},{44,52},{72,80},{76,84},{88... | collective-permute-start | bytes 233480 | tf_op jit(solution)/shard_map/ppermute | solution.py:337
  18.4 24.7 %collective-permute-start.3 = (f32[19,8,128]{2,1,0:T(8,128)S(1)}, f32[19,8,128]{2,1,0:T(8,128)S(1)}, u32[]{:S(2)}, u32[]{:S(2)}) collective-permute-start(f32[19,8,128]{2,1,0:T(8,128)S(1)} %get-tuple-element.10), channel_id=1, source_target_pairs={{48,64},{52,68},{112,128},{116,132},{176,192},{180,196},{240,256},... | collective-permute-start | bytes 233480 | tf_op jit(solution)/shard_map/ppermute | solution.py:337
  19.1 24.1 %collective-permute-start.2 = (f32[19,8,128]{2,1,0:T(8,128)S(1)}, f32[19,8,128]{2,1,0:T(8,128)S(1)}, u32[]{:S(2)}, u32[]{:S(2)}) collective-permute-start(f32[19,8,128]{2,1,0:T(8,128)S(1)} %get-tuple-element.10), channel_id=1, source_target_pairs={{0,16},{4,20},{16,32},{20,36},{32,48},{36,52},{64,80},{68,84},{80,... | collective-permute-start | bytes 233480 | tf_op jit(solution)/shard_map/ppermute | solution.py:337
  27.3 15.8 %collective-permute-start = (f32[10,8,128]{2,1,0:T(8,128)S(1)}, f32[10,8,128]{2,1,0:T(8,128)S(1)}, u32[]{:S(2)}, u32[]{:S(2)}) collective-permute-start(f32[10,8,128]{2,1,0:T(8,128)S(1)} %get-tuple-element.9), channel_id=1, source_target_pairs={{8,32},{12,36},{24,48},{28,52},{56,80},{60,84},{72,96},{76,100},{8... | collective-permute-start | bytes 122888 | tf_op jit(solution)/shard_map/ppermute | solution.py:337
